TPU v7x, 512 devices: a whole 4x4x16 slice. The times are simulated.
512 devices in a mesh: tok: 8 (over x, core), voc: 64 (over z, y).
Axes of the slice: x: 4, y: 4, z: 16, core: 2. Of those that a mesh axis runs over, the one named last changes fastest.
Arguments:
- teacher_hidden: bfloat16 [1024, 8192], P('voc', 'tok'), may hold values from -8 to 8
- teacher_head: bfloat16 [8192, 65536], P('tok', 'voc'), may hold values from -1 to 1
- student_hidden: bfloat16 [1024, 1536], P('tok'), may hold values from -8 to 8
- student_head: bfloat16 [1536, 81920], P('tok', 'voc'), may hold values from -1 to 1
- pair_owner: int32 [512, 8], replicated, may hold values from 0 to 63, all different within a row; in each aligned block of 8 rows (0 to 7, 8 to 15, ...) at most 2 rows name the same one
- pair_block: int32 [512, 8], replicated, may hold values from 0 to 9
- pair_shift: int32 [512, 8], replicated, may hold values from 0 to 127
- pair_count: int32 [512, 8], replicated, may hold values from 1 to 8
Outputs:
- token_loss: float32 [1024], P('tok')
- hidden_grad: bfloat16 [1024, 1536], P('tok')
Inputs may be any that keep to these rules, and one draw needn't show every extreme that they name: `pair_owner`: each row names 8 different owners. Within the 8 rows of the teacher blocks of one index of voc (aligned blocks of 8 rows) no owner is named more than 2 times, and in every draw some owner is named exactly 2 times in some such block. Every owner is named somewhere.
All inputs are finite; a program needn't handle non-finite values.
Results may differ from a plain program's by a relative error of at most 0.0046.
Values may be sent and summed in bfloat16 or wider, within the bound.
No kernel may reach another device: no remote copies, remote signals or barrier semaphores. Data moves between devices by JAX's collectives and lax.ppermute only.
A program may use at most 64 MiB of HBM per device.

v0:
```python
import jax
import jax.numpy as jnp
from jax import lax
from jax.sharding import PartitionSpec as P

BLOCK = 128
TB_DEV = 8
SB_DEV = 10


kernel_decay = 0.8
loss_scale = 256.0


def joined(value, axis, join):
    pieces = jax.tree.map(lambda part: lax.all_gather(part, axis), value)
    head = jax.tree.map(lambda part: part[0], pieces)
    tail = jax.tree.map(lambda part: part[1:], pieces)
    running, _ = lax.scan(lambda running, share: (join(running, share), None), head, tail)
    return running


def kernel_table(offsets):
    offsets = jnp.asarray(offsets)[..., None, None]
    row_index = jnp.arange(BLOCK, dtype=jnp.int32)[:, None]
    col_index = jnp.arange(BLOCK, dtype=jnp.int32)[None, :]
    distance = (row_index - col_index + offsets) % BLOCK
    distance = jnp.minimum(distance, BLOCK - distance)
    return jnp.power(jnp.float32(kernel_decay), distance.astype(jnp.float32)).astype(jnp.bfloat16)


def body(
    teacher_hidden,
    teacher_head,
    student_hidden,
    student_head,
    pair_owner,
    pair_block,
    pair_shift,
    pair_count,
):
    tok_rows = student_hidden.shape[0]
    voc_size = lax.axis_size("voc")
    voc_index = lax.axis_index("voc")
    fanout = pair_owner.shape[1]
    slot_depth = max(2, TB_DEV * fanout // voc_size)
    slot_count = voc_size * slot_depth
    partial_logits = jnp.dot(
        lax.all_gather(teacher_hidden, "voc", axis=0, tiled=True),
        teacher_head,
        preferred_element_type=jnp.float32,
    )
    logits = lax.psum_scatter(partial_logits, "tok", scatter_dimension=0, tiled=True)
    row_peak = lax.pmax(jnp.max(logits, axis=1), "voc")
    teacher_probs = jnp.exp(logits - row_peak[:, None]).astype(jnp.bfloat16)
    blocks = teacher_probs.reshape(tok_rows, TB_DEV, BLOCK)
    owners = pair_owner.reshape(voc_size, TB_DEV * fanout)
    owner_hits = (
        owners[:, :, None] == jnp.arange(voc_size, dtype=jnp.int32)[None, None, :]
    ).astype(jnp.int32)
    before = jnp.cumsum(owner_hits, axis=1) - owner_hits
    pair_rank = jnp.sum(before * owner_hits, axis=2)
    source = jnp.arange(voc_size, dtype=jnp.int32)[:, None]
    recv_slot = jnp.where(owners == voc_index, source * slot_depth + pair_rank, -1).reshape(-1)
    slot_ids = jnp.arange(slot_count, dtype=jnp.int32)
    recv_match = (recv_slot[None, :] == slot_ids[:, None]).astype(jnp.int32)
    local_ids = pair_block.reshape(-1)
    block_weight = (local_ids[:, None] == jnp.arange(SB_DEV, dtype=jnp.int32)[None, :]).astype(
        jnp.float32
    )
    block_weight = block_weight * pair_count.reshape(-1)[:, None].astype(jnp.float32)
    slot_weight = jnp.dot(
        recv_match.astype(jnp.float32), block_weight, precision=lax.Precision.HIGHEST
    ).astype(jnp.bfloat16)
    recv_shift = jnp.sum(recv_match * pair_shift.reshape(-1)[None, :], axis=1)
    sender_owner = lax.dynamic_index_in_dim(owners, voc_index, 0, keepdims=False)
    sender_rank = lax.dynamic_index_in_dim(pair_rank, voc_index, 0, keepdims=False)
    send_slot = sender_owner * slot_depth + sender_rank
    send_match = (slot_ids[:, None] == send_slot[None, :]).astype(jnp.bfloat16)
    block_match = send_match.reshape(slot_count, TB_DEV, fanout).sum(axis=2)
    outgoing = jnp.einsum(
        "si,tib->stb", block_match, blocks, preferred_element_type=jnp.float32
    ).astype(jnp.bfloat16)
    slot_tables = kernel_table(recv_shift)
    received = lax.all_to_all(outgoing, "voc", split_axis=0, concat_axis=0, tiled=True)
    tile_values = jnp.einsum(
        "stb,sbj->stj", received, slot_tables, preferred_element_type=jnp.float32
    ).astype(jnp.bfloat16)
    placed = jnp.einsum("sk,stj->tkj", slot_weight, tile_values, preferred_element_type=jnp.float32)
    aligned = placed.reshape(received.shape[1], SB_DEV * BLOCK)
    head_full = lax.all_gather(student_head, "tok", axis=0, tiled=True)
    student_logits = jnp.dot(student_hidden, head_full, preferred_element_type=jnp.float32)
    local_top = jnp.max(student_logits, axis=1)
    local_total = jnp.sum(jnp.exp(student_logits - local_top[:, None]), axis=1)
    local_norm = jnp.sum(aligned, axis=1)
    local_cross = jnp.sum(aligned * student_logits, axis=1)

    def combine(earlier, later):
        joint_top = jnp.maximum(earlier[0], later[0])
        joint_total = earlier[1] * jnp.exp(earlier[0] - joint_top) + later[1] * jnp.exp(
            later[0] - joint_top
        )
        return (joint_top, joint_total, earlier[2] + later[2], earlier[3] + later[3])

    student_top, student_total, target_norm, target_cross = joined(
        (local_top, local_total, local_norm, local_cross), "voc", combine
    )
    log_total = student_top + jnp.log(student_total)
    token_loss = log_total - target_cross / target_norm
    logit_grad = (
        loss_scale * (jnp.exp(student_logits - log_total[:, None]) - aligned / target_norm[:, None])
    ).astype(jnp.bfloat16)
    grad_terms = lax.dot_general(
        logit_grad, head_full, (((1,), (1,)), ((), ())), preferred_element_type=jnp.float32
    )
    hidden_grad = lax.psum(grad_terms, "voc").astype(jnp.bfloat16)
    return (token_loss, hidden_grad)


def solution(mesh):
    in_specs = (
        P("voc", "tok"),
        P("tok", "voc"),
        P("tok", None),
        P("tok", "voc"),
        P(),
        P(),
        P(),
        P(),
    )
    out_specs = (P("tok"), P("tok", None))
    return jax.shard_map(body, mesh=mesh, in_specs=in_specs, out_specs=out_specs, check_vma=False)
```

profile of v0, /device:TPU:6, one launch (start us, length us, event | category | flops | bytes accessed | tf_op | source)
XLA Modules:
  0.0 1115.4 jit_solution(11003184104276851065)
XLA Ops:
  7.2 0.7 all-gather.13.cloned.1.call-update
  8.0 148.7 %all-gather.13.cloned.1.call-done = bf16[1024,1024]{1,0:T(8,128)(2,1)} async-done(((bf16[16,1024]{1,0:T(8,128)(2,1)}), bf16[1024,1024]{1,0:T(8,128)(2,1)}) %all-gather.13.cloned.1.call-update) | async-done | bytes 2097168 | tf_op jit(solution)/shard_map/all_gather | solution.py:49
  156.6 5.8 fusion.62
  162.5 0.7 copy-done.2
  163.5 2.3 fusion.29
  165.8 0.2 add_reduce_fusion
  166.2 34.4 %reduce-scatter.2.cloned.1.call-done = f32[128,1024]{1,0:T(8,128)} async-done(((f32[1024,1024]{1,0:T(8,128)}), f32[128,1024]{1,0:T(8,128)}) %reduce-scatter.2.cloned.1.call-update) | async-done | bytes 524304 | tf_op jit(solution)/shard_map/reduce_scatter | solution.py:53
  200.5 1.2 reduce_max.19
  201.7 146.2 %pmax.7 = f32[128]{0:T(128)S(1)} all-reduce(f32[128]{0:T(128)S(1)} %reduce_max.19), channel_id=1, replica_groups=mesh['tok'=8,'voc'=64] {'voc'}, use_global_device_ids=true, to_apply=%region_7.8 | all-reduce | flops 128 | bytes 1024 | tf_op jit(solution)/shard_map/pmax | solution.py:54
  347.9 1.2 fusion.45
  349.1 1.3 convolution_convert_fusion
  350.4 4.7 copy.61
  355.1 8.4 all-to-all-start
  363.5 0.2 all-gather.11.cloned.1.call-start
  363.7 0.5 all-gather.11.cloned.1.call-update
  365.7 1.9 fusion.36
  367.6 0.3 select_reduce_fusion
  367.9 38.8 %all-gather.11.cloned.1.call-done = bf16[1536,1280]{1,0:T(8,128)(2,1)} async-done(((bf16[192,1280]{1,0:T(8,128)(2,1)}), bf16[1536,1280]{1,0:T(8,128)(2,1)}) %all-gather.11.cloned.1.call-update) | async-done | bytes 3932176 | tf_op jit(solution)/shard_map/all_gather | solution.py:91
  406.7 3.7 fusion.60
  410.3 176.5 %all-gather.4 = f32[64,1,128]{2,1,0:T(1,128)S(1)} all-gather(f32[1,1,128]{2,1,0:T(1,128)S(1)} %bitcast.74), channel_id=2, replica_groups=mesh['tok'=8,'voc'=64] {'voc'}, dimensions={0}, use_global_device_ids=true | all-gather | bytes 33280 | tf_op jit(solution)/shard_map/all_gather | solution.py:16
  586.8 8.3 fusion.25
  595.1 3.0 fusion.61
  598.1 1.2 copy.68
  599.3 1.3 copy.69
  600.6 1.3 multiply_reduce_fusion
  602.0 73.2 %all-gather.7 = f32[64,1,128]{2,1,0:T(1,128)S(1)} all-gather(f32[1,1,128]{2,1,0:T(1,128)S(1)} %bitcast.77), channel_id=5, replica_groups=mesh['tok'=8,'voc'=64] {'voc'}, dimensions={0}, use_global_device_ids=true | all-gather | bytes 33280 | tf_op jit(solution)/shard_map/all_gather | solution.py:16
  675.2 71.1 %all-gather.5 = f32[64,1,128]{2,1,0:T(1,128)S(1)} all-gather(f32[1,1,128]{2,1,0:T(1,128)S(1)} %bitcast.76), channel_id=3, replica_groups=mesh['tok'=8,'voc'=64] {'voc'}, dimensions={0}, use_global_device_ids=true | all-gather | bytes 33280 | tf_op jit(solution)/shard_map/all_gather | solution.py:16
  746.3 72.0 %all-gather.6 = f32[64,1,128]{2,1,0:T(1,128)S(1)} all-gather(f32[1,1,128]{2,1,0:T(1,128)S(1)} %bitcast.75), channel_id=4, replica_groups=mesh['tok'=8,'voc'=64] {'voc'}, dimensions={0}, use_global_device_ids=true | all-gather | bytes 33280 | tf_op jit(solution)/shard_map/all_gather | solution.py:16
  818.3 4.1 while.16
  822.4 0.5 divide_subtract_fusion
  823.0 3.7 fusion.41
  826.7 282.2 %all-reduce.1 = bf16[128,1536]{1,0:T(8,128)(2,1)} all-reduce(f32[128,1536]{1,0:T(8,128)S(1)} %fusion.41), channel_id=1, replica_groups=mesh['tok'=8,'voc'=64] {'voc'}, use_global_device_ids=true, to_apply=%region_13.14 | all-reduce | flops 196608 | bytes 1179648 | tf_op jit(solution)/shard_map/psum | solution.py:116
  (175 shorter events, 5.1 us)
Async XLA Ops:
  7.2 149.5 %copy-start = (bf16[1024,1024]{1,0:T(8,128)(2,1)S(1)}, bf16[1024,1024]{1,0:T(8,128)(2,1)}, u32[]{:S(2)}) copy-start(bf16[1024,1024]{1,0:T(8,128)(2,1)} %param.11) | copy-start | bytes 6291460
  7.2 149.4 %all-gather.13.cloned.1.call-start = ((), (), s32[]{:S(2)}) async-start(), calls=%async_computation.3 | async-start | bytes 2129920 | tf_op jit(solution)/shard_map/all_gather | solution.py:49
  7.9 192.6 %reduce-scatter.2.cloned.1.call-start = ((), (), s32[]{:S(2)}) async-start(), calls=%async_computation.4 | async-start | bytes 4718592 | tf_op jit(solution)/shard_map/reduce_scatter | solution.py:53
  162.5 0.7 copy-start.2
  355.1 9.7 copy-start.3
  355.1 10.0 copy-start.5
  355.1 10.3 copy-start.4
  355.1 51.6 %copy-start.1 = (bf16[128,1536]{1,0:T(8,128)(2,1)S(1)}, bf16[128,1536]{1,0:T(8,128)(2,1)}, u32[]{:S(2)}) copy-start(bf16[128,1536]{1,0:T(8,128)(2,1)} %param.12) | copy-start | bytes 1179652
  355.1 231.7 %all-to-all-start = ((bf16[128,128,128]{2,1,0:T(8,128)(2,1)}), bf16[128,128,128]{2,1,0:T(8,128)(2,1)}, u32[]{:S(2)}, u32[]{:S(2)}) async-start(bf16[128,128,128]{2,1,0:T(8,128)(2,1)} %copy.61), calls=%async_computation.1 | async-start | bytes 8388608 | tf_op jit(solution)/shard_map/all_to_all | solution.py:85
  363.5 43.2 %all-gather.11.cloned.1.call-start = ((), (), s32[]{:S(2)}) async-start(), calls=%async_computation.2 | async-start | bytes 4423680 | tf_op jit(solution)/shard_map/all_gather | solution.py:91
Sparse Core Ops, SparseCore 0:
  10.9 145.6 all-gather.12
  162.6 37.8 reduce-scatter.1
  366.4 40.2 all-gather.10
where the time goes:
time: 1120 us
  blocking collectives  821 us (73%)
  waiting for transfers between devices  223 us (20%)
  matrix products  27.7 us (2%)
  between operations  14 us (1%)
    all_gather x4, blocking collectives, joined(): pieces = jax.tree.map(lambda part: lax.all_gather(part, axis), value)  393 us
    psum x1, blocking collectives, body(): hidden_grad = lax.psum(grad_terms, 'voc').astype(jnp.bfloat16)  282 us
    all_gather x1, waiting for transfers between devices, body(): lax.all_gather(teacher_hidden, 'voc', axis=0, tiled=True)  149 us
    pmax x1, blocking collectives, body(): row_peak = lax.pmax(jnp.max(logits, axis=1), 'voc')  146 us
    all_gather x1, waiting for transfers between devices, body(): head_full = lax.all_gather(student_head, 'tok', axis=0, tiled=True)  38.8 us
    reduce_scatter x1, waiting for transfers between devices, body(): lax.psum_scatter(partial_logits, 'tok', scatter_dimension=0, tiled=True)  34.4 us
  transfers between devices with their start and end apart: 4, of which 3 were waited for; matrix products, arithmetic and copies ran while one was open for 1% of the time, Pallas kernels for 0%

commit v1 on v0

v1 whole, which is shorter than its diff:
```python
import jax
import jax.numpy as jnp
from jax import lax
from jax.experimental import pallas as pl
from jax.experimental.pallas import tpu as pltpu
from jax.sharding import Mesh
from jax.sharding import PartitionSpec as P

BLOCK = 128
TB_DEV = 8
SB_DEV = 10
FANOUT = 8
N_VOC = 64
NX, NC, NZ, NY = 4, 2, 16, 4
TBLOCKS = N_VOC * TB_DEV
SBLOCKS = N_VOC * SB_DEV
OWN = 2
TCOLS = TB_DEV * BLOCK
SCOLS = SB_DEV * BLOCK

kernel_decay = 0.8
loss_scale = 256.0
F32 = jnp.float32
BF16 = jnp.bfloat16


def base_kernel():
    row_index = lax.broadcasted_iota(jnp.int32, (BLOCK, BLOCK), 0)
    col_index = lax.broadcasted_iota(jnp.int32, (BLOCK, BLOCK), 1)
    distance = (row_index - col_index) % BLOCK
    distance = jnp.minimum(distance, BLOCK - distance)
    return jnp.power(F32(kernel_decay), distance.astype(F32)).astype(BF16)


def three_parts(value):
    first = lax.reduce_precision(value, 8, 7)
    rest = value - first
    second = lax.reduce_precision(rest, 8, 7)
    third = rest - second
    return [first, second, third]


def pack_columns(values):
    parts = []
    for value in values:
        parts.extend(three_parts(value))
    lanes = lax.broadcasted_iota(jnp.int32, (values[0].shape[0], BLOCK), 1)
    packed = jnp.zeros((values[0].shape[0], BLOCK), F32)
    for place, part in enumerate(parts):
        packed = jnp.where(lanes == place, part[:, None], packed)
    return packed.astype(BF16)


def unpack_column(packed, place):
    spot = 3 * place
    cols = packed[:, spot : spot + 3].astype(F32)
    return (cols[:, 0:1] + cols[:, 1:2]) + cols[:, 2:3]


def align_kernel(recv_ref, table_ref, weight_ref, shift_ref, out_ref, rolled_ref):
    lanes = lax.broadcasted_iota(jnp.int32, (TBLOCKS, BLOCK), 1)
    out_lanes = lax.broadcasted_iota(jnp.int32, (N_VOC, BLOCK), 1)
    for t in range(OWN):
        extra = recv_ref[t, :, TCOLS:]
        peak = unpack_column(extra, 0)
        scale = jnp.exp(peak - jnp.max(peak, axis=0, keepdims=True))
        smooth = []
        for j in range(TB_DEV):
            probs = recv_ref[t, :, j * BLOCK : (j + 1) * BLOCK]
            tile = jnp.dot(probs, table_ref[...], preferred_element_type=F32) * scale
            smooth.append(tile.astype(BF16).astype(F32))
        smooth = jnp.concatenate(smooth, axis=0)
        for k in range(FANOUT):
            index = (lanes - shift_ref[:, k : k + 1]) & (BLOCK - 1)
            rolled = jnp.take_along_axis(smooth, index, axis=1)
            rolled_ref[k * TBLOCKS : (k + 1) * TBLOCKS, t * BLOCK : (t + 1) * BLOCK] = rolled.astype(BF16)
    aligned = jnp.dot(weight_ref[...], rolled_ref[...], preferred_element_type=F32)
    for t in range(OWN):
        mine = aligned[:, t * BLOCK : (t + 1) * BLOCK]
        norm = jnp.sum(jnp.sum(mine, axis=0, keepdims=True), axis=1, keepdims=True)
        mine = mine / norm
        for b in range(SB_DEV):
            out_ref[t, :, b * BLOCK : (b + 1) * BLOCK] = mine[b * N_VOC : (b + 1) * N_VOC, :].astype(BF16)
        extra = recv_ref[t, :, TCOLS:]
        top = unpack_column(extra, 1)
        total = unpack_column(extra, 2)
        joint_top = jnp.max(top, axis=0, keepdims=True)
        joint_total = jnp.sum(total * jnp.exp(top - joint_top), axis=0, keepdims=True)
        log_total = joint_top + jnp.log(joint_total)
        first = log_total.astype(BF16).astype(F32)
        rest = log_total - first
        second = rest.astype(BF16).astype(F32)
        third = rest - second
        packed = jnp.where(out_lanes == 0, first, jnp.where(out_lanes == 1, second, jnp.where(out_lanes == 2, third, 0.0)))
        out_ref[t, :, SCOLS:] = packed.astype(BF16)


def align(recv, table, weight, shift):
    return pl.pallas_call(
        align_kernel,
        out_shape=jax.ShapeDtypeStruct((OWN, N_VOC, SCOLS + BLOCK), BF16),
        scratch_shapes=[pltpu.VMEM((FANOUT * TBLOCKS, OWN * BLOCK), BF16)],
        compiler_params=pltpu.CompilerParams(vmem_limit_bytes=40 * 1024 * 1024),
        name="align",
    )(recv, table, weight, shift)


def exchange(value, axis):
    return lax.all_to_all(value, axis, split_axis=0, concat_axis=0, tiled=True)


def spread(value, axis, size):
    return exchange(jnp.broadcast_to(value[None], (size,) + value.shape), axis)


def by_source(pairs):
    return pairs.reshape(N_VOC, TB_DEV, FANOUT).transpose(1, 0, 2).reshape(TBLOCKS, FANOUT)


def body(
    teacher_hidden,
    teacher_head,
    student_hidden,
    student_head,
    pair_owner,
    pair_block,
    pair_shift,
    pair_count,
):
    tok_rows = student_hidden.shape[0]
    head_full = lax.all_gather(student_head, ("x", "c"), axis=0, tiled=True)

    rows = spread(teacher_hidden, "z", NZ)
    rows = spread(rows, "y", NY)
    rows = rows.transpose(1, 0, 2, 3).reshape(-1, teacher_hidden.shape[1])

    table = base_kernel()
    shift = by_source(pair_shift)
    place = by_source(pair_block * N_VOC + pair_owner).T.reshape(1, -1)
    count = by_source(pair_count).T.reshape(1, -1)
    weight = jnp.where(
        place == lax.broadcasted_iota(jnp.int32, (SBLOCKS, TBLOCKS * FANOUT), 0), count, 0
    ).astype(BF16)

    partial_logits = jnp.dot(rows, teacher_head, preferred_element_type=F32)
    logits = lax.psum_scatter(partial_logits, ("x", "c"), scatter_dimension=0, tiled=True)
    peak = jnp.max(logits, axis=1)
    probs = jnp.exp(logits - peak[:, None]).astype(BF16)

    student_logits = jnp.dot(student_hidden, head_full, preferred_element_type=F32)
    local_top = jnp.max(student_logits, axis=1)
    local_total = jnp.sum(jnp.exp(student_logits - local_top[:, None]), axis=1)

    outgoing = jnp.concatenate([probs, pack_columns([peak, local_top, local_total])], axis=1)
    received = exchange(outgoing.reshape(N_VOC, OWN, TCOLS + BLOCK), ("z", "y"))
    target = align(received.transpose(1, 0, 2), table, weight, shift)
    target = exchange(target.transpose(1, 0, 2), ("z", "y")).reshape(tok_rows, SCOLS + BLOCK)

    log_total = unpack_column(target[:, SCOLS:], 0)
    target = target[:, :SCOLS].astype(F32)
    local_cross = jnp.sum(target * student_logits, axis=1)
    logit_grad = (loss_scale * (jnp.exp(student_logits - log_total) - target)).astype(BF16)
    grad_terms = lax.dot_general(
        logit_grad, head_full, (((1,), (1,)), ((), ())), preferred_element_type=F32
    )
    width = grad_terms.shape[1]
    terms = jnp.concatenate(
        [grad_terms, jnp.broadcast_to(local_cross[:, None], (tok_rows, BLOCK))], axis=1
    )
    terms = exchange(terms.reshape(NY, tok_rows // NY, width + BLOCK), "y").sum(axis=0)
    terms = exchange(terms.reshape(NZ, OWN, width + BLOCK), "z").sum(axis=0)
    result = jnp.concatenate([terms[:, :width].astype(BF16), pack_columns([terms[:, width]])], axis=1)
    result = spread(result, "z", NZ).reshape(NZ * OWN, width + BLOCK)
    result = spread(result, "y", NY).reshape(tok_rows, width + BLOCK)
    token_loss = log_total - unpack_column(result[:, width:], 0)
    return (token_loss[:, 0], result[:, :width])


def solution(mesh):
    grid = Mesh(mesh.devices.reshape(NX, NC, NZ, NY), ("x", "c", "z", "y"))
    tok = ("x", "c")
    voc = ("z", "y")
    in_specs = (
        P(voc, tok),
        P(tok, voc),
        P(tok, None),
        P(tok, voc),
        P(),
        P(),
        P(),
        P(),
    )
    out_specs = (P(tok), P(tok, None))
    return jax.shard_map(body, mesh=grid, in_specs=in_specs, out_specs=out_specs, check_vma=False)
```

time: 1120 us -> 284 us (0.25)
  blocking collectives: 821 us -> 163 us
  waiting for transfers between devices: 223 us -> 55 us
  matrix products: 27.7 us -> 10.7 us
    all_gather x4 -> x0, blocking collectives: 393 us -> none  [joined(): pieces = jax.tree.map(lambda part: lax.all_gather(part, axis), value)]
    psum x1 -> x0, blocking collectives: 282 us -> none  [body(): hidden_grad = lax.psum(grad_terms, 'voc').astype(jnp.bfloat16)]
    all_gather x2 -> x1, waiting for transfers between devices: 187 us -> 0.02 us  [body(): head_full = lax.all_gather(student_head, ('x', 'c'), axis=0, tiled=True)]
    all_to_all x0 -> x7, blocking collectives: none -> 163 us  [exchange(): return lax.all_to_all(value, axis, split_axis=0, concat_axis=0, tiled=True)]
    pmax x1 -> x0, blocking collectives: 146 us -> none  [body(): row_peak = lax.pmax(jnp.max(logits, axis=1), 'voc')]
    dot_general x6 -> x2, matrix products: 24 us -> 7.15 us  [the longest x1 4.27 us: body(): partial_logits = jnp.dot(rows, teacher_head, preferred_element_type=F32)]
    all_to_all x1, waiting for transfers between devices: 0.01 us -> 16.3 us  [exchange(): return lax.all_to_all(value, axis, split_axis=0, concat_axis=0, tiled=True)]
  transfers between devices with their start and end apart: 4 -> 3, of which waited for: 3 -> 2; matrix products, arithmetic and copies ran while one was open for 1% -> 6% of each run, Pallas kernels for 0% -> 0%
where the time goes in v1:
time: 284 us
  blocking collectives  163 us (57%)
  waiting for transfers between devices  55 us (19%)
  starting transfers between devices  15.9 us (6%)
  between operations  14.3 us (5%)
  local copies, waits for them, and re-layouts  11 us (4%)
  matrix products  10.7 us (4%)
  other arithmetic  8.41 us (3%)
  Pallas kernels  5.43 us (2%)
    all_to_all x7, blocking collectives, exchange(): return lax.all_to_all(value, axis, split_axis=0, concat_axis=0, tiled=True)  163 us
    reduce_scatter x1, waiting for transfers between devices, body(): lax.psum_scatter(partial_logits, ('x', 'c'), scatter_dimension=0, tiled=T...  38.1 us
    all_to_all x1, waiting for transfers between devices, exchange(): return lax.all_to_all(value, axis, split_axis=0, concat_axis=0, tiled=True)  16.3 us
    all_to_all x1, starting transfers between devices, exchange(): return lax.all_to_all(value, axis, split_axis=0, concat_axis=0, tiled=True)  15.8 us
  transfers between devices with their start and end apart: 3, of which 2 were waited for; matrix products, arithmetic and copies ran while one was open for 6% of the time, Pallas kernels for 0%

profile of v1, /device:TPU:6, one launch (start us, length us, event | category | flops | bytes accessed | tf_op | source)
XLA Modules:
  0.0 283.7 jit_solution(15257637225493682327)
XLA Ops:
  7.2 0.7 all-gather.2.cloned.1.call-update
  8.0 0.8 broadcast_in_dim.137
  8.8 44.1 %all_to_all.40 = bf16[16,16,1024]{2,1,0:T(8,128)(2,1)S(1)} all-to-all(bf16[16,16,1024]{2,1,0:T(8,128)(2,1)S(1)} %broadcast_in_dim.137), channel_id=1, replica_groups=mesh['x'=4,'c'=2,'z'=16,'y'=4] {'z'}, dimensions={0} | all-to-all | bytes 1048576 | tf_op jit(solution)/shard_map/all_to_all | solution.py:109
  52.8 0.3 broadcast_in_dim.138
  53.1 24.3 %all_to_all.41 = bf16[4,16,16,1024]{3,2,1,0:T(8,128)(2,1)S(1)} all-to-all(bf16[4,16,16,1024]{3,2,1,0:T(8,128)(2,1)S(1)} %broadcast_in_dim.138), channel_id=1, replica_groups=mesh['x'=4,'c'=2,'z'=16,'y'=4] {'y'}, dimensions={0} | all-to-all | bytes 4194304 | tf_op jit(solution)/shard_map/all_to_all | solution.py:109
  77.4 0.3 copy.36
  77.7 4.3 %fusion.21 = f32[1024,1024]{1,0:T(8,128)} fusion(bf16[1024,1024]{1,0:T(8,128)(2,1)S(1)} %bitcast.38, bf16[1024,1024]{1,0:T(8,128)(2,1)S(1)} %copy-done), kind=kOutput, calls=%fused_computation.63 | convolution fusion | flops 2147483648 | bytes 8388608 | tf_op jit(solution)/shard_map/dot_general | solution.py:145
  82.1 0.8 copy-done.2
  82.9 2.9 %fusion.20 = (f32[128]{0:T(128)S(1)}, f32[128,1280]{1,0:T(8,128)S(1)}) fusion(bf16[128,1536]{1,0:T(8,128)(2,1)S(1)} %copy-done.2, bf16[1536,1280]{1,0:T(8,128)(2,1)} %all-gather.2.cloned.1.call-done), kind=kOutput, calls=%fused_computation.62 | convolution fusion | flops 503480192 | bytes 4981248 | tf_op jit(solution)/shard_map/dot_general | solution.py:150
  85.8 0.3 exponential_reduce_fusion
  86.1 38.1 %reduce-scatter.2.cloned.1.call-done = f32[128,1024]{1,0:T(8,128)} async-done(((f32[1024,1024]{1,0:T(8,128)}), f32[128,1024]{1,0:T(8,128)}) %reduce-scatter.2.cloned.1.call-update) | async-done | bytes 524304 | tf_op jit(solution)/shard_map/reduce_scatter | solution.py:146
  124.1 1.2 reduce_max.18
  125.3 0.2 select_convert_fusion.1
  125.5 1.2 exponential_convert_fusion
  126.8 0.8 reshape.82
  127.6 15.8 %all-to-all-start.2 = ((bf16[64,2,1152]{2,1,0:T(2,128)(2,1)}), bf16[64,2,1152]{2,1,0:T(2,128)(2,1)S(1)}, u32[]{:S(2)}, u32[]{:S(2)}) async-start(bf16[64,2,1152]{2,1,0:T(2,128)(2,1)} %reshape.82), calls=%async_computation.3 | async-start | bytes 589824 | tf_op jit(solution)/shard_map/all_to_all | solution.py:109
  144.2 0.9 reshape.87
  145.1 1.2 copy.40
  146.4 4.0 %select_convert_fusion.weight_ref = bf16[640,4096]{1,0:T(8,128)(2,1)} fusion(s32[4096]{0:T(1024)S(1)} %bitcast.44, s32[4096]{0:T(1024)S(1)} %bitcast.45), kind=kLoop, calls=%fused_computation | loop fusion | flops 7864320 | bytes 5275648 | tf_op jit(solution)/shard_map/convert_element_type | solution.py:143
  150.3 16.3 %all-to-all-done.2 = bf16[64,2,1152]{2,1,0:T(2,128)(2,1)S(1)} async-done(((bf16[64,2,1152]{2,1,0:T(2,128)(2,1)}), bf16[64,2,1152]{2,1,0:T(2,128)(2,1)S(1)}, u32[]{:S(2)}, u32[]{:S(2)}) %all-to-all-start.2) | async-done | bytes 294944 | tf_op jit(solution)/shard_map/all_to_all | solution.py:109
  166.7 2.5 copy-done.1
  169.1 5.4 %align.1 = bf16[2,64,1408]{2,1,0:T(8,128)(2,1)S(1)} custom-call(bf16[2,64,1152]{2,1,0:T(8,128)(2,1)S(1)} %bitcast.35, bf16[128,128]{1,0:T(8,128)(2,1)S(1)} %fusion.11.table_ref, bf16[640,4096]{1,0:T(8,128)(2,1)S(1)} %copy-done.1, s32[512,8]{1,0:T(8,128)S(1)} %bitcast.36), custom_call_target="tpu_custom_call" | custom-call | tf_op jit(solution)/shard_map/align/pallas_call | solution.py:99
  174.6 0.4 copy.41
  175.0 32.7 %all_to_all.42 = bf16[64,2,1408]{2,1,0:T(2,128)(2,1)} all-to-all(bf16[64,2,1408]{2,1,0:T(2,128)(2,1)S(1)} %copy.41), channel_id=1, replica_groups=mesh['x'=4,'c'=2,'z'=16,'y'=4] {'z','y'}, dimensions={0} | all-to-all | bytes 720896 | tf_op jit(solution)/shard_map/all_to_all | solution.py:109
  207.6 1.1 reshape.89
  209.1 3.5 %fusion.3 = f32[128,1536]{1,0:T(8,128)S(1)} fusion(bf16[1536,1280]{1,0:T(8,128)(2,1)} %all-gather.2.cloned.1.call-done, f32[128,1280]{1,0:T(8,128)S(1)} %get-tuple-element.15, f32[128]{0:T(128)S(1)} %fusion.19, bf16[128,1408]{1,0:T(8,128)(2,1)S(1)} %reshape.89), kind=kOutput, calls=%fused_computation.10 | convolution fusion | flops 504135680 | bytes 5702144 | tf_op jit(solution)/shard_map/dot_general | solution.py:163
  212.7 16.0 %all_to_all.43 = f32[4,32,1664]{2,1,0:T(8,128)S(1)} all-to-all(f32[4,32,1664]{2,1,0:T(8,128)S(1)} %bitcast.37), channel_id=1, replica_groups=mesh['x'=4,'c'=2,'z'=16,'y'=4] {'y'}, dimensions={0} | all-to-all | bytes 1703936 | tf_op jit(solution)/shard_map/all_to_all | solution.py:109
  228.9 18.6 %all_to_all.44 = f32[16,2,1664]{2,1,0:T(2,128)S(1)} all-to-all(f32[16,2,1664]{2,1,0:T(2,128)S(1)} %reshape.91), channel_id=1, replica_groups=mesh['x'=4,'c'=2,'z'=16,'y'=4] {'z'}, dimensions={0} | all-to-all | bytes 425984 | tf_op jit(solution)/shard_map/all_to_all | solution.py:109
  247.9 17.4 %all_to_all.45 = bf16[16,2,1664]{2,1,0:T(2,128)(2,1)S(1)} all-to-all(bf16[16,2,1664]{2,1,0:T(2,128)(2,1)S(1)} %broadcast_in_dim.160), channel_id=1, replica_groups=mesh['x'=4,'c'=2,'z'=16,'y'=4] {'z'}, dimensions={0} | all-to-all | bytes 212992 | tf_op jit(solution)/shard_map/all_to_all | solution.py:109
  265.4 9.9 %all_to_all.46 = bf16[4,32,1664]{2,1,0:T(8,128)(2,1)S(1)} all-to-all(bf16[4,32,1664]{2,1,0:T(8,128)(2,1)S(1)} %broadcast_in_dim.162), channel_id=1, replica_groups=mesh['x'=4,'c'=2,'z'=16,'y'=4] {'y'}, dimensions={0} | all-to-all | bytes 851968 | tf_op jit(solution)/shard_map/all_to_all | solution.py:109
  275.3 0.8 slice.64
  276.1 0.7 fusion.13
  (51 shorter events, 2.1 us)
Async XLA Ops:
  7.2 70.5 %copy-start = (bf16[1024,1024]{1,0:T(8,128)(2,1)S(1)}, bf16[1024,1024]{1,0:T(8,128)(2,1)}, u32[]{:S(2)}) copy-start(bf16[1024,1024]{1,0:T(8,128)(2,1)} %param.9) | copy-start | bytes 6291460
  7.2 74.9 %all-gather.2.cloned.1.call-start = ((), (), s32[]{:S(2)}) async-start(), calls=%async_computation.10 | async-start | bytes 4423680 | tf_op jit(solution)/shard_map/all_gather | solution.py:131
  7.9 116.2 %reduce-scatter.2.cloned.1.call-start = ((), (), s32[]{:S(2)}) async-start(), calls=%async_computation.9 | async-start | bytes 4718592 | tf_op jit(solution)/shard_map/reduce_scatter | solution.py:146
  81.9 1.0 copy-start.2
  82.0 61.4 %copy-start.3 = (s32[512,8]{0,1:T(8,128)S(1)}, s32[512,8]{0,1:T(8,128)}, u32[]{:S(2)}) copy-start(s32[512,8]{0,1:T(8,128)} %param.12) | copy-start | bytes 49156
  82.0 61.4 %copy-start.4 = (s32[512,8]{0,1:T(8,128)S(1)}, s32[512,8]{0,1:T(8,128)}, u32[]{:S(2)}) copy-start(s32[512,8]{0,1:T(8,128)} %param.13) | copy-start | bytes 49156
  82.1 61.4 %copy-start.5 = (s32[512,8]{0,1:T(8,128)S(1)}, s32[512,8]{0,1:T(8,128)}, u32[]{:S(2)}) copy-start(s32[512,8]{0,1:T(8,128)} %param.15) | copy-start | bytes 49156
  82.1 62.1 %copy-start.6 = (s32[512,8]{0,1:T(8,128)S(1)}, s32[512,8]{0,1:T(8,128)}, u32[]{:S(2)}) copy-start(s32[512,8]{0,1:T(8,128)} %param.14) | copy-start | bytes 49156
  127.6 39.0 %all-to-all-start.2 = ((bf16[64,2,1152]{2,1,0:T(2,128)(2,1)}), bf16[64,2,1152]{2,1,0:T(2,128)(2,1)S(1)}, u32[]{:S(2)}, u32[]{:S(2)}) async-start(bf16[64,2,1152]{2,1,0:T(2,128)(2,1)} %reshape.82), calls=%async_computation.3 | async-start | bytes 589824 | tf_op jit(solution)/shard_map/all_to_all | solution.py:109
  166.6 2.5 copy-start.1
Sparse Core Ops, SparseCore 0:
  10.1 41.1 all-gather.1
  82.1 41.9 reduce-scatter.1

commit v2 on v1

v2 whole, which is shorter than its diff:
```python
import jax
import jax.numpy as jnp
from jax import lax
from jax.experimental import pallas as pl
from jax.experimental.pallas import tpu as pltpu
from jax.sharding import Mesh
from jax.sharding import PartitionSpec as P

BLOCK = 128
TB_DEV = 8
SB_DEV = 10
FANOUT = 8
N_VOC = 64
NX, NC, NZ, NY = 4, 2, 16, 4
TBLOCKS = N_VOC * TB_DEV
SBLOCKS = N_VOC * SB_DEV
OWN = 2
DS = 1536
PIECE = DS // (NX * NC)
ROWS = PIECE // N_VOC
TCOLS = TB_DEV * BLOCK
SCOLS = SB_DEV * BLOCK
WIDE = DS + BLOCK

kernel_decay = 0.8
loss_scale = 256.0
F32 = jnp.float32
BF16 = jnp.bfloat16
VMEM_BYTES = 24 * 1024 * 1024


def kernel_call(kernel, out_shape, scratch=(), name=None, spots=False, arrays=0):
    specs = {}
    if spots:
        whole = pl.BlockSpec(memory_space=pltpu.VMEM)
        specs = dict(in_specs=[pl.BlockSpec(memory_space=pltpu.SMEM)] + [whole] * arrays)
    return pl.pallas_call(
        kernel,
        out_shape=out_shape,
        scratch_shapes=list(scratch),
        compiler_params=pltpu.CompilerParams(vmem_limit_bytes=VMEM_BYTES),
        name=name,
        **specs,
    )


def base_kernel():
    row_index = lax.broadcasted_iota(jnp.int32, (BLOCK, BLOCK), 0)
    col_index = lax.broadcasted_iota(jnp.int32, (BLOCK, BLOCK), 1)
    distance = (row_index - col_index) % BLOCK
    distance = jnp.minimum(distance, BLOCK - distance)
    return jnp.power(F32(kernel_decay), distance.astype(F32)).astype(BF16)


def pull_kernel(head_ref, select_ref, shift_ref, count_ref, out_ref, stacked_ref):
    for r in range(ROWS):
        for b in range(SB_DEV):
            stacked_ref[b * N_VOC : (b + 1) * N_VOC, r * BLOCK : (r + 1) * BLOCK] = head_ref[
                r, :, b * BLOCK : (b + 1) * BLOCK
            ]
    lanes = lax.broadcasted_iota(jnp.int32, (TBLOCKS, BLOCK), 1)
    sums = [jnp.zeros((TBLOCKS, BLOCK), F32) for _ in range(ROWS)]
    for k in range(FANOUT):
        picked = jnp.dot(
            select_ref[k * TBLOCKS : (k + 1) * TBLOCKS, :], stacked_ref[...], preferred_element_type=F32
        )
        index = (lanes + shift_ref[:, k : k + 1]) & (BLOCK - 1)
        count = count_ref[:, k : k + 1].astype(F32)
        for r in range(ROWS):
            rolled = jnp.take_along_axis(picked[:, r * BLOCK : (r + 1) * BLOCK], index, axis=1)
            sums[r] = sums[r] + count * rolled
    for r in range(ROWS):
        for j in range(TB_DEV):
            out_ref[r, :, j * BLOCK : (j + 1) * BLOCK] = sums[r][j * N_VOC : (j + 1) * N_VOC, :].astype(BF16)


def with_stats(rows, peak, mass):
    lanes = lax.broadcasted_iota(jnp.int32, (rows, BLOCK), 1)
    return jnp.where(lanes == 0, peak, jnp.where(lanes == 1, mass, 0.0))


def put_rows(full_ref, spots_ref, step, core, value):
    x = (spots_ref[0] + step) % NX
    start = (x * NC + core) * PIECE
    full_ref[pl.ds(pl.multiple_of(start, 64), PIECE), :] = value


def student_kernel(spots_ref, hidden_ref, mine_ref, theirs_ref, out_ref, head_ref):
    c = spots_ref[1]
    for step in range(NX):
        rows = slice(step * PIECE, (step + 1) * PIECE)
        put_rows(head_ref, spots_ref, step, c, mine_ref[rows, :])
        put_rows(head_ref, spots_ref, step, 1 - c, theirs_ref[rows, :])
    head = head_ref[...]
    logits = jnp.dot(hidden_ref[...], head, preferred_element_type=F32)
    top = jnp.max(logits, axis=1, keepdims=True)
    probs = jnp.exp(logits - top)
    total = jnp.sum(probs, axis=1, keepdims=True)
    out_ref[:, :DS] = lax.dot_general(
        probs.astype(BF16), head, (((1,), (1,)), ((), ())), preferred_element_type=F32
    )
    out_ref[:, DS:] = with_stats(out_ref.shape[0], top, total)


def rows_kernel(spots_ref, own_ref, after_ref, before_ref, low_ref, high_ref, head_ref, far_ref, rest_ref, mine_ref, rows_ref, theirs_ref):
    x, c, y = spots_ref[0], spots_ref[1], spots_ref[2]
    part = own_ref.shape[0] // NZ
    half = NZ // 2
    for step, ref in ((0, own_ref), (1, after_ref), (3, before_ref), (2, None)):
        spot = (y + step) % NY
        for z in range(NZ):
            source, local = ref, z
            if ref is None:
                source, local = (low_ref, z) if z < half else (high_ref, z - half)
            start = pl.multiple_of((z * NY + spot) * part, 16)
            rows_ref[pl.ds(start, part), :] = source[local * part : (local + 1) * part, :]
    chunk = far_ref.shape[0]
    for place, step in enumerate((2, 1, 3, 0)):
        first = ((x + step) % NX) * NC
        spot = slice(place * chunk, (place + 1) * chunk)
        theirs_ref[spot, :] = rows_ref[pl.ds(pl.multiple_of((first + 1 - c) * chunk, chunk), chunk), :]
        mine_ref[spot, :] = rows_ref[pl.ds(pl.multiple_of((first + c) * chunk, chunk), chunk), :]
    product = jnp.dot(theirs_ref[...], head_ref[...], preferred_element_type=F32)
    far_ref[...] = product[:chunk, :]
    rest_ref[...] = product[chunk:, :]


def teacher_kernel(spots_ref, own_ref, prev_ref, next_ref, table_ref, weight_ref, near_ref, far_ref, their_near_ref, their_far_ref, out_ref, smooth_ref, pulled_ref):
    c = spots_ref[1]
    for place, step in enumerate((0, 1, 3)):
        rows = slice(place * PIECE, (place + 1) * PIECE)
        put_rows(pulled_ref, spots_ref, step, c, near_ref[rows, :])
        put_rows(pulled_ref, spots_ref, step, 1 - c, their_near_ref[rows, :])
    put_rows(pulled_ref, spots_ref, 2, c, far_ref[...])
    put_rows(pulled_ref, spots_ref, 2, 1 - c, their_far_ref[...])
    logits = own_ref[...] + prev_ref[...] + next_ref[...]
    peak = jnp.max(logits, axis=1, keepdims=True)
    probs = jnp.exp(logits - peak).astype(BF16)
    for j in range(TB_DEV):
        part = slice(j * BLOCK, (j + 1) * BLOCK)
        smooth_ref[:, part] = jnp.dot(probs[:, part], table_ref[...], preferred_element_type=F32).astype(BF16)
    smooth = smooth_ref[...]
    norm = jnp.sum(smooth.astype(F32) * weight_ref[...], axis=1, keepdims=True)
    out_ref[:, :DS] = lax.dot_general(
        smooth, pulled_ref[...], (((1,), (1,)), ((), ())), preferred_element_type=F32
    )
    out_ref[:, DS:] = with_stats(out_ref.shape[0], peak, norm)


def merged(parts_ref):
    number = parts_ref.shape[0]
    stats = [parts_ref[i, :, DS:] for i in range(number)]
    peak = stats[0][:, 0:1]
    for i in range(1, number):
        peak = jnp.maximum(peak, stats[i][:, 0:1])
    rows, mass = 0.0, 0.0
    for i in range(number):
        scale = jnp.exp(stats[i][:, 0:1] - peak)
        rows = rows + scale * parts_ref[i, :, :DS]
        mass = mass + scale * stats[i][:, 1:2]
    return rows, peak, mass


def merge_kernel(parts_ref, out_ref):
    rows, peak, mass = merged(parts_ref)
    out_ref[:, :DS] = rows
    out_ref[:, DS:] = with_stats(out_ref.shape[0], peak, mass)


def finish_kernel(student_ref, target_ref, hidden_ref, out_ref):
    student, top, total = merged(student_ref)
    target, _, norm = merged(target_ref)
    target = target / norm
    cross = jnp.sum(target * hidden_ref[...], axis=1, keepdims=True)
    loss = top + jnp.log(total) - cross
    out_ref[:, :DS] = (loss_scale * (student / total - target)).astype(BF16)
    first = loss.astype(BF16).astype(F32)
    second = (loss - first).astype(BF16).astype(F32)
    third = loss - first - second
    lanes = lax.broadcasted_iota(jnp.int32, (OWN, BLOCK), 1)
    packed = jnp.where(lanes == 0, first, jnp.where(lanes == 1, second, jnp.where(lanes == 2, third, 0.0)))
    out_ref[:, DS:] = packed.astype(BF16)


def exchange(value, axis):
    return lax.all_to_all(value, axis, split_axis=0, concat_axis=0, tiled=True)


def spread(value, axis, size):
    return exchange(jnp.broadcast_to(value[None], (size,) + value.shape), axis)


def send(value, axis, size, step):
    return lax.ppermute(value, axis, [(i, (i + step) % size) for i in range(size)])


def send_x(value, step):
    return send(value, "x", NX, step)


def send_c(value):
    return lax.ppermute(value, "c", [(0, 1), (1, 0)])


def around(piece, axis, size):
    half = piece.shape[0] // 2
    after = send(piece, axis, size, -1)
    before = send(piece, axis, size, 1)
    far_low = send(after[:half], axis, size, -1)
    far_high = send(before[half:], axis, size, 1)
    return after, before, far_low, far_high


def by_source(pairs):
    return pairs.reshape(N_VOC, TB_DEV, FANOUT).transpose(1, 0, 2).reshape(TBLOCKS, FANOUT)


def logit_parts(rows, head, spots):
    size, width = NZ * rows.shape[1], rows.shape[2]
    rows = rows.reshape(size, width)
    pieces = around(rows, "y", NY)
    chunk = size * NY // (NX * NC)
    far_theirs, theirs, mine = kernel_call(
        rows_kernel,
        (
            jax.ShapeDtypeStruct((chunk, TCOLS), F32),
            jax.ShapeDtypeStruct((3 * chunk, TCOLS), F32),
            jax.ShapeDtypeStruct((4 * chunk, width), BF16),
        ),
        [pltpu.VMEM((NY * size, width), BF16), pltpu.VMEM((4 * chunk, width), BF16)],
        "rows",
        True,
        6,
    )(spots, rows, *pieces, head)
    far_theirs = send_c(far_theirs)
    theirs = send_c(theirs)
    mine = jnp.dot(mine, head, preferred_element_type=F32)
    far = mine[:chunk] + far_theirs
    half = chunk // 2
    low = send_x(far[:half], 1)
    high = send_x(far[half:], -1)
    near = mine[chunk:] + theirs
    after = jnp.concatenate([near[:half] + low, near[half:chunk]], axis=0)
    before = jnp.concatenate([near[chunk : chunk + half], near[chunk + half : 2 * chunk] + high], axis=0)
    return near[2 * chunk :], send_x(after, 1), send_x(before, -1)


def body(
    teacher_hidden,
    teacher_head,
    student_hidden,
    student_head,
    pair_owner,
    pair_block,
    pair_shift,
    pair_count,
):
    tok_rows = student_hidden.shape[0]
    x = lax.axis_index("x")
    c = lax.axis_index("c")
    z = lax.axis_index("z")
    y = lax.axis_index("y")
    spots = jnp.stack([x, c, y]).astype(jnp.int32)

    shift = by_source(pair_shift)
    count = by_source(pair_count)
    place = by_source(pair_block * N_VOC + pair_owner).T.reshape(-1, 1)
    select = (
        place == lax.broadcasted_iota(jnp.int32, (TBLOCKS * FANOUT, SBLOCKS), 1)
    ).astype(BF16)
    split = exchange(student_head.reshape(N_VOC, ROWS, SCOLS), ("z", "y"))
    pulled = kernel_call(
        pull_kernel,
        jax.ShapeDtypeStruct((ROWS, N_VOC, TCOLS), BF16),
        [pltpu.VMEM((SBLOCKS, ROWS * BLOCK), BF16)],
        "pull",
    )(split.transpose(1, 0, 2), select, shift, count)
    rows = spread(teacher_hidden, "z", NZ)
    pulled, hidden = lax.optimization_barrier((pulled, student_hidden))
    pulled = exchange(pulled.transpose(1, 0, 2), ("z", "y")).reshape(PIECE, TCOLS)

    head_mine = jnp.concatenate(
        [student_head, send_x(student_head, -1), send_x(student_head, 2), send_x(student_head, 1)], axis=0
    )
    head_theirs = send_c(head_mine)
    wide = jax.ShapeDtypeStruct((tok_rows, WIDE), F32)
    short = jax.ShapeDtypeStruct((tok_rows // NY, WIDE), F32)
    student = kernel_call(
        student_kernel, wide, [pltpu.VMEM((DS, SCOLS), BF16)], "student", True, 3
    )(spots, hidden, head_mine, head_theirs)
    pulled, student = lax.optimization_barrier((pulled, student))
    student = exchange(student.reshape(NY, tok_rows // NY, WIDE), "y")
    student = kernel_call(merge_kernel, short, name="merge_student")(student)

    own, before, after = logit_parts(rows, teacher_head, spots)
    student, own = lax.optimization_barrier((student, own))
    student = exchange(student.reshape(NZ, OWN, WIDE), "z")

    near, prior, low, high = around(pulled, "x", NX)
    near = jnp.concatenate([pulled, near, prior], axis=0)
    far = jnp.concatenate([low, high], axis=0)
    table = base_kernel()
    weight = jnp.sum(pair_count, axis=1).reshape(N_VOC, TB_DEV)
    weight = lax.dynamic_index_in_dim(weight, z * NY + y, 0, keepdims=False).astype(F32)
    weight = jnp.broadcast_to(weight[:, None], (TB_DEV, BLOCK)).reshape(1, TCOLS)
    target = kernel_call(
        teacher_kernel,
        wide,
        [pltpu.VMEM((tok_rows, TCOLS), BF16), pltpu.VMEM((DS, TCOLS), BF16)],
        "teacher",
        True,
        9,
    )(spots, own, before, after, table, weight, near, far, send_c(near), send_c(far))
    student, target = lax.optimization_barrier((student, target))
    target = exchange(target.reshape(NY, tok_rows // NY, WIDE), "y")
    target = kernel_call(merge_kernel, short, name="merge_target")(target)
    target = exchange(target.reshape(NZ, OWN, WIDE), "z")

    mine = lax.dynamic_slice_in_dim(student_hidden, (y * NZ + z) * OWN, OWN, 0).astype(F32)
    result = kernel_call(
        finish_kernel, jax.ShapeDtypeStruct((OWN, WIDE), BF16), name="finish"
    )(student, target, mine)
    result = spread(result, "z", NZ).reshape(NZ * OWN, WIDE)
    result = spread(result, "y", NY).reshape(tok_rows, WIDE)
    loss = result[:, DS : DS + 3].astype(F32)
    token_loss = (loss[:, 0] + loss[:, 1]) + loss[:, 2]
    return (token_loss, result[:, :DS])


def solution(mesh):
    grid = Mesh(mesh.devices.reshape(NX, NC, NZ, NY), ("x", "c", "z", "y"))
    tok = ("x", "c")
    voc = ("z", "y")
    in_specs = (
        P(voc, tok),
        P(tok, voc),
        P(tok, None),
        P(tok, voc),
        P(),
        P(),
        P(),
        P(),
    )
    out_specs = (P(tok), P(tok, None))
    return jax.shard_map(body, mesh=grid, in_specs=in_specs, out_specs=out_specs, check_vma=False)
```

time: 284 us -> 311 us (1.095)
  blocking collectives: 163 us -> 44.2 us
  starting transfers between devices: 15.9 us -> 122 us
  waiting for transfers between devices: 55 us -> 81.7 us
  local copies, waits for them, and re-layouts: 11 us -> 28.7 us
  between operations: 14.3 us -> 1.32 us
  Pallas kernels: 5.43 us -> 17.7 us
  matrix products: 10.7 us -> 1.28 us
    all_to_all x7 -> x3, blocking collectives: 163 us -> 44.2 us  [exchange(): return lax.all_to_all(value, axis, split_axis=0, concat_axis=0, tiled=True)]
    ppermute x0 -> x20, starting transfers between devices: none -> 61.3 us  [the longest x15 51.1 us: send(): lax.ppermute(value, axis, [(i, (i + step) % size) for i in range(size)])]
    all_to_all x1 -> x6, starting transfers between devices: 15.8 us -> 61.1 us  [exchange(): return lax.all_to_all(value, axis, split_axis=0, concat_axis=0, tiled=True)]
    reduce_scatter x1 -> x0, waiting for transfers between devices: 38.1 us -> none  [body(): lax.psum_scatter(partial_logits, ('x', 'c'), scatter_dimension=0, tiled=T...]
    all_to_all x1 -> x6, waiting for transfers between devices: 16.3 us -> 52.8 us  [exchange(): return lax.all_to_all(value, axis, split_axis=0, concat_axis=0, tiled=True)]
    ppermute x0 -> x20, waiting for transfers between devices: none -> 28.9 us  [the longest x15 27.4 us: send(): lax.ppermute(value, axis, [(i, (i + step) % size) for i in range(size)])]
    pallas_call x1 -> x7, Pallas kernels: 5.43 us -> 17.7 us  [the longest x1 5.35 us: body(): kernel_call(pull_kernel, jax.ShapeDtypeStruct((ROWS, N_VOC, TCOLS), BF16)...]
    dot_general x3 -> x1, matrix products: 10.7 us -> 1.28 us  [logit_parts(): mine = jnp.dot(mine, head, preferred_element_type=F32)]
  transfers between devices with their start and end apart: 3 -> 26, of which waited for: 2 -> 9; matrix products, arithmetic and copies ran while one was open for 6% -> 10% of each run, Pallas kernels for 0% -> 6%
where the time goes in v2:
time: 311 us; the launch traced here: 308 us
  starting transfers between devices  122 us (39%)
  waiting for transfers between devices  81.7 us (26%)
  blocking collectives  44.2 us (14%)
  local copies, waits for them, and re-layouts  28.7 us (9%)
  Pallas kernels  17.7 us (6%)
  other arithmetic  11.2 us (4%)
    all_to_all x6, starting transfers between devices, exchange(): return lax.all_to_all(value, axis, split_axis=0, concat_axis=0, tiled=True)  61.1 us
    all_to_all x6, waiting for transfers between devices, exchange(): return lax.all_to_all(value, axis, split_axis=0, concat_axis=0, tiled=True)  52.8 us
    ppermute x15, starting transfers between devices, send(): lax.ppermute(value, axis, [(i, (i + step) % size) for i in range(size)])  51.1 us
    all_to_all x3, blocking collectives, exchange(): return lax.all_to_all(value, axis, split_axis=0, concat_axis=0, tiled=True)  44.2 us
    ppermute x15, waiting for transfers between devices, send(): lax.ppermute(value, axis, [(i, (i + step) % size) for i in range(size)])  27.4 us
    ppermute x5, starting transfers between devices, send_c(): return lax.ppermute(value, 'c', [(0, 1), (1, 0)])  10.2 us
    unnamed x41, local copies, waits for them, and re-layouts  7.43 us
  transfers between devices with their start and end apart: 26, of which 9 were waited for; matrix products, arithmetic and copies ran while one was open for 10% of the time, Pallas kernels for 6%

profile of v2, /device:TPU:6, one launch (start us, length us, event | category | flops | bytes accessed | tf_op | source)
XLA Modules:
  0.0 308.5 jit_solution(8315305839593462105)
XLA Ops:
  2.9 18.9 %all-to-all-start = ((bf16[64,3,1280]{2,1,0:T(4,128)(2,1)}), bf16[64,3,1280]{2,1,0:T(4,128)(2,1)S(1)}, u32[]{:S(2)}, u32[]{:S(2)}) async-start(bf16[64,3,1280]{2,1,0:T(4,128)(2,1)} %reshape.65), calls=%async_computation | async-start | bytes 1310720 | tf_op jit(solution)/shard_map/all_to_all | solution.py:186
  21.8 2.7 collective-permute-start
  24.6 3.0 collective-permute-start.1
  27.6 4.0 %collective-permute-start.2 = (bf16[192,1280]{1,0:T(8,128)(2,1)S(1)}, bf16[192,1280]{1,0:T(8,128)(2,1)}, u32[]{:S(2)}, u32[]{:S(2)}) collective-permute-start(bf16[192,1280]{1,0:T(8,128)(2,1)S(1)} %copy-done.10), channel_id=1, source_target_pairs={{0,128},{128,256},{256,384},{384,0},{1,129},{129,257},{257,385},{3... | collective-permute-start | bytes 1474568 | tf_op jit(solution)/shard_map/ppermute | solution.py:194
  31.7 28.6 %all-to-all-done = bf16[64,3,1280]{2,1,0:T(4,128)(2,1)S(1)} async-done(((bf16[64,3,1280]{2,1,0:T(4,128)(2,1)}), bf16[64,3,1280]{2,1,0:T(4,128)(2,1)S(1)}, u32[]{:S(2)}, u32[]{:S(2)}) %all-to-all-start) | async-done | bytes 491552 | tf_op jit(solution)/shard_map/all_to_all | solution.py:186
  61.3 4.1 %all-to-all-start.3 = ((bf16[16,16,1024]{2,1,0:T(8,128)(2,1)}), bf16[16,16,1024]{2,1,0:T(8,128)(2,1)S(1)}, u32[]{:S(2)}, u32[]{:S(2)}) async-start(bf16[16,16,1024]{2,1,0:T(8,128)(2,1)} %broadcast_in_dim.10), calls=%async_computation.3 | async-start | bytes 1048576 | tf_op jit(solution)/shard_map/all_to_all | solution.py:186
  75.5 5.4 %pull.1 = bf16[3,64,1024]{2,1,0:T(8,128)(2,1)S(1)} custom-call(bf16[3,64,1280]{2,1,0:T(8,128)(2,1)S(1)} %bitcast.36, bf16[4096,640]{1,0:T(8,128)(2,1)S(1)} %fusion.select_ref, s32[512,8]{1,0:T(8,128)S(1)} %bitcast.38, s32[512,8]{1,0:T(8,128)S(1)} %bitcast.39), custom_call_target="tpu_custom_call" | custom-call | tf_op jit(solution)/shard_map/pull/pallas_call | solution.py:272
  82.0 9.5 %all-to-all-done.3 = bf16[16,16,1024]{2,1,0:T(8,128)(2,1)S(1)} async-done(((bf16[16,16,1024]{2,1,0:T(8,128)(2,1)}), bf16[16,16,1024]{2,1,0:T(8,128)(2,1)S(1)}, u32[]{:S(2)}, u32[]{:S(2)}) %all-to-all-start.3) | async-done | bytes 524320 | tf_op jit(solution)/shard_map/all_to_all | solution.py:186
  91.5 11.3 %all-to-all-start.1 = ((bf16[64,3,1024]{2,1,0:T(4,128)(2,1)}), bf16[64,3,1024]{2,1,0:T(4,128)(2,1)}, u32[]{:S(2)}, u32[]{:S(2)}) async-start(bf16[64,3,1024]{2,1,0:T(4,128)(2,1)} %copy.22), calls=%async_computation.1 | async-start | bytes 1048576 | tf_op jit(solution)/shard_map/all_to_all | solution.py:186
  102.8 4.6 %collective-permute-start.4 = (bf16[256,1024]{1,0:T(8,128)(2,1)S(1)}, bf16[256,1024]{1,0:T(8,128)(2,1)S(1)}, u32[]{:S(2)}, u32[]{:S(2)}) collective-permute-start(bf16[256,1024]{1,0:T(8,128)(2,1)S(1)} %bitcast.33), channel_id=1, source_target_pairs={{0,3},{1,0},{2,1},{3,2},{4,7},{5,4},{6,5},{7,6},{8,11},{9,8},{10,9... | collective-permute-start | bytes 1572872 | tf_op jit(solution)/shard_map/ppermute | solution.py:194
  109.3 11.7 %collective-permute-done.4.after_ref = bf16[256,1024]{1,0:T(8,128)(2,1)S(1)} collective-permute-done((bf16[256,1024]{1,0:T(8,128)(2,1)S(1)}, bf16[256,1024]{1,0:T(8,128)(2,1)S(1)}, u32[]{:S(2)}, u32[]{:S(2)}) %collective-permute-start.4) | collective-permute-done | bytes 524320 | tf_op jit(solution)/shard_map/ppermute | solution.py:194
  121.7 5.7 %collective-permute-start.6 = (bf16[128,1024]{1,0:T(8,128)(2,1)}, bf16[128,1024]{1,0:T(8,128)(2,1)}, u32[]{:S(2)}, u32[]{:S(2)}) collective-permute-start(bf16[128,1024]{1,0:T(8,128)(2,1)} %slice.72), channel_id=1, source_target_pairs={{0,3},{1,0},{2,1},{3,2},{4,7},{5,4},{6,5},{7,6},{8,11},{9,8},{10,9... | collective-permute-start | bytes 786440 | tf_op jit(solution)/shard_map/ppermute | solution.py:194
  131.8 6.1 %collective-permute-done.7.high_ref = bf16[128,1024]{1,0:T(8,128)(2,1)} collective-permute-done((bf16[128,1024]{1,0:T(8,128)(2,1)}, bf16[128,1024]{1,0:T(8,128)(2,1)}, u32[]{:S(2)}, u32[]{:S(2)}) %collective-permute-start.7) | collective-permute-done | bytes 262176 | tf_op jit(solution)/shard_map/ppermute | solution.py:194
  139.6 3.7 %rows.1 = (f32[128,1024]{1,0:T(8,128)}, f32[384,1024]{1,0:T(8,128)}, bf16[512,1024]{1,0:T(8,128)(2,1)S(1)}) custom-call(s32[3]{0:T(128)S(1)} %pad_add_fusion.spots_ref, bf16[256,1024]{1,0:T(8,128)(2,1)S(1)} %bitcast.35, bf16[256,1024]{1,0:T(8,128)(2,1)S(1)} %collective-permute-done.4.after_ref, bf16[256,1024]{1,0:T(8,128)(2,1)S(1)} %collective-permute-done.5.before_ref, ...), custom_call_target="tpu_custom_call" | custom-call | tf_op jit(solution)/shard_map/rows/pallas_call | solution.py:223
  145.2 2.5 collective-permute-start.9
  147.8 4.9 %student.1 = f32[128,1664]{1,0:T(8,128)} custom-call(s32[3]{0:T(128)S(1)} %pad_add_fusion.spots_ref, bf16[128,1536]{1,0:T(8,128)(2,1)S(1)} %copy-done.4, bf16[768,1280]{1,0:T(8,128)(2,1)S(1)} %constant_dynamic-update-slice_fusion.mine_ref, bf16[768,1280]{1,0:T(8,128)(2,1)} %collective-permute-done.3.theirs_ref), custom_call_target="tpu_custom_call" | custom-call | tf_op jit(solution)/shard_map/student/pallas_call | solution.py:288
  155.8 2.7 collective-permute-start.14
  158.5 4.3 %collective-permute-start.15 = (bf16[192,1024]{1,0:T(8,128)(2,1)S(1)}, bf16[192,1024]{1,0:T(8,128)(2,1)}, u32[]{:S(2)}, u32[]{:S(2)}) collective-permute-start(bf16[192,1024]{1,0:T(8,128)(2,1)S(1)} %reshape.72), channel_id=1, source_target_pairs={{0,128},{128,256},{256,384},{384,0},{1,129},{129,257},{257,385},{3... | collective-permute-start | bytes 1179656 | tf_op jit(solution)/shard_map/ppermute | solution.py:194
  162.8 3.5 %all-to-all-start.2 = ((f32[4,32,1664]{2,1,0:T(8,128)}), f32[4,32,1664]{2,1,0:T(8,128)S(1)}, u32[]{:S(2)}, u32[]{:S(2)}) async-start(f32[4,32,1664]{2,1,0:T(8,128)} %bitcast.11), calls=%async_computation.2 | async-start | bytes 1703936 | tf_op jit(solution)/shard_map/all_to_all | solution.py:186
  170.2 5.1 %collective-permute-start.10 = (f32[64,1024]{1,0:T(8,128)}, f32[64,1024]{1,0:T(8,128)}, u32[]{:S(2)}, u32[]{:S(2)}) collective-permute-start(f32[64,1024]{1,0:T(8,128)} %get-tuple-element.29), channel_id=1, source_target_pairs={{0,128},{128,256},{256,384},{384,0},{1,129},{129,257},{257,385},{3... | collective-permute-start | bytes 786440 | tf_op jit(solution)/shard_map/ppermute | solution.py:194
  180.6 5.1 %collective-permute-start.17 = (bf16[96,1024]{1,0:T(8,128)(2,1)}, bf16[96,1024]{1,0:T(8,128)(2,1)}, u32[]{:S(2)}, u32[]{:S(2)}) collective-permute-start(bf16[96,1024]{1,0:T(8,128)(2,1)} %slice.84), channel_id=1, source_target_pairs={{0,128},{128,256},{256,384},{384,0},{1,129},{129,257},{257,385},{3... | collective-permute-start | bytes 589832 | tf_op jit(solution)/shard_map/ppermute | solution.py:194
  189.9 3.4 %slice_add_fusion = f32[384,1024]{1,0:T(8,128)} fusion(f32[384,1024]{1,0:T(8,128)} %collective-permute-done.8, f32[512,1024]{1,0:T(8,128)} %copy-done.9), kind=kLoop, calls=%fused_computation.2 | loop fusion | flops 393216 | bytes 4718592 | tf_op jit(solution)/shard_map/add | solution.py:242
  195.2 11.9 %all-to-all-start.4 = ((f32[16,2,1664]{2,1,0:T(2,128)}), f32[16,2,1664]{2,1,0:T(2,128)S(1)}, u32[]{:S(2)}, u32[]{:S(2)}) async-start(f32[16,2,1664]{2,1,0:T(2,128)} %reshape.75), calls=%async_computation.4 | async-start | bytes 425984 | tf_op jit(solution)/shard_map/all_to_all | solution.py:186
  212.2 3.9 %collective-permute-start.13 = (f32[128,1024]{1,0:T(8,128)}, f32[128,1024]{1,0:T(8,128)}, u32[]{:S(2)}, u32[]{:S(2)}) collective-permute-start(f32[128,1024]{1,0:T(8,128)} %pad_maximum_fusion.1), channel_id=1, source_target_pairs={{0,384},{128,0},{256,128},{384,256},{1,385},{129,1},{257,129},{385... | collective-permute-start | bytes 1572872 | tf_op jit(solution)/shard_map/ppermute | solution.py:194
  220.7 4.8 %collective-permute-done.11.prev_ref = f32[128,1024]{1,0:T(8,128)S(1)} collective-permute-done((f32[128,1024]{1,0:T(8,128)}, f32[128,1024]{1,0:T(8,128)S(1)}, u32[]{:S(2)}, u32[]{:S(2)}) %collective-permute-start.11) | collective-permute-done | bytes 524320 | tf_op jit(solution)/shard_map/ppermute | solution.py:194
  226.3 3.3 %collective-permute-done.13.next_ref = f32[128,1024]{1,0:T(8,128)} collective-permute-done((f32[128,1024]{1,0:T(8,128)}, f32[128,1024]{1,0:T(8,128)}, u32[]{:S(2)}, u32[]{:S(2)}) %collective-permute-start.13) | collective-permute-done | bytes 524320 | tf_op jit(solution)/shard_map/ppermute | solution.py:194
  231.4 3.0 teacher.1
  234.4 17.1 %all_to_all.45.parts_ref = f32[4,32,1664]{2,1,0:T(8,128)S(1)} all-to-all(f32[4,32,1664]{2,1,0:T(8,128)S(1)} %bitcast.32), channel_id=1, replica_groups=mesh['x'=4,'c'=2,'z'=16,'y'=4] {'y'}, dimensions={0} | all-to-all | bytes 1703936 | tf_op jit(solution)/shard_map/all_to_all | solution.py:186
  252.4 11.5 %all-to-all-start.6 = ((f32[16,2,1664]{2,1,0:T(2,128)}), f32[16,2,1664]{2,1,0:T(2,128)S(1)}, u32[]{:S(2)}, u32[]{:S(2)}) async-start(f32[16,2,1664]{2,1,0:T(2,128)} %reshape.79), calls=%async_computation.6 | async-start | bytes 425984 | tf_op jit(solution)/shard_map/all_to_all | solution.py:186
  264.6 14.7 %all-to-all-done.6.target_ref = f32[16,2,1664]{2,1,0:T(2,128)S(1)} async-done(((f32[16,2,1664]{2,1,0:T(2,128)}), f32[16,2,1664]{2,1,0:T(2,128)S(1)}, u32[]{:S(2)}, u32[]{:S(2)}) %all-to-all-start.6) | async-done | bytes 213024 | tf_op jit(solution)/shard_map/all_to_all | solution.py:186
  279.7 17.2 %all_to_all.46 = bf16[16,2,1664]{2,1,0:T(2,128)(2,1)S(1)} all-to-all(bf16[16,2,1664]{2,1,0:T(2,128)(2,1)S(1)} %broadcast_in_dim.12), channel_id=1, replica_groups=mesh['x'=4,'c'=2,'z'=16,'y'=4] {'z'}, dimensions={0} | all-to-all | bytes 212992 | tf_op jit(solution)/shard_map/all_to_all | solution.py:186
  297.1 9.9 %all_to_all.47 = bf16[4,32,1664]{2,1,0:T(8,128)(2,1)S(1)} all-to-all(bf16[4,32,1664]{2,1,0:T(8,128)(2,1)S(1)} %broadcast_in_dim.14), channel_id=1, replica_groups=mesh['x'=4,'c'=2,'z'=16,'y'=4] {'y'}, dimensions={0} | all-to-all | bytes 851968 | tf_op jit(solution)/shard_map/all_to_all | solution.py:186
  (115 shorter events, 58.8 us)
Async XLA Ops:
  0.6 21.2 %copy-start.10 = (bf16[192,1280]{1,0:T(8,128)(2,1)S(1)}, bf16[192,1280]{1,0:T(8,128)(2,1)}, u32[]{:S(2)}) copy-start(bf16[192,1280]{1,0:T(8,128)(2,1)} %param.11) | copy-start | bytes 1474564
  0.6 59.6 %copy-start.13 = (bf16[16,1024]{1,0:T(8,128)(2,1)S(1)}, bf16[16,1024]{1,0:T(8,128)(2,1)}, u32[]{:S(2)}) copy-start(bf16[16,1024]{1,0:T(8,128)(2,1)} %param.8) | copy-start | bytes 98308
  2.9 62.5 %copy-start.14 = (s32[512,8]{0,1:T(8,128)S(1)}, s32[512,8]{0,1:T(8,128)}, u32[]{:S(2)}) copy-start(s32[512,8]{0,1:T(8,128)} %param.12) | copy-start | bytes 49156
  2.9 62.5 %copy-start.15 = (s32[512,8]{0,1:T(8,128)S(1)}, s32[512,8]{0,1:T(8,128)}, u32[]{:S(2)}) copy-start(s32[512,8]{0,1:T(8,128)} %param.13) | copy-start | bytes 49156
  2.9 57.3 %all-to-all-start = ((bf16[64,3,1280]{2,1,0:T(4,128)(2,1)}), bf16[64,3,1280]{2,1,0:T(4,128)(2,1)S(1)}, u32[]{:S(2)}, u32[]{:S(2)}) async-start(bf16[64,3,1280]{2,1,0:T(4,128)(2,1)} %reshape.65), calls=%async_computation | async-start | bytes 1310720 | tf_op jit(solution)/shard_map/all_to_all | solution.py:186
  21.8 44.0 %copy-start.16 = (s32[512,8]{0,1:T(8,128)S(1)}, s32[512,8]{0,1:T(8,128)}, u32[]{:S(2)}) copy-start(s32[512,8]{0,1:T(8,128)} %param.14) | copy-start | bytes 49156
  21.8 44.4 %copy-start.11 = (s32[512,8]{0,1:T(8,128)S(1)}, s32[512,8]{0,1:T(8,128)}, u32[]{:S(2)}) copy-start(s32[512,8]{0,1:T(8,128)} %param.15) | copy-start | bytes 49156
  21.8 46.5 %collective-permute-start = (bf16[192,1280]{1,0:T(8,128)(2,1)S(1)}, bf16[192,1280]{1,0:T(8,128)(2,1)}, u32[]{:S(2)}, u32[]{:S(2)}) collective-permute-start(bf16[192,1280]{1,0:T(8,128)(2,1)S(1)} %copy-done.10), channel_id=1, source_target_pairs={{0,384},{128,0},{256,128},{384,256},{1,385},{129,1},{257,129},{385... | collective-permute-start | bytes 1474568 | tf_op jit(solution)/shard_map/ppermute | solution.py:194
  24.6 44.8 %collective-permute-start.1 = (bf16[192,1280]{1,0:T(8,128)(2,1)S(1)}, bf16[192,1280]{1,0:T(8,128)(2,1)}, u32[]{:S(2)}, u32[]{:S(2)}) collective-permute-start(bf16[192,1280]{1,0:T(8,128)(2,1)S(1)} %copy-done.10), channel_id=1, source_target_pairs={{0,256},{128,384},{256,0},{384,128},{1,257},{129,385},{257,1},{385... | collective-permute-start | bytes 1474568 | tf_op jit(solution)/shard_map/ppermute | solution.py:194
  27.6 42.9 %collective-permute-start.2 = (bf16[192,1280]{1,0:T(8,128)(2,1)S(1)}, bf16[192,1280]{1,0:T(8,128)(2,1)}, u32[]{:S(2)}, u32[]{:S(2)}) collective-permute-start(bf16[192,1280]{1,0:T(8,128)(2,1)S(1)} %copy-done.10), channel_id=1, source_target_pairs={{0,128},{128,256},{256,384},{384,0},{1,129},{129,257},{257,385},{3... | collective-permute-start | bytes 1474568 | tf_op jit(solution)/shard_map/ppermute | solution.py:194
  61.3 30.2 %all-to-all-start.3 = ((bf16[16,16,1024]{2,1,0:T(8,128)(2,1)}), bf16[16,16,1024]{2,1,0:T(8,128)(2,1)S(1)}, u32[]{:S(2)}, u32[]{:S(2)}) async-start(bf16[16,16,1024]{2,1,0:T(8,128)(2,1)} %broadcast_in_dim.10), calls=%async_computation.3 | async-start | bytes 1048576 | tf_op jit(solution)/shard_map/all_to_all | solution.py:186
  71.6 76.2 %collective-permute-start.3 = (bf16[768,1280]{1,0:T(8,128)(2,1)S(1)}, bf16[768,1280]{1,0:T(8,128)(2,1)}, u32[]{:S(2)}, u32[]{:S(2)}) collective-permute-start(bf16[768,1280]{1,0:T(8,128)(2,1)S(1)} %constant_dynamic-update-slice_fusion.mine_ref), channel_id=1, source_target_pairs={{0,64},{64,0},{1,65},{65,1},{2,66},{66,2},{3,67},{67,3},{4,68},{68... | collective-permute-start | bytes 5898248 | tf_op jit(solution)/shard_map/ppermute | solution.py:202
  91.5 62.6 %all-to-all-start.1 = ((bf16[64,3,1024]{2,1,0:T(4,128)(2,1)}), bf16[64,3,1024]{2,1,0:T(4,128)(2,1)}, u32[]{:S(2)}, u32[]{:S(2)}) async-start(bf16[64,3,1024]{2,1,0:T(4,128)(2,1)} %copy.22), calls=%async_computation.1 | async-start | bytes 1048576 | tf_op jit(solution)/shard_map/all_to_all | solution.py:186
  102.8 18.2 %collective-permute-start.4 = (bf16[256,1024]{1,0:T(8,128)(2,1)S(1)}, bf16[256,1024]{1,0:T(8,128)(2,1)S(1)}, u32[]{:S(2)}, u32[]{:S(2)}) collective-permute-start(bf16[256,1024]{1,0:T(8,128)(2,1)S(1)} %bitcast.33), channel_id=1, source_target_pairs={{0,3},{1,0},{2,1},{3,2},{4,7},{5,4},{6,5},{7,6},{8,11},{9,8},{10,9... | collective-permute-start | bytes 1572872 | tf_op jit(solution)/shard_map/ppermute | solution.py:194
  107.4 20.1 %collective-permute-start.5 = (bf16[256,1024]{1,0:T(8,128)(2,1)S(1)}, bf16[256,1024]{1,0:T(8,128)(2,1)S(1)}, u32[]{:S(2)}, u32[]{:S(2)}) collective-permute-start(bf16[256,1024]{1,0:T(8,128)(2,1)S(1)} %bitcast.34), channel_id=1, source_target_pairs={{0,1},{1,2},{2,3},{3,0},{4,5},{5,6},{6,7},{7,4},{8,9},{9,10},{10,1... | collective-permute-start | bytes 1572872 | tf_op jit(solution)/shard_map/ppermute | solution.py:194
  121.7 10.1 %collective-permute-start.6 = (bf16[128,1024]{1,0:T(8,128)(2,1)}, bf16[128,1024]{1,0:T(8,128)(2,1)}, u32[]{:S(2)}, u32[]{:S(2)}) collective-permute-start(bf16[128,1024]{1,0:T(8,128)(2,1)} %slice.72), channel_id=1, source_target_pairs={{0,3},{1,0},{2,1},{3,2},{4,7},{5,4},{6,5},{7,6},{8,11},{9,8},{10,9... | collective-permute-start | bytes 786440 | tf_op jit(solution)/shard_map/ppermute | solution.py:194
  128.2 9.8 %collective-permute-start.7 = (bf16[128,1024]{1,0:T(8,128)(2,1)}, bf16[128,1024]{1,0:T(8,128)(2,1)}, u32[]{:S(2)}, u32[]{:S(2)}) collective-permute-start(bf16[128,1024]{1,0:T(8,128)(2,1)} %slice.73), channel_id=1, source_target_pairs={{0,1},{1,2},{2,3},{3,0},{4,5},{5,6},{6,7},{7,4},{8,9},{9,10},{10,1... | collective-permute-start | bytes 786440 | tf_op jit(solution)/shard_map/ppermute | solution.py:194
  143.3 44.6 %collective-permute-start.8 = (f32[384,1024]{1,0:T(8,128)}, f32[384,1024]{1,0:T(8,128)}, u32[]{:S(2)}, u32[]{:S(2)}) collective-permute-start(f32[384,1024]{1,0:T(8,128)} %get-tuple-element.17), channel_id=1, source_target_pairs={{0,64},{64,0},{1,65},{65,1},{2,66},{66,2},{3,67},{67,3},{4,68},{68... | collective-permute-start | bytes 4718600 | tf_op jit(solution)/shard_map/ppermute | solution.py:202
  145.2 21.1 %collective-permute-start.9 = (f32[128,1024]{1,0:T(8,128)}, f32[128,1024]{1,0:T(8,128)}, u32[]{:S(2)}, u32[]{:S(2)}) collective-permute-start(f32[128,1024]{1,0:T(8,128)} %get-tuple-element.20), channel_id=1, source_target_pairs={{0,64},{64,0},{1,65},{65,1},{2,66},{66,2},{3,67},{67,3},{4,68},{68... | collective-permute-start | bytes 1572872 | tf_op jit(solution)/shard_map/ppermute | solution.py:202
  155.8 19.6 %collective-permute-start.14 = (bf16[192,1024]{1,0:T(8,128)(2,1)S(1)}, bf16[192,1024]{1,0:T(8,128)(2,1)}, u32[]{:S(2)}, u32[]{:S(2)}) collective-permute-start(bf16[192,1024]{1,0:T(8,128)(2,1)S(1)} %reshape.72), channel_id=1, source_target_pairs={{0,384},{128,0},{256,128},{384,256},{1,385},{129,1},{257,129},{385... | collective-permute-start | bytes 1179656 | tf_op jit(solution)/shard_map/ppermute | solution.py:194
  158.5 20.4 %collective-permute-start.15 = (bf16[192,1024]{1,0:T(8,128)(2,1)S(1)}, bf16[192,1024]{1,0:T(8,128)(2,1)}, u32[]{:S(2)}, u32[]{:S(2)}) collective-permute-start(bf16[192,1024]{1,0:T(8,128)(2,1)S(1)} %reshape.72), channel_id=1, source_target_pairs={{0,128},{128,256},{256,384},{384,0},{1,129},{129,257},{257,385},{3... | collective-permute-start | bytes 1179656 | tf_op jit(solution)/shard_map/ppermute | solution.py:194
  162.8 24.9 %all-to-all-start.2 = ((f32[4,32,1664]{2,1,0:T(8,128)}), f32[4,32,1664]{2,1,0:T(8,128)S(1)}, u32[]{:S(2)}, u32[]{:S(2)}) async-start(f32[4,32,1664]{2,1,0:T(8,128)} %bitcast.11), calls=%async_computation.2 | async-start | bytes 1703936 | tf_op jit(solution)/shard_map/all_to_all | solution.py:186
  168.3 38.8 %collective-permute-start.12 = (f32[64,1024]{1,0:T(8,128)}, f32[64,1024]{1,0:T(8,128)}, u32[]{:S(2)}, u32[]{:S(2)}) collective-permute-start(f32[64,1024]{1,0:T(8,128)} %get-tuple-element.28), channel_id=1, source_target_pairs={{0,384},{128,0},{256,128},{384,256},{1,385},{129,1},{257,129},{385... | collective-permute-start | bytes 786440 | tf_op jit(solution)/shard_map/ppermute | solution.py:194
  170.2 36.9 %collective-permute-start.10 = (f32[64,1024]{1,0:T(8,128)}, f32[64,1024]{1,0:T(8,128)}, u32[]{:S(2)}, u32[]{:S(2)}) collective-permute-start(f32[64,1024]{1,0:T(8,128)} %get-tuple-element.29), channel_id=1, source_target_pairs={{0,128},{128,256},{256,384},{384,0},{1,129},{129,257},{257,385},{3... | collective-permute-start | bytes 786440 | tf_op jit(solution)/shard_map/ppermute | solution.py:194
  177.0 39.1 %collective-permute-start.16 = (bf16[96,1024]{1,0:T(8,128)(2,1)}, bf16[96,1024]{1,0:T(8,128)(2,1)S(1)}, u32[]{:S(2)}, u32[]{:S(2)}) collective-permute-start(bf16[96,1024]{1,0:T(8,128)(2,1)} %slice.83), channel_id=1, source_target_pairs={{0,384},{128,0},{256,128},{384,256},{1,385},{129,1},{257,129},{385... | collective-permute-start | bytes 589832 | tf_op jit(solution)/shard_map/ppermute | solution.py:194
  180.6 35.5 %collective-permute-start.17 = (bf16[96,1024]{1,0:T(8,128)(2,1)}, bf16[96,1024]{1,0:T(8,128)(2,1)}, u32[]{:S(2)}, u32[]{:S(2)}) collective-permute-start(bf16[96,1024]{1,0:T(8,128)(2,1)} %slice.84), channel_id=1, source_target_pairs={{0,128},{128,256},{256,384},{384,0},{1,129},{129,257},{257,385},{3... | collective-permute-start | bytes 589832 | tf_op jit(solution)/shard_map/ppermute | solution.py:194
  188.0 41.7 %collective-permute-start.18 = (bf16[576,1024]{1,0:T(8,128)(2,1)S(1)}, bf16[576,1024]{1,0:T(8,128)(2,1)}, u32[]{:S(2)}, u32[]{:S(2)}) collective-permute-start(bf16[576,1024]{1,0:T(8,128)(2,1)S(1)} %constant_dynamic-update-slice_fusion.4.near_ref), channel_id=1, source_target_pairs={{0,64},{64,0},{1,65},{65,1},{2,66},{66,2},{3,67},{67,3},{4,68},{68... | collective-permute-start | bytes 3538952 | tf_op jit(solution)/shard_map/ppermute | solution.py:202
  195.2 39.2 %all-to-all-start.4 = ((f32[16,2,1664]{2,1,0:T(2,128)}), f32[16,2,1664]{2,1,0:T(2,128)S(1)}, u32[]{:S(2)}, u32[]{:S(2)}) async-start(f32[16,2,1664]{2,1,0:T(2,128)} %reshape.75), calls=%async_computation.4 | async-start | bytes 425984 | tf_op jit(solution)/shard_map/all_to_all | solution.py:186
  209.4 16.1 %collective-permute-start.11 = (f32[128,1024]{1,0:T(8,128)}, f32[128,1024]{1,0:T(8,128)S(1)}, u32[]{:S(2)}, u32[]{:S(2)}) collective-permute-start(f32[128,1024]{1,0:T(8,128)} %pad_maximum_fusion), channel_id=1, source_target_pairs={{0,128},{128,256},{256,384},{384,0},{1,129},{129,257},{257,385},{3... | collective-permute-start | bytes 1572872 | tf_op jit(solution)/shard_map/ppermute | solution.py:194
  212.2 17.5 %collective-permute-start.13 = (f32[128,1024]{1,0:T(8,128)}, f32[128,1024]{1,0:T(8,128)}, u32[]{:S(2)}, u32[]{:S(2)}) collective-permute-start(f32[128,1024]{1,0:T(8,128)} %pad_maximum_fusion.1), channel_id=1, source_target_pairs={{0,384},{128,0},{256,128},{384,256},{1,385},{129,1},{257,129},{385... | collective-permute-start | bytes 1572872 | tf_op jit(solution)/shard_map/ppermute | solution.py:194
  217.1 3.6 %collective-permute-start.19 = (bf16[192,1024]{1,0:T(8,128)(2,1)S(1)}, bf16[192,1024]{1,0:T(8,128)(2,1)S(1)}, u32[]{:S(2)}, u32[]{:S(2)}) collective-permute-start(bf16[192,1024]{1,0:T(8,128)(2,1)S(1)} %constant_dynamic-update-slice_fusion.7.far_ref), channel_id=1, source_target_pairs={{0,64},{64,0},{1,65},{65,1},{2,66},{66,2},{3,67},{67,3},{4,68},{68... | collective-permute-start | bytes 1179656 | tf_op jit(solution)/shard_map/ppermute | solution.py:202
  252.4 26.9 %all-to-all-start.6 = ((f32[16,2,1664]{2,1,0:T(2,128)}), f32[16,2,1664]{2,1,0:T(2,128)S(1)}, u32[]{:S(2)}, u32[]{:S(2)}) async-start(f32[16,2,1664]{2,1,0:T(2,128)} %reshape.79), calls=%async_computation.6 | async-start | bytes 425984 | tf_op jit(solution)/shard_map/all_to_all | solution.py:186
  (11 other events, 66.8 us)

commit v3 on v1

v3 whole, which is shorter than its diff:
```python
import jax
import jax.numpy as jnp
from jax import lax
from jax.experimental import pallas as pl
from jax.experimental.pallas import tpu as pltpu
from jax.sharding import Mesh
from jax.sharding import PartitionSpec as P

BLOCK = 128
TB_DEV = 8
SB_DEV = 10
FANOUT = 8
N_VOC = 64
NX, NC, NZ, NY = 4, 2, 16, 4
TBLOCKS = N_VOC * TB_DEV
SBLOCKS = N_VOC * SB_DEV
OWN = 2
DS = 1536
PIECE = DS // (NX * NC)
TCOLS = TB_DEV * BLOCK
SCOLS = SB_DEV * BLOCK
WIDE = DS + BLOCK

kernel_decay = 0.8
loss_scale = 256.0
F32 = jnp.float32
BF16 = jnp.bfloat16
VMEM_BYTES = 24 * 1024 * 1024
WHOLE_VMEM = 60 * 1024 * 1024


def kernel_call(kernel, out_shape, scratch=(), name=None, inputs=""):
    spaces = {"s": pltpu.SMEM, "v": pltpu.VMEM, "h": pl.ANY}
    return pl.pallas_call(
        kernel,
        out_shape=out_shape,
        in_specs=[pl.BlockSpec(memory_space=spaces[kind]) for kind in inputs],
        scratch_shapes=list(scratch),
        compiler_params=pltpu.CompilerParams(vmem_limit_bytes=WHOLE_VMEM if "h" in inputs else VMEM_BYTES),
        name=name,
    )


def arriving(array, dtype=BF16):
    return [pltpu.VMEM(array, dtype), pltpu.SemaphoreType.DMA]


def base_kernel():
    row_index = lax.broadcasted_iota(jnp.int32, (BLOCK, BLOCK), 0)
    col_index = lax.broadcasted_iota(jnp.int32, (BLOCK, BLOCK), 1)
    distance = (row_index - col_index) % BLOCK
    distance = jnp.minimum(distance, BLOCK - distance)
    return jnp.power(F32(kernel_decay), distance.astype(F32)).astype(BF16)


def split_parts(value):
    first = value.astype(BF16).astype(F32)
    second = (value - first).astype(BF16).astype(F32)
    return first, second, value - first - second


def pack_lanes(rows, values):
    lanes = lax.broadcasted_iota(jnp.int32, (rows, BLOCK), 1)
    packed = jnp.zeros((rows, BLOCK), F32)
    for place, value in enumerate(values):
        for step, part in enumerate(split_parts(value)):
            packed = jnp.where(lanes == 3 * place + step, part, packed)
    return packed.astype(BF16)


def unpack_lane(packed, place):
    spot = 3 * place
    cols = packed[:, spot : spot + 3].astype(F32)
    return (cols[:, 0:1] + cols[:, 1:2]) + cols[:, 2:3]


def put_rows(full_ref, spots_ref, step, core, value):
    x = (spots_ref[0] + step) % NX
    start = (x * NC + core) * PIECE
    full_ref[pl.ds(pl.multiple_of(start, 64), PIECE), :] = value


def student_kernel(spots_ref, hidden_ref, mine_ref, theirs_ref, head_ref, logits_ref, stats_ref):
    c = spots_ref[1]
    for step in range(NX):
        rows = slice(step * PIECE, (step + 1) * PIECE)
        put_rows(head_ref, spots_ref, step, c, mine_ref[rows, :])
        put_rows(head_ref, spots_ref, step, 1 - c, theirs_ref[rows, :])
    logits = jnp.dot(hidden_ref[...], head_ref[...], preferred_element_type=F32)
    top = jnp.max(logits, axis=1, keepdims=True)
    total = jnp.sum(jnp.exp(logits - top), axis=1, keepdims=True)
    logits_ref[...] = logits
    lanes = lax.broadcasted_iota(jnp.int32, stats_ref.shape, 1)
    stats_ref[...] = jnp.where(lanes == 0, top, total)


def rows_kernel(spots_ref, gathered_ref, head_ref, far_ref, rest_ref, mine_ref, rows_ref, theirs_ref):
    x, c = spots_ref[0], spots_ref[1]
    part = gathered_ref.shape[0] // (NZ * NY)
    for spot in range(NY):
        for z in range(NZ):
            rows_ref[(z * NY + spot) * part : (z * NY + spot + 1) * part, :] = gathered_ref[
                (spot * NZ + z) * part : (spot * NZ + z + 1) * part, :
            ]
    chunk = far_ref.shape[0]
    for place, step in enumerate((2, 1, 3, 0)):
        first = ((x + step) % NX) * NC
        spot = slice(place * chunk, (place + 1) * chunk)
        theirs_ref[spot, :] = rows_ref[pl.ds(pl.multiple_of((first + 1 - c) * chunk, chunk), chunk), :]
        mine_ref[spot, :] = rows_ref[pl.ds(pl.multiple_of((first + c) * chunk, chunk), chunk), :]
    product = jnp.dot(theirs_ref[...], head_ref[...], preferred_element_type=F32)
    far_ref[...] = product[:chunk, :]
    rest_ref[...] = product[chunk:, :]


def softmax_kernel(own_ref, prev_ref, next_ref, stats_ref, out_ref):
    logits = own_ref[...] + prev_ref[...] + next_ref[...]
    peak = jnp.max(logits, axis=1, keepdims=True)
    out_ref[:, :TCOLS] = jnp.exp(logits - peak).astype(BF16)
    out_ref[:, TCOLS:] = pack_lanes(out_ref.shape[0], [peak, stats_ref[:, 0:1], stats_ref[:, 1:2]])


def align_kernel(recv_ref, table_ref, source_ref, shift_ref, out_ref, rolled_ref, weight_ref, sem):
    copy = pltpu.make_async_copy(source_ref, weight_ref, sem)
    copy.start()
    lanes = lax.broadcasted_iota(jnp.int32, (TBLOCKS, BLOCK), 1)
    for t in range(OWN):
        extra = recv_ref[t, :, TCOLS:]
        peak = unpack_lane(extra, 0)
        scale = jnp.exp(peak - jnp.max(peak, axis=0, keepdims=True))
        smooth = []
        for j in range(TB_DEV):
            probs = recv_ref[t, :, j * BLOCK : (j + 1) * BLOCK]
            tile = jnp.dot(probs, table_ref[...], preferred_element_type=F32) * scale
            smooth.append(tile.astype(BF16).astype(F32))
        smooth = jnp.concatenate(smooth, axis=0)
        for k in range(FANOUT):
            index = (lanes - shift_ref[:, k : k + 1]) & (BLOCK - 1)
            rolled = jnp.take_along_axis(smooth, index, axis=1)
            rolled_ref[k * TBLOCKS : (k + 1) * TBLOCKS, t * BLOCK : (t + 1) * BLOCK] = rolled.astype(BF16)
    copy.wait()
    aligned = jnp.dot(weight_ref[...], rolled_ref[...], preferred_element_type=F32)
    for t in range(OWN):
        mine = aligned[:, t * BLOCK : (t + 1) * BLOCK]
        norm = jnp.sum(jnp.sum(mine, axis=0, keepdims=True), axis=1, keepdims=True)
        mine = mine / norm
        for b in range(SB_DEV):
            out_ref[t, :, b * BLOCK : (b + 1) * BLOCK] = mine[b * N_VOC : (b + 1) * N_VOC, :].astype(BF16)
        extra = recv_ref[t, :, TCOLS:]
        top = unpack_lane(extra, 1)
        total = unpack_lane(extra, 2)
        joint_top = jnp.max(top, axis=0, keepdims=True)
        joint_total = jnp.sum(total * jnp.exp(top - joint_top), axis=0, keepdims=True)
        log_total = joint_top + jnp.log(joint_total)
        out_ref[t, :, SCOLS:] = pack_lanes(N_VOC, [log_total])


def grad_kernel(target_ref, logits_ref, source_ref, out_ref, log_ref, head_ref, sem):
    copy = pltpu.make_async_copy(source_ref, head_ref, sem)
    copy.start()
    log_total = unpack_lane(target_ref[:, SCOLS:], 0)
    target = target_ref[:, :SCOLS].astype(F32)
    logits = logits_ref[...]
    cross = jnp.sum(target * logits, axis=1, keepdims=True)
    grad = (loss_scale * (jnp.exp(logits - log_total) - target)).astype(BF16)
    copy.wait()
    out_ref[:, :DS] = lax.dot_general(
        grad, head_ref[...], (((1,), (1,)), ((), ())), preferred_element_type=F32
    )
    out_ref[:, DS:] = jnp.broadcast_to(cross, (out_ref.shape[0], BLOCK))
    log_ref[...] = jnp.broadcast_to(log_total, log_ref.shape)


def finish_kernel(parts_ref, out_ref):
    terms = parts_ref[0]
    for i in range(1, NZ):
        terms = terms + parts_ref[i]
    out_ref[:, :DS] = terms[:, :DS].astype(BF16)
    out_ref[:, DS:] = pack_lanes(OWN, [terms[:, DS : DS + 1]])


def exchange(value, axis):
    return lax.all_to_all(value, axis, split_axis=0, concat_axis=0, tiled=True)


def spread(value, axis, size):
    return exchange(jnp.broadcast_to(value[None], (size,) + value.shape), axis)


def send(value, axis, size, step):
    return lax.ppermute(value, axis, [(i, (i + step) % size) for i in range(size)])


def send_x(value, step):
    return send(value, "x", NX, step)


def send_c(value):
    return lax.ppermute(value, "c", [(0, 1), (1, 0)])


def by_source(pairs):
    return pairs.reshape(N_VOC, TB_DEV, FANOUT).transpose(1, 0, 2).reshape(TBLOCKS, FANOUT)


def logit_parts(rows, head, spots):
    width = rows.shape[-1]
    rows = rows.reshape(-1, width)
    chunk = rows.shape[0] // (NX * NC)
    far_theirs, theirs, mine = kernel_call(
        rows_kernel,
        (
            jax.ShapeDtypeStruct((chunk, TCOLS), F32),
            jax.ShapeDtypeStruct((3 * chunk, TCOLS), F32),
            jax.ShapeDtypeStruct((4 * chunk, width), BF16),
        ),
        [pltpu.VMEM(rows.shape, BF16), pltpu.VMEM((4 * chunk, width), BF16)] ,
        "rows",
        "svv",
    )(spots, rows, head)
    far_theirs = send_c(far_theirs)
    theirs = send_c(theirs)
    mine = jnp.dot(mine, head, preferred_element_type=F32)
    far = mine[:chunk] + far_theirs
    half = chunk // 2
    low = send_x(far[:half], 1)
    high = send_x(far[half:], -1)
    near = mine[chunk:] + theirs
    after = jnp.concatenate([near[:half] + low, near[half:chunk]], axis=0)
    before = jnp.concatenate([near[chunk : chunk + half], near[chunk + half : 2 * chunk] + high], axis=0)
    return near[2 * chunk :], send_x(after, 1), send_x(before, -1)


def body(
    teacher_hidden,
    teacher_head,
    student_hidden,
    student_head,
    pair_owner,
    pair_block,
    pair_shift,
    pair_count,
):
    tok_rows = student_hidden.shape[0]
    spots = jnp.stack([lax.axis_index("x"), lax.axis_index("c")]).astype(jnp.int32)

    rows = spread(teacher_hidden, "z", NZ)
    head_mine = jnp.concatenate(
        [student_head, send_x(student_head, -1), send_x(student_head, 2), send_x(student_head, 1)], axis=0
    )
    head_theirs = send_c(head_mine)
    rows = spread(rows, "y", NY)

    shift = by_source(pair_shift)
    place = by_source(pair_block * N_VOC + pair_owner).T.reshape(1, -1)
    count = by_source(pair_count).T.reshape(1, -1)
    weight = jnp.where(
        place == lax.broadcasted_iota(jnp.int32, (SBLOCKS, TBLOCKS * FANOUT), 0), count, 0
    ).astype(BF16)

    head_full, student_logits, stats = kernel_call(
        student_kernel,
        (
            jax.ShapeDtypeStruct((DS, SCOLS), BF16),
            jax.ShapeDtypeStruct((tok_rows, SCOLS), F32),
            jax.ShapeDtypeStruct((tok_rows, BLOCK), F32),
        ),
        (),
        "student",
        "svvv",
    )(spots, student_hidden, head_mine, head_theirs)
    rows, weight, shift, stats = lax.optimization_barrier((rows, weight, shift, stats))

    own, before, after = logit_parts(rows, teacher_head, spots)
    outgoing = kernel_call(
        softmax_kernel, jax.ShapeDtypeStruct((tok_rows, TCOLS + BLOCK), BF16), name="softmax", inputs="vvvv"
    )(own, before, after, stats)
    received = exchange(outgoing.reshape(N_VOC, OWN, TCOLS + BLOCK), ("z", "y"))
    target = kernel_call(
        align_kernel,
        jax.ShapeDtypeStruct((OWN, N_VOC, SCOLS + BLOCK), BF16),
        [pltpu.VMEM((FANOUT * TBLOCKS, OWN * BLOCK), BF16)] + arriving((SBLOCKS, FANOUT * TBLOCKS)),
        "align",
        "vvhv",
    )(received.transpose(1, 0, 2), base_kernel(), weight, shift)
    target = exchange(target.transpose(1, 0, 2), ("z", "y")).reshape(tok_rows, SCOLS + BLOCK)

    terms, log_total = kernel_call(
        grad_kernel,
        (jax.ShapeDtypeStruct((tok_rows, WIDE), F32), jax.ShapeDtypeStruct((tok_rows, BLOCK), F32)),
        arriving((DS, SCOLS)),
        "gradient",
        "vvh",
    )(target, student_logits, head_full)
    terms = exchange(terms.reshape(NY, tok_rows // NY, WIDE), "y").sum(axis=0)
    terms = exchange(terms.reshape(NZ, OWN, WIDE), "z")
    result = kernel_call(
        finish_kernel, jax.ShapeDtypeStruct((OWN, WIDE), BF16), name="finish", inputs="v"
    )(terms)
    result = spread(result, "z", NZ).reshape(NZ * OWN, WIDE)
    result = spread(result, "y", NY).reshape(tok_rows, WIDE)
    token_loss = log_total[:, 0] - unpack_lane(result[:, DS:], 0)[:, 0]
    return (token_loss, result[:, :DS])


def solution(mesh):
    grid = Mesh(mesh.devices.reshape(NX, NC, NZ, NY), ("x", "c", "z", "y"))
    tok = ("x", "c")
    voc = ("z", "y")
    in_specs = (
        P(voc, tok),
        P(tok, voc),
        P(tok, None),
        P(tok, voc),
        P(),
        P(),
        P(),
        P(),
    )
    out_specs = (P(tok), P(tok, None))
    return jax.shard_map(body, mesh=grid, in_specs=in_specs, out_specs=out_specs, check_vma=False)
```

time: 284 us -> 272 us (0.958); the launches traced: 284 us -> 269 us
  blocking collectives: 163 us -> 88.8 us
  starting transfers between devices: 15.9 us -> 62.7 us
  waiting for transfers between devices: 55 us -> 71.3 us
  Pallas kernels: 5.43 us -> 19 us
  between operations: 14.3 us -> 0.93 us
  matrix products: 10.7 us -> 1.25 us
  local copies, waits for them, and re-layouts: 11 us -> 18.8 us
    all_to_all x7 -> x5, blocking collectives: 163 us -> 88.8 us  [exchange(): return lax.all_to_all(value, axis, split_axis=0, concat_axis=0, tiled=True)]
    reduce_scatter x1 -> x0, waiting for transfers between devices: 38.1 us -> none  [body(): lax.psum_scatter(partial_logits, ('x', 'c'), scatter_dimension=0, tiled=T...]
    ppermute x0 -> x10, waiting for transfers between devices: none -> 35.2 us  [the longest x7 34.8 us: send(): lax.ppermute(value, axis, [(i, (i + step) % size) for i in range(size)])]
    ppermute x0 -> x10, starting transfers between devices: none -> 29.5 us  [the longest x7 23.3 us: send(): lax.ppermute(value, axis, [(i, (i + step) % size) for i in range(size)])]
    all_to_all x1 -> x3, waiting for transfers between devices: 16.3 us -> 36.1 us  [exchange(): return lax.all_to_all(value, axis, split_axis=0, concat_axis=0, tiled=True)]
    all_to_all x1 -> x3, starting transfers between devices: 15.8 us -> 33.2 us  [exchange(): return lax.all_to_all(value, axis, split_axis=0, concat_axis=0, tiled=True)]
    pallas_call x1 -> x6, Pallas kernels: 5.43 us -> 19 us  [the longest x1 7.78 us: body(): kernel_call(align_kernel, jax.ShapeDtypeStruct((OWN, N_VOC, SCOLS + BLOCK...]
    dot_general x3 -> x1, matrix products: 10.7 us -> 1.25 us  [logit_parts(): mine = jnp.dot(mine, head, preferred_element_type=F32)]
  transfers between devices with their start and end apart: 3 -> 13, of which waited for: 2 -> 9; matrix products, arithmetic and copies ran while one was open for 6% -> 5% of each run, Pallas kernels for 0% -> 1%
where the time goes in v3:
time: 272 us; the launch traced here: 269 us
  blocking collectives  88.8 us (33%)
  waiting for transfers between devices  71.3 us (26%)
  starting transfers between devices  62.7 us (23%)
  Pallas kernels  19 us (7%)
  local copies, waits for them, and re-layouts  18.8 us (7%)
  other arithmetic  6 us (2%)
    all_to_all x5, blocking collectives, exchange(): return lax.all_to_all(value, axis, split_axis=0, concat_axis=0, tiled=True)  88.8 us
    all_to_all x3, waiting for transfers between devices, exchange(): return lax.all_to_all(value, axis, split_axis=0, concat_axis=0, tiled=True)  36.1 us
    ppermute x7, waiting for transfers between devices, send(): lax.ppermute(value, axis, [(i, (i + step) % size) for i in range(size)])  34.8 us
    all_to_all x3, starting transfers between devices, exchange(): return lax.all_to_all(value, axis, split_axis=0, concat_axis=0, tiled=True)  33.2 us
    ppermute x7, starting transfers between devices, send(): lax.ppermute(value, axis, [(i, (i + step) % size) for i in range(size)])  23.3 us
    unnamed x23, local copies, waits for them, and re-layouts  8 us
    pallas_call x1, Pallas kernels, body(): kernel_call(align_kernel, jax.ShapeDtypeStruct((OWN, N_VOC, SCOLS + BLOCK...  7.78 us
    ppermute x3, starting transfers between devices, send_c(): return lax.ppermute(value, 'c', [(0, 1), (1, 0)])  6.24 us
  transfers between devices with their start and end apart: 13, of which 9 were waited for; matrix products, arithmetic and copies ran while one was open for 5% of the time, Pallas kernels for 1%

profile of v3, /device:TPU:6, one launch (start us, length us, event | category | flops | bytes accessed | tf_op | source)
XLA Modules:
  0.0 268.8 jit_solution(11018878081658605486)
XLA Ops:
  0.6 1.6 broadcast_in_dim.39
  2.3 15.2 %all-to-all-start = ((bf16[16,16,1024]{2,1,0:T(8,128)(2,1)}), bf16[16,16,1024]{2,1,0:T(8,128)(2,1)S(1)}, u32[]{:S(2)}, u32[]{:S(2)}) async-start(bf16[16,16,1024]{2,1,0:T(8,128)(2,1)} %broadcast_in_dim.39), calls=%async_computation | async-start | bytes 1048576 | tf_op jit(solution)/shard_map/all_to_all | solution.py:183
  17.5 2.7 %collective-permute-start = (bf16[192,1280]{1,0:T(8,128)(2,1)}, bf16[192,1280]{1,0:T(8,128)(2,1)S(1)}, u32[]{:S(2)}, u32[]{:S(2)}) collective-permute-start(bf16[192,1280]{1,0:T(8,128)(2,1)} %param.11), channel_id=1, source_target_pairs={{0,384},{128,0},{256,128},{384,256},{1,385},{129,1},{257,129},{385... | collective-permute-start | bytes 1474568 | tf_op jit(solution)/shard_map/ppermute | solution.py:191
  20.2 3.0 %collective-permute-start.1 = (bf16[192,1280]{1,0:T(8,128)(2,1)}, bf16[192,1280]{1,0:T(8,128)(2,1)S(1)}, u32[]{:S(2)}, u32[]{:S(2)}) collective-permute-start(bf16[192,1280]{1,0:T(8,128)(2,1)} %param.11), channel_id=1, source_target_pairs={{0,256},{128,384},{256,0},{384,128},{1,257},{129,385},{257,1},{385... | collective-permute-start | bytes 1474568 | tf_op jit(solution)/shard_map/ppermute | solution.py:191
  23.2 4.0 %collective-permute-start.2 = (bf16[192,1280]{1,0:T(8,128)(2,1)}, bf16[192,1280]{1,0:T(8,128)(2,1)S(1)}, u32[]{:S(2)}, u32[]{:S(2)}) collective-permute-start(bf16[192,1280]{1,0:T(8,128)(2,1)} %param.11), channel_id=1, source_target_pairs={{0,128},{128,256},{256,384},{384,0},{1,129},{129,257},{257,385},{3... | collective-permute-start | bytes 1474568 | tf_op jit(solution)/shard_map/ppermute | solution.py:191
  27.2 1.9 constant_dynamic-update-slice_fusion.3
  29.1 14.9 %collective-permute-done = bf16[192,1280]{1,0:T(8,128)(2,1)S(1)} collective-permute-done((bf16[192,1280]{1,0:T(8,128)(2,1)}, bf16[192,1280]{1,0:T(8,128)(2,1)S(1)}, u32[]{:S(2)}, u32[]{:S(2)}) %collective-permute-start) | collective-permute-done | bytes 491552 | tf_op jit(solution)/shard_map/ppermute | solution.py:191
  47.4 1.9 collective-permute-start.3
  50.9 4.6 %all-to-all-start.1 = ((bf16[4,16,16,1024]{3,2,1,0:T(8,128)(2,1)}), bf16[4,16,16,1024]{3,2,1,0:T(8,128)(2,1)S(1)}, u32[]{:S(2)}, u32[]{:S(2)}) async-start(bf16[4,16,16,1024]{3,2,1,0:T(8,128)(2,1)} %broadcast_in_dim.40), calls=%async_computation.1 | async-start | bytes 4194304 | tf_op jit(solution)/shard_map/all_to_all | solution.py:183
  57.5 4.0 %select_convert_fusion.source_ref = bf16[640,4096]{1,0:T(8,128)(2,1)} fusion(s32[4096]{0:T(1024)S(1)} %bitcast.42, s32[4096]{0:T(1024)S(1)} %bitcast.41), kind=kLoop, calls=%fused_computation | loop fusion | flops 7864320 | bytes 5275648 | tf_op jit(solution)/shard_map/convert_element_type | solution.py:259
  61.5 3.3 %student.1 = (bf16[1536,1280]{1,0:T(8,128)(2,1)S(1)}, f32[128,1280]{1,0:T(8,128)S(1)}, f32[128,128]{1,0:T(8,128)S(1)}) custom-call(s32[2]{0:T(128)S(1)} %pad_add_fusion.spots_ref, bf16[128,1536]{1,0:T(8,128)(2,1)S(1)} %copy-done.3, bf16[768,1280]{1,0:T(8,128)(2,1)} %constant_dynamic-update-slice_fusion.mine_ref, ...), custom_call_target="tpu_custom_call" | custom-call | tf_op jit(solution)/shard_map/student/pallas_call | solution.py:261
  64.8 1.9 copy-done
  67.6 14.9 %all-to-all-done.1 = bf16[4,16,16,1024]{3,2,1,0:T(8,128)(2,1)S(1)} async-done(((bf16[4,16,16,1024]{3,2,1,0:T(8,128)(2,1)}), bf16[4,16,16,1024]{3,2,1,0:T(8,128)(2,1)S(1)}, u32[]{:S(2)}, u32[]{:S(2)}) %all-to-all-start.1) | async-done | bytes 2097184 | tf_op jit(solution)/shard_map/all_to_all | solution.py:183
  84.1 1.9 rows.1
  86.0 1.9 collective-permute-start.4
  88.0 2.4 collective-permute-start.5
  92.2 4.5 %collective-permute-start.6 = (f32[64,1024]{1,0:T(8,128)S(1)}, f32[64,1024]{1,0:T(8,128)S(1)}, u32[]{:S(2)}, u32[]{:S(2)}) collective-permute-start(f32[64,1024]{1,0:T(8,128)S(1)} %get-tuple-element.31), channel_id=1, source_target_pairs={{0,128},{128,256},{256,384},{384,0},{1,129},{129,257},{257,385},{3... | collective-permute-start | bytes 786440 | tf_op jit(solution)/shard_map/ppermute | solution.py:191
  96.7 1.9 collective-permute-start.8
  98.9 3.7 %collective-permute-done.6 = f32[64,1024]{1,0:T(8,128)S(1)} collective-permute-done((f32[64,1024]{1,0:T(8,128)S(1)}, f32[64,1024]{1,0:T(8,128)S(1)}, u32[]{:S(2)}, u32[]{:S(2)}) %collective-permute-start.6) | collective-permute-done | bytes 262176 | tf_op jit(solution)/shard_map/ppermute | solution.py:191
  102.6 5.3 %collective-permute-done.8 = f32[64,1024]{1,0:T(8,128)S(1)} collective-permute-done((f32[64,1024]{1,0:T(8,128)S(1)}, f32[64,1024]{1,0:T(8,128)S(1)}, u32[]{:S(2)}, u32[]{:S(2)}) %collective-permute-start.8) | collective-permute-done | bytes 262176 | tf_op jit(solution)/shard_map/ppermute | solution.py:191
  108.1 1.9 collective-permute-start.9
  110.1 5.1 %collective-permute-start.7 = (f32[128,1024]{1,0:T(8,128)S(1)}, f32[128,1024]{1,0:T(8,128)S(1)}, u32[]{:S(2)}, u32[]{:S(2)}) collective-permute-start(f32[128,1024]{1,0:T(8,128)S(1)} %pad_maximum_fusion), channel_id=1, source_target_pairs={{0,128},{128,256},{256,384},{384,0},{1,129},{129,257},{257,385},{3... | collective-permute-start | bytes 1572872 | tf_op jit(solution)/shard_map/ppermute | solution.py:191
  115.3 8.8 %collective-permute-done.9.next_ref = f32[128,1024]{1,0:T(8,128)S(1)} collective-permute-done((f32[128,1024]{1,0:T(8,128)S(1)}, f32[128,1024]{1,0:T(8,128)S(1)}, u32[]{:S(2)}, u32[]{:S(2)}) %collective-permute-start.9) | collective-permute-done | bytes 524320 | tf_op jit(solution)/shard_map/ppermute | solution.py:191
  126.4 13.4 %all-to-all-start.2 = ((bf16[64,2,1152]{2,1,0:T(2,128)(2,1)}), bf16[64,2,1152]{2,1,0:T(2,128)(2,1)S(1)}, u32[]{:S(2)}, u32[]{:S(2)}) async-start(bf16[64,2,1152]{2,1,0:T(2,128)(2,1)} %reshape.56), calls=%async_computation.2 | async-start | bytes 589824 | tf_op jit(solution)/shard_map/all_to_all | solution.py:183
  140.5 21.2 %all-to-all-done.2 = bf16[64,2,1152]{2,1,0:T(2,128)(2,1)S(1)} async-done(((bf16[64,2,1152]{2,1,0:T(2,128)(2,1)}), bf16[64,2,1152]{2,1,0:T(2,128)(2,1)S(1)}, u32[]{:S(2)}, u32[]{:S(2)}) %all-to-all-start.2) | async-done | bytes 294944 | tf_op jit(solution)/shard_map/all_to_all | solution.py:183
  162.4 7.8 %align.1 = bf16[2,64,1408]{2,1,0:T(8,128)(2,1)} custom-call(bf16[2,64,1152]{2,1,0:T(8,128)(2,1)} %bitcast.35, bf16[128,128]{1,0:T(8,128)(2,1)} %fusion.3.table_ref, bf16[640,4096]{1,0:T(8,128)(2,1)} %select_convert_fusion.source_ref, s32[512,8]{1,0:T(8,128)} %bitcast.36), custom_call_target="tpu_custom_call" | custom-call | tf_op jit(solution)/shard_map/align/pallas_call | solution.py:279
  171.6 29.4 %all_to_all.40 = bf16[64,2,1408]{2,1,0:T(2,128)(2,1)S(1)} all-to-all(bf16[64,2,1408]{2,1,0:T(2,128)(2,1)S(1)} %copy.21), channel_id=1, replica_groups=mesh['x'=4,'c'=2,'z'=16,'y'=4] {'z','y'}, dimensions={0} | all-to-all | bytes 720896 | tf_op jit(solution)/shard_map/all_to_all | solution.py:183
  201.9 5.6 %gradient.1 = (f32[128,1664]{1,0:T(8,128)}, f32[128,128]{1,0:T(8,128)}) custom-call(bf16[128,1408]{1,0:T(8,128)(2,1)} %reshape.57.target_ref, f32[128,1280]{1,0:T(8,128)} %copy-done.2, bf16[1536,1280]{1,0:T(8,128)(2,1)} %copy-done), custom_call_target="tpu_custom_call" | custom-call | tf_op jit(solution)/shard_map/gradient/pallas_call | solution.py:288
  207.5 13.4 %all_to_all.41 = f32[4,32,1664]{2,1,0:T(8,128)S(1)} all-to-all(f32[4,32,1664]{2,1,0:T(8,128)} %bitcast.40), channel_id=1, replica_groups=mesh['x'=4,'c'=2,'z'=16,'y'=4] {'y'}, dimensions={0} | all-to-all | bytes 1703936 | tf_op jit(solution)/shard_map/all_to_all | solution.py:183
  221.2 18.1 %all_to_all.42.parts_ref = f32[16,2,1664]{2,1,0:T(2,128)S(1)} all-to-all(f32[16,2,1664]{2,1,0:T(2,128)S(1)} %reshape.59), channel_id=1, replica_groups=mesh['x'=4,'c'=2,'z'=16,'y'=4] {'z'}, dimensions={0} | all-to-all | bytes 425984 | tf_op jit(solution)/shard_map/all_to_all | solution.py:183
  239.4 17.9 %all_to_all.43 = bf16[16,2,1664]{2,1,0:T(2,128)(2,1)S(1)} all-to-all(bf16[16,2,1664]{2,1,0:T(2,128)(2,1)S(1)} %broadcast_in_dim.44), channel_id=1, replica_groups=mesh['x'=4,'c'=2,'z'=16,'y'=4] {'z'}, dimensions={0} | all-to-all | bytes 212992 | tf_op jit(solution)/shard_map/all_to_all | solution.py:183
  257.4 9.9 %all_to_all.44 = bf16[4,32,1664]{2,1,0:T(8,128)(2,1)S(1)} all-to-all(bf16[4,32,1664]{2,1,0:T(8,128)(2,1)S(1)} %broadcast_in_dim.46), channel_id=1, replica_groups=mesh['x'=4,'c'=2,'z'=16,'y'=4] {'y'}, dimensions={0} | all-to-all | bytes 851968 | tf_op jit(solution)/shard_map/all_to_all | solution.py:183
  (63 shorter events, 19.4 us)
Async XLA Ops:
  2.3 47.1 %all-to-all-start = ((bf16[16,16,1024]{2,1,0:T(8,128)(2,1)}), bf16[16,16,1024]{2,1,0:T(8,128)(2,1)S(1)}, u32[]{:S(2)}, u32[]{:S(2)}) async-start(bf16[16,16,1024]{2,1,0:T(8,128)(2,1)} %broadcast_in_dim.39), calls=%async_computation | async-start | bytes 1048576 | tf_op jit(solution)/shard_map/all_to_all | solution.py:183
  17.5 26.5 %collective-permute-start = (bf16[192,1280]{1,0:T(8,128)(2,1)}, bf16[192,1280]{1,0:T(8,128)(2,1)S(1)}, u32[]{:S(2)}, u32[]{:S(2)}) collective-permute-start(bf16[192,1280]{1,0:T(8,128)(2,1)} %param.11), channel_id=1, source_target_pairs={{0,384},{128,0},{256,128},{384,256},{1,385},{129,1},{257,129},{385... | collective-permute-start | bytes 1474568 | tf_op jit(solution)/shard_map/ppermute | solution.py:191
  20.2 24.6 %collective-permute-start.1 = (bf16[192,1280]{1,0:T(8,128)(2,1)}, bf16[192,1280]{1,0:T(8,128)(2,1)S(1)}, u32[]{:S(2)}, u32[]{:S(2)}) collective-permute-start(bf16[192,1280]{1,0:T(8,128)(2,1)} %param.11), channel_id=1, source_target_pairs={{0,256},{128,384},{256,0},{384,128},{1,257},{129,385},{257,1},{385... | collective-permute-start | bytes 1474568 | tf_op jit(solution)/shard_map/ppermute | solution.py:191
  23.2 23.3 %collective-permute-start.2 = (bf16[192,1280]{1,0:T(8,128)(2,1)}, bf16[192,1280]{1,0:T(8,128)(2,1)S(1)}, u32[]{:S(2)}, u32[]{:S(2)}) collective-permute-start(bf16[192,1280]{1,0:T(8,128)(2,1)} %param.11), channel_id=1, source_target_pairs={{0,128},{128,256},{256,384},{384,0},{1,129},{129,257},{257,385},{3... | collective-permute-start | bytes 1474568 | tf_op jit(solution)/shard_map/ppermute | solution.py:191
  47.4 14.1 %collective-permute-start.3 = (bf16[768,1280]{1,0:T(8,128)(2,1)}, bf16[768,1280]{1,0:T(8,128)(2,1)}, u32[]{:S(2)}, u32[]{:S(2)}) collective-permute-start(bf16[768,1280]{1,0:T(8,128)(2,1)} %constant_dynamic-update-slice_fusion.mine_ref), channel_id=1, source_target_pairs={{0,64},{64,0},{1,65},{65,1},{2,66},{66,2},{3,67},{67,3},{4,68},{68... | collective-permute-start | bytes 5898248 | tf_op jit(solution)/shard_map/ppermute | solution.py:199
  50.9 4.6 %copy-start.5 = (s32[512,8]{0,1:T(8,128)S(1)}, s32[512,8]{0,1:T(8,128)}, u32[]{:S(2)}) copy-start(s32[512,8]{0,1:T(8,128)} %param.12) | copy-start | bytes 49156
  50.9 4.6 %copy-start.6 = (s32[512,8]{0,1:T(8,128)S(1)}, s32[512,8]{0,1:T(8,128)}, u32[]{:S(2)}) copy-start(s32[512,8]{0,1:T(8,128)} %param.13) | copy-start | bytes 49156
  50.9 5.0 %copy-start.7 = (s32[512,8]{0,1:T(8,128)S(1)}, s32[512,8]{0,1:T(8,128)}, u32[]{:S(2)}) copy-start(s32[512,8]{0,1:T(8,128)} %param.15) | copy-start | bytes 49156
  50.9 5.4 %copy-start.8 = (s32[512,8]{0,1:T(8,128)S(1)}, s32[512,8]{0,1:T(8,128)}, u32[]{:S(2)}) copy-start(s32[512,8]{0,1:T(8,128)} %param.14) | copy-start | bytes 49156
  50.9 31.6 %all-to-all-start.1 = ((bf16[4,16,16,1024]{3,2,1,0:T(8,128)(2,1)}), bf16[4,16,16,1024]{3,2,1,0:T(8,128)(2,1)S(1)}, u32[]{:S(2)}, u32[]{:S(2)}) async-start(bf16[4,16,16,1024]{3,2,1,0:T(8,128)(2,1)} %broadcast_in_dim.40), calls=%async_computation.1 | async-start | bytes 4194304 | tf_op jit(solution)/shard_map/all_to_all | solution.py:183
  57.5 4.0 %copy-start.3 = (bf16[128,1536]{1,0:T(8,128)(2,1)S(1)}, bf16[128,1536]{1,0:T(8,128)(2,1)}, u32[]{:S(2)}) copy-start(bf16[128,1536]{1,0:T(8,128)(2,1)} %hidden_ref.1) | copy-start | bytes 1179652
  64.8 1.9 copy-start
  66.8 0.9 copy-start.2
  82.5 1.6 copy-start.1
  86.0 12.6 %collective-permute-start.4 = (f32[384,1024]{1,0:T(8,128)S(1)}, f32[384,1024]{1,0:T(8,128)S(1)}, u32[]{:S(2)}, u32[]{:S(2)}) collective-permute-start(f32[384,1024]{1,0:T(8,128)S(1)} %get-tuple-element.17), channel_id=1, source_target_pairs={{0,64},{64,0},{1,65},{65,1},{2,66},{66,2},{3,67},{67,3},{4,68},{68... | collective-permute-start | bytes 4718600 | tf_op jit(solution)/shard_map/ppermute | solution.py:199
  88.0 4.1 %collective-permute-start.5 = (f32[128,1024]{1,0:T(8,128)S(1)}, f32[128,1024]{1,0:T(8,128)S(1)}, u32[]{:S(2)}, u32[]{:S(2)}) collective-permute-start(f32[128,1024]{1,0:T(8,128)S(1)} %get-tuple-element.18), channel_id=1, source_target_pairs={{0,64},{64,0},{1,65},{65,1},{2,66},{66,2},{3,67},{67,3},{4,68},{68... | collective-permute-start | bytes 1572872 | tf_op jit(solution)/shard_map/ppermute | solution.py:199
  92.2 10.4 %collective-permute-start.6 = (f32[64,1024]{1,0:T(8,128)S(1)}, f32[64,1024]{1,0:T(8,128)S(1)}, u32[]{:S(2)}, u32[]{:S(2)}) collective-permute-start(f32[64,1024]{1,0:T(8,128)S(1)} %get-tuple-element.31), channel_id=1, source_target_pairs={{0,128},{128,256},{256,384},{384,0},{1,129},{129,257},{257,385},{3... | collective-permute-start | bytes 786440 | tf_op jit(solution)/shard_map/ppermute | solution.py:191
  96.7 11.2 %collective-permute-start.8 = (f32[64,1024]{1,0:T(8,128)S(1)}, f32[64,1024]{1,0:T(8,128)S(1)}, u32[]{:S(2)}, u32[]{:S(2)}) collective-permute-start(f32[64,1024]{1,0:T(8,128)S(1)} %get-tuple-element.30), channel_id=1, source_target_pairs={{0,384},{128,0},{256,128},{384,256},{1,385},{129,1},{257,129},{385... | collective-permute-start | bytes 786440 | tf_op jit(solution)/shard_map/ppermute | solution.py:191
  108.1 16.0 %collective-permute-start.9 = (f32[128,1024]{1,0:T(8,128)S(1)}, f32[128,1024]{1,0:T(8,128)S(1)}, u32[]{:S(2)}, u32[]{:S(2)}) collective-permute-start(f32[128,1024]{1,0:T(8,128)S(1)} %pad_maximum_fusion.1), channel_id=1, source_target_pairs={{0,384},{128,0},{256,128},{384,256},{1,385},{129,1},{257,129},{385... | collective-permute-start | bytes 1572872 | tf_op jit(solution)/shard_map/ppermute | solution.py:191
  110.1 15.2 %collective-permute-start.7 = (f32[128,1024]{1,0:T(8,128)S(1)}, f32[128,1024]{1,0:T(8,128)S(1)}, u32[]{:S(2)}, u32[]{:S(2)}) collective-permute-start(f32[128,1024]{1,0:T(8,128)S(1)} %pad_maximum_fusion), channel_id=1, source_target_pairs={{0,128},{128,256},{256,384},{384,0},{1,129},{129,257},{257,385},{3... | collective-permute-start | bytes 1572872 | tf_op jit(solution)/shard_map/ppermute | solution.py:191
  126.4 35.3 %all-to-all-start.2 = ((bf16[64,2,1152]{2,1,0:T(2,128)(2,1)}), bf16[64,2,1152]{2,1,0:T(2,128)(2,1)S(1)}, u32[]{:S(2)}, u32[]{:S(2)}) async-start(bf16[64,2,1152]{2,1,0:T(2,128)(2,1)} %reshape.56), calls=%async_computation.2 | async-start | bytes 589824 | tf_op jit(solution)/shard_map/all_to_all | solution.py:183
  221.0 47.1 %copy-start.4 = (f32[128,128]{1,0:T(8,128)S(1)}, f32[128,128]{1,0:T(8,128)}, u32[]{:S(2)}) copy-start(f32[128,128]{1,0:T(8,128)} %get-tuple-element.24) | copy-start | bytes 196612

commit v4 on v3

--- a/solution.py
+++ b/solution.py
@@ -15,6 +15,7 @@
 TBLOCKS = N_VOC * TB_DEV
 SBLOCKS = N_VOC * SB_DEV
 OWN = 2
+GROUP = 8
 DS = 1536
 PIECE = DS // (NX * NC)
 TCOLS = TB_DEV * BLOCK
@@ -25,7 +26,7 @@
 loss_scale = 256.0
 F32 = jnp.float32
 BF16 = jnp.bfloat16
-VMEM_BYTES = 24 * 1024 * 1024
+VMEM_BYTES = 28 * 1024 * 1024
 WHOLE_VMEM = 60 * 1024 * 1024
 
 
@@ -120,39 +121,45 @@
     out_ref[:, TCOLS:] = pack_lanes(out_ref.shape[0], [peak, stats_ref[:, 0:1], stats_ref[:, 1:2]])
 
 
-def align_kernel(recv_ref, table_ref, source_ref, shift_ref, out_ref, rolled_ref, weight_ref, sem):
-    copy = pltpu.make_async_copy(source_ref, weight_ref, sem)
-    copy.start()
-    lanes = lax.broadcasted_iota(jnp.int32, (TBLOCKS, BLOCK), 1)
-    for t in range(OWN):
-        extra = recv_ref[t, :, TCOLS:]
+def align_kernel(recv_ref, table_ref, weight_ref, index_ref, count_ref, out_ref, wide_ref, smooth_ref, rolled_ref):
+    for y in range(NY):
+        size = recv_ref.shape[1]
+        for j in range(TB_DEV + 1):
+            part = recv_ref[y, :, j * BLOCK : (j + 1) * BLOCK]
+            wide_ref[j, y * size : (y + 1) * size, :] = part.astype(F32)
+    norms, logs = [], []
+    for t in range(GROUP):
+        rows = [wide_ref[j, pl.ds(t, N_VOC, stride=GROUP), :] for j in range(TB_DEV + 1)]
+        extra = rows[TB_DEV]
         peak = unpack_lane(extra, 0)
         scale = jnp.exp(peak - jnp.max(peak, axis=0, keepdims=True))
-        smooth = []
-        for j in range(TB_DEV):
-            probs = recv_ref[t, :, j * BLOCK : (j + 1) * BLOCK]
-            tile = jnp.dot(probs, table_ref[...], preferred_element_type=F32) * scale
-            smooth.append(tile.astype(BF16).astype(F32))
-        smooth = jnp.concatenate(smooth, axis=0)
-        for k in range(FANOUT):
-            index = (lanes - shift_ref[:, k : k + 1]) & (BLOCK - 1)
-            rolled = jnp.take_along_axis(smooth, index, axis=1)
-            rolled_ref[k * TBLOCKS : (k + 1) * TBLOCKS, t * BLOCK : (t + 1) * BLOCK] = rolled.astype(BF16)
-    copy.wait()
-    aligned = jnp.dot(weight_ref[...], rolled_ref[...], preferred_element_type=F32)
-    for t in range(OWN):
-        mine = aligned[:, t * BLOCK : (t + 1) * BLOCK]
-        norm = jnp.sum(jnp.sum(mine, axis=0, keepdims=True), axis=1, keepdims=True)
-        mine = mine / norm
-        for b in range(SB_DEV):
-            out_ref[t, :, b * BLOCK : (b + 1) * BLOCK] = mine[b * N_VOC : (b + 1) * N_VOC, :].astype(BF16)
-        extra = recv_ref[t, :, TCOLS:]
+        blocks = jnp.concatenate(rows[:TB_DEV], axis=0)
+        smooth = jnp.dot(blocks.astype(BF16), table_ref[...], preferred_element_type=F32)
+        smooth = (smooth * jnp.concatenate([scale] * TB_DEV, axis=0)).astype(BF16).astype(F32)
+        smooth_ref[t] = smooth
+        mass = jnp.sum(smooth * count_ref[...], axis=0, keepdims=True)
+        norms.append(jnp.sum(mass, axis=1, keepdims=True))
         top = unpack_lane(extra, 1)
         total = unpack_lane(extra, 2)
         joint_top = jnp.max(top, axis=0, keepdims=True)
         joint_total = jnp.sum(total * jnp.exp(top - joint_top), axis=0, keepdims=True)
-        log_total = joint_top + jnp.log(joint_total)
-        out_ref[t, :, SCOLS:] = pack_lanes(N_VOC, [log_total])
+        logs.append(joint_top + jnp.log(joint_total))
+
+    def roll(k, carry):
+        index = index_ref[k]
+        for t in range(GROUP):
+            rolled = jnp.take_along_axis(smooth_ref[t], index, axis=1)
+            start = pl.multiple_of(k * TBLOCKS, TBLOCKS)
+            rolled_ref[pl.ds(start, TBLOCKS), t * BLOCK : (t + 1) * BLOCK] = rolled.astype(BF16)
+        return carry
+
+    lax.fori_loop(0, FANOUT, roll, 0)
+    aligned = jnp.dot(weight_ref[...], rolled_ref[...], preferred_element_type=F32)
+    for t in range(GROUP):
+        mine = aligned[:, t * BLOCK : (t + 1) * BLOCK] / norms[t]
+        for b in range(SB_DEV):
+            out_ref[t, :, b * BLOCK : (b + 1) * BLOCK] = mine[b * NZ : (b + 1) * NZ, :].astype(BF16)
+        out_ref[t, :, SCOLS:] = pack_lanes(NZ, [logs[t]])
 
 
 def grad_kernel(target_ref, logits_ref, source_ref, out_ref, log_ref, head_ref, sem):
@@ -166,8 +173,8 @@
     copy.wait()
     out_ref[:, :DS] = lax.dot_general(
         grad, head_ref[...], (((1,), (1,)), ((), ())), preferred_element_type=F32
-    )
-    out_ref[:, DS:] = jnp.broadcast_to(cross, (out_ref.shape[0], BLOCK))
+    ).astype(BF16)
+    out_ref[:, DS:] = pack_lanes(out_ref.shape[0], [cross])
     log_ref[...] = jnp.broadcast_to(log_total, log_ref.shape)
 
 
@@ -176,7 +183,8 @@
     for i in range(1, NZ):
         terms = terms + parts_ref[i]
     out_ref[:, :DS] = terms[:, :DS].astype(BF16)
-    out_ref[:, DS:] = pack_lanes(OWN, [terms[:, DS : DS + 1]])
+    cross = (terms[:, DS : DS + 1] + terms[:, DS + 1 : DS + 2]) + terms[:, DS + 2 : DS + 3]
+    out_ref[:, DS:] = pack_lanes(OWN, [cross])
 
 
 def exchange(value, axis):
@@ -200,7 +208,8 @@
 
 
 def by_source(pairs):
-    return pairs.reshape(N_VOC, TB_DEV, FANOUT).transpose(1, 0, 2).reshape(TBLOCKS, FANOUT)
+    pairs = pairs.reshape(NZ, NY, TB_DEV, FANOUT).transpose(2, 1, 0, 3)
+    return pairs.reshape(TBLOCKS, FANOUT)
 
 
 def logit_parts(rows, head, spots):
@@ -245,18 +254,25 @@
     spots = jnp.stack([lax.axis_index("x"), lax.axis_index("c")]).astype(jnp.int32)
 
     rows = spread(teacher_hidden, "z", NZ)
-    head_mine = jnp.concatenate(
-        [student_head, send_x(student_head, -1), send_x(student_head, 2), send_x(student_head, 1)], axis=0
-    )
+    pieces = [student_head, send_x(student_head, -1), send_x(student_head, 2), send_x(student_head, 1)]
+    pieces = lax.optimization_barrier((rows, *pieces))[1:]
+    head_mine = jnp.concatenate(pieces, axis=0)
     head_theirs = send_c(head_mine)
     rows = spread(rows, "y", NY)
 
     shift = by_source(pair_shift)
-    place = by_source(pair_block * N_VOC + pair_owner).T.reshape(1, -1)
-    count = by_source(pair_count).T.reshape(1, -1)
+    count = by_source(pair_count)
+    owner = by_source(pair_owner)
+    place = by_source(pair_block) * NZ + owner // NY
+    place = jnp.where(owner % NY == lax.axis_index("y"), place, -1)
     weight = jnp.where(
-        place == lax.broadcasted_iota(jnp.int32, (SBLOCKS, TBLOCKS * FANOUT), 0), count, 0
+        place.T.reshape(1, -1) == lax.broadcasted_iota(jnp.int32, (NZ * SB_DEV, TBLOCKS * FANOUT), 0),
+        count.T.reshape(1, -1),
+        0,
     ).astype(BF16)
+    lanes = lax.broadcasted_iota(jnp.int32, (FANOUT, TBLOCKS, BLOCK), 2)
+    index = (lanes - shift.T[:, :, None]) & (BLOCK - 1)
+    mass = jnp.broadcast_to(jnp.sum(count, axis=1, keepdims=True).astype(F32), (TBLOCKS, BLOCK))
 
     head_full, student_logits, stats = kernel_call(
         student_kernel,
@@ -269,30 +285,35 @@
         "student",
         "svvv",
     )(spots, student_hidden, head_mine, head_theirs)
-    rows, weight, shift, stats = lax.optimization_barrier((rows, weight, shift, stats))
+    rows, weight, index, mass = lax.optimization_barrier((rows, weight, index, mass))
 
     own, before, after = logit_parts(rows, teacher_head, spots)
     outgoing = kernel_call(
         softmax_kernel, jax.ShapeDtypeStruct((tok_rows, TCOLS + BLOCK), BF16), name="softmax", inputs="vvvv"
     )(own, before, after, stats)
-    received = exchange(outgoing.reshape(N_VOC, OWN, TCOLS + BLOCK), ("z", "y"))
+    received = exchange(outgoing.reshape(NZ, GROUP, TCOLS + BLOCK), "z")
+    received = spread(received.reshape(tok_rows, TCOLS + BLOCK), "y", NY)
     target = kernel_call(
         align_kernel,
-        jax.ShapeDtypeStruct((OWN, N_VOC, SCOLS + BLOCK), BF16),
-        [pltpu.VMEM((FANOUT * TBLOCKS, OWN * BLOCK), BF16)] + arriving((SBLOCKS, FANOUT * TBLOCKS)),
+        jax.ShapeDtypeStruct((GROUP, NZ, SCOLS + BLOCK), BF16),
+        [
+            pltpu.VMEM((TB_DEV + 1, N_VOC * GROUP, BLOCK), F32),
+            pltpu.VMEM((GROUP, TBLOCKS, BLOCK), F32),
+            pltpu.VMEM((FANOUT * TBLOCKS, GROUP * BLOCK), BF16),
+        ],
         "align",
-        "vvhv",
-    )(received.transpose(1, 0, 2), base_kernel(), weight, shift)
-    target = exchange(target.transpose(1, 0, 2), ("z", "y")).reshape(tok_rows, SCOLS + BLOCK)
+        "vvvvv",
+    )(received, base_kernel(), weight, index, mass)
+    target = exchange(target.transpose(1, 0, 2), "z").reshape(tok_rows, SCOLS + BLOCK)
 
     terms, log_total = kernel_call(
         grad_kernel,
-        (jax.ShapeDtypeStruct((tok_rows, WIDE), F32), jax.ShapeDtypeStruct((tok_rows, BLOCK), F32)),
+        (jax.ShapeDtypeStruct((tok_rows, WIDE), BF16), jax.ShapeDtypeStruct((tok_rows, BLOCK), F32)),
         arriving((DS, SCOLS)),
         "gradient",
         "vvh",
     )(target, student_logits, head_full)
-    terms = exchange(terms.reshape(NY, tok_rows // NY, WIDE), "y").sum(axis=0)
+    terms = exchange(terms.reshape(NY, tok_rows // NY, WIDE), "y").astype(F32).sum(axis=0)
     terms = exchange(terms.reshape(NZ, OWN, WIDE), "z")
     result = kernel_call(
         finish_kernel, jax.ShapeDtypeStruct((OWN, WIDE), BF16), name="finish", inputs="v"

time: 272 us -> 285 us (1.048)
  blocking collectives: 88.8 us -> 123 us
  waiting for transfers between devices: 71.3 us -> 60.7 us
  starting transfers between devices: 62.7 us -> 54.8 us
  other arithmetic: 6 us -> 2.39 us
    all_to_all x5 -> x6, blocking collectives: 88.8 us -> 123 us  [exchange(): return lax.all_to_all(value, axis, split_axis=0, concat_axis=0, tiled=True)]
    ppermute x7, waiting for transfers between devices: 34.8 us -> 16.1 us  [send(): lax.ppermute(value, axis, [(i, (i + step) % size) for i in range(size)])]
    all_to_all x3, starting transfers between devices: 33.2 us -> 24.2 us  [exchange(): return lax.all_to_all(value, axis, split_axis=0, concat_axis=0, tiled=True)]
    all_to_all x3, waiting for transfers between devices: 36.1 us -> 44.5 us  [exchange(): return lax.all_to_all(value, axis, split_axis=0, concat_axis=0, tiled=True)]
    convert_element_type x1 -> x2, other arithmetic: 4.01 us -> 0.27 us  [the longest x1 0.26 us: body(): weight = jnp.where(place.T.reshape(1, -1) == lax.broadcasted_iota(jnp.int...]
    unnamed x23 -> x25, local copies, waits for them, and re-layouts: 8 us -> 8.44 us
  transfers between devices with their start and end apart: 13 -> 13, of which waited for: 9 -> 7; matrix products, arithmetic and copies ran while one was open for 5% -> 5% of each run, Pallas kernels for 1% -> 1%
where the time goes in v4:
time: 285 us; the launch traced here: 283 us
  blocking collectives  123 us (43%)
  waiting for transfers between devices  60.7 us (21%)
  starting transfers between devices  54.8 us (19%)
  Pallas kernels  21 us (7%)
  local copies, waits for them, and re-layouts  19.3 us (7%)
    all_to_all x6, blocking collectives, exchange(): return lax.all_to_all(value, axis, split_axis=0, concat_axis=0, tiled=True)  123 us
    all_to_all x3, waiting for transfers between devices, exchange(): return lax.all_to_all(value, axis, split_axis=0, concat_axis=0, tiled=True)  44.5 us
    ppermute x7, starting transfers between devices, send(): lax.ppermute(value, axis, [(i, (i + step) % size) for i in range(size)])  24.3 us
    all_to_all x3, starting transfers between devices, exchange(): return lax.all_to_all(value, axis, split_axis=0, concat_axis=0, tiled=True)  24.2 us
    ppermute x7, waiting for transfers between devices, send(): lax.ppermute(value, axis, [(i, (i + step) % size) for i in range(size)])  16.1 us
    pallas_call x1, Pallas kernels, body(): kernel_call(align_kernel, jax.ShapeDtypeStruct((GROUP, NZ, SCOLS + BLOCK)...  10.3 us
    unnamed x25, local copies, waits for them, and re-layouts  8.44 us
    ppermute x3, starting transfers between devices, send_c(): return lax.ppermute(value, 'c', [(0, 1), (1, 0)])  6.25 us
  transfers between devices with their start and end apart: 13, of which 7 were waited for; matrix products, arithmetic and copies ran while one was open for 5% of the time, Pallas kernels for 1%

profile of v4, /device:TPU:6, one launch (start us, length us, event | category | flops | bytes accessed | tf_op | source)
XLA Modules:
  0.0 283.1 jit_solution(4930355651659506745)
XLA Ops:
  0.6 1.6 broadcast_in_dim.32
  2.3 15.3 %all-to-all-start = ((bf16[16,16,1024]{2,1,0:T(8,128)(2,1)}), bf16[16,16,1024]{2,1,0:T(8,128)(2,1)S(1)}, u32[]{:S(2)}, u32[]{:S(2)}) async-start(bf16[16,16,1024]{2,1,0:T(8,128)(2,1)} %broadcast_in_dim.32), calls=%async_computation | async-start | bytes 1048576 | tf_op jit(solution)/shard_map/all_to_all | solution.py:191
  17.6 2.7 collective-permute-start.6
  20.4 3.0 %collective-permute-start.7 = (bf16[192,1280]{1,0:T(8,128)(2,1)}, bf16[192,1280]{1,0:T(8,128)(2,1)}, u32[]{:S(2)}, u32[]{:S(2)}) collective-permute-start(bf16[192,1280]{1,0:T(8,128)(2,1)} %param.11), channel_id=1, source_target_pairs={{0,256},{128,384},{256,0},{384,128},{1,257},{129,385},{257,1},{385... | collective-permute-start | bytes 1474568 | tf_op jit(solution)/shard_map/ppermute | solution.py:199
  23.4 4.0 %collective-permute-start.8 = (bf16[192,1280]{1,0:T(8,128)(2,1)}, bf16[192,1280]{1,0:T(8,128)(2,1)}, u32[]{:S(2)}, u32[]{:S(2)}) collective-permute-start(bf16[192,1280]{1,0:T(8,128)(2,1)} %param.11), channel_id=1, source_target_pairs={{0,128},{128,256},{256,384},{384,0},{1,129},{129,257},{257,385},{3... | collective-permute-start | bytes 1474568 | tf_op jit(solution)/shard_map/ppermute | solution.py:199
  30.8 15.9 %all-to-all-done = bf16[16,16,1024]{2,1,0:T(8,128)(2,1)S(1)} async-done(((bf16[16,16,1024]{2,1,0:T(8,128)(2,1)}), bf16[16,16,1024]{2,1,0:T(8,128)(2,1)S(1)}, u32[]{:S(2)}, u32[]{:S(2)}) %all-to-all-start) | async-done | bytes 524320 | tf_op jit(solution)/shard_map/all_to_all | solution.py:191
  48.3 4.5 %all-to-all-start.1 = ((bf16[4,16,16,1024]{3,2,1,0:T(8,128)(2,1)}), bf16[4,16,16,1024]{3,2,1,0:T(8,128)(2,1)}, u32[]{:S(2)}, u32[]{:S(2)}) async-start(bf16[4,16,16,1024]{3,2,1,0:T(8,128)(2,1)} %broadcast_in_dim.56), calls=%async_computation.1 | async-start | bytes 4194304 | tf_op jit(solution)/shard_map/all_to_all | solution.py:191
  54.0 1.9 constant_dynamic-update-slice_fusion.3
  55.8 17.2 %all-to-all-done.1 = bf16[4,16,16,1024]{3,2,1,0:T(8,128)(2,1)} async-done(((bf16[4,16,16,1024]{3,2,1,0:T(8,128)(2,1)}), bf16[4,16,16,1024]{3,2,1,0:T(8,128)(2,1)}, u32[]{:S(2)}, u32[]{:S(2)}) %all-to-all-start.1) | async-done | bytes 2097184 | tf_op jit(solution)/shard_map/all_to_all | solution.py:191
  75.5 3.1 %rows.1 = (f32[128,1024]{1,0:T(8,128)S(1)}, f32[384,1024]{1,0:T(8,128)S(1)}, bf16[512,1024]{1,0:T(8,128)(2,1)S(1)}) custom-call(s32[2]{0:T(128)S(1)} %pad_add_fusion.spots_ref, bf16[1024,1024]{1,0:T(8,128)(2,1)} %bitcast.9.gathered_ref, bf16[1024,1024]{1,0:T(8,128)(2,1)S(1)} %copy-done.2), custom_call_target="tpu_custom_call" | custom-call | tf_op jit(solution)/shard_map/rows/pallas_call | solution.py:219
  78.6 1.9 collective-permute-start
  82.7 2.4 collective-permute-start.1
  86.2 1.9 collective-permute-start.9
  89.5 2.7 collective-permute-start.4
  92.2 4.3 %collective-permute-start.2 = (f32[64,1024]{1,0:T(8,128)S(1)}, f32[64,1024]{1,0:T(8,128)S(1)}, u32[]{:S(2)}, u32[]{:S(2)}) collective-permute-start(f32[64,1024]{1,0:T(8,128)S(1)} %get-tuple-element.39), channel_id=1, source_target_pairs={{0,128},{128,256},{256,384},{384,0},{1,129},{129,257},{257,385},{3... | collective-permute-start | bytes 786440 | tf_op jit(solution)/shard_map/ppermute | solution.py:199
  96.9 4.5 %collective-permute-done.4 = f32[64,1024]{1,0:T(8,128)S(1)} collective-permute-done((f32[64,1024]{1,0:T(8,128)S(1)}, f32[64,1024]{1,0:T(8,128)S(1)}, u32[]{:S(2)}, u32[]{:S(2)}) %collective-permute-start.4) | collective-permute-done | bytes 262176 | tf_op jit(solution)/shard_map/ppermute | solution.py:199
  102.7 5.5 %collective-permute-start.3 = (f32[128,1024]{1,0:T(8,128)S(1)}, f32[128,1024]{1,0:T(8,128)S(1)}, u32[]{:S(2)}, u32[]{:S(2)}) collective-permute-start(f32[128,1024]{1,0:T(8,128)S(1)} %pad_maximum_fusion), channel_id=1, source_target_pairs={{0,128},{128,256},{256,384},{384,0},{1,129},{129,257},{257,385},{3... | collective-permute-start | bytes 1572872 | tf_op jit(solution)/shard_map/ppermute | solution.py:199
  108.3 1.9 collective-permute-start.5
  110.3 1.7 student.1
  112.0 1.9 copy-done
  113.9 5.1 %collective-permute-done.3.prev_ref = f32[128,1024]{1,0:T(8,128)S(1)} collective-permute-done((f32[128,1024]{1,0:T(8,128)S(1)}, f32[128,1024]{1,0:T(8,128)S(1)}, u32[]{:S(2)}, u32[]{:S(2)}) %collective-permute-start.3) | collective-permute-done | bytes 524320 | tf_op jit(solution)/shard_map/ppermute | solution.py:199
  119.0 5.4 %collective-permute-done.5.next_ref = f32[128,1024]{1,0:T(8,128)S(1)} collective-permute-done((f32[128,1024]{1,0:T(8,128)S(1)}, f32[128,1024]{1,0:T(8,128)S(1)}, u32[]{:S(2)}, u32[]{:S(2)}) %collective-permute-start.5) | collective-permute-done | bytes 524320 | tf_op jit(solution)/shard_map/ppermute | solution.py:199
  124.6 30.7 %all_to_all.45 = bf16[16,8,1152]{2,1,0:T(8,128)(2,1)S(1)} all-to-all(bf16[16,8,1152]{2,1,0:T(8,128)(2,1)S(1)} %bitcast.41), channel_id=1, replica_groups=mesh['x'=4,'c'=2,'z'=16,'y'=4] {'z'}, dimensions={0} | all-to-all | bytes 589824 | tf_op jit(solution)/shard_map/all_to_all | solution.py:191
  156.4 4.4 %all-to-all-start.3 = ((bf16[4,128,1152]{2,1,0:T(8,128)(2,1)}), bf16[4,128,1152]{2,1,0:T(8,128)(2,1)}, u32[]{:S(2)}, u32[]{:S(2)}) async-start(bf16[4,128,1152]{2,1,0:T(8,128)(2,1)} %broadcast_in_dim.62), calls=%async_computation.3 | async-start | bytes 2359296 | tf_op jit(solution)/shard_map/all_to_all | solution.py:191
  160.9 11.4 %all-to-all-done.3.recv_ref = bf16[4,128,1152]{2,1,0:T(8,128)(2,1)} async-done(((bf16[4,128,1152]{2,1,0:T(8,128)(2,1)}), bf16[4,128,1152]{2,1,0:T(8,128)(2,1)}, u32[]{:S(2)}, u32[]{:S(2)}) %all-to-all-start.3) | async-done | bytes 1179680 | tf_op jit(solution)/shard_map/all_to_all | solution.py:191
  173.3 10.3 %align.1 = bf16[8,16,1408]{2,1,0:T(8,128)(2,1)S(1)} custom-call(bf16[4,128,1152]{2,1,0:T(8,128)(2,1)} %all-to-all-done.3.recv_ref, bf16[128,128]{1,0:T(8,128)(2,1)S(1)} %fusion.3.table_ref, bf16[160,4096]{1,0:T(8,128)(2,1)S(1)} %select_convert_fusion.weight_ref, s32[8,512,128]{2,1,0:T(8,128)S(1)} %subtract_and_fusion.index_ref, f32[512,128]{1,0:T(8,128)S(1)} %copy-done.3), custom_call_target="tpu_custom_call" | custom-call | tf_op jit(solution)/shard_map/align/pallas_call | solution.py:296
  183.7 31.2 %all_to_all.46 = bf16[16,8,1408]{2,1,0:T(8,128)(2,1)} all-to-all(bf16[16,8,1408]{2,1,0:T(8,128)(2,1)S(1)} %copy.38), channel_id=1, replica_groups=mesh['x'=4,'c'=2,'z'=16,'y'=4] {'z'}, dimensions={0} | all-to-all | bytes 720896 | tf_op jit(solution)/shard_map/all_to_all | solution.py:191
  214.8 5.5 %gradient.1 = (bf16[128,1664]{1,0:T(8,128)(2,1)}, f32[128,128]{1,0:T(8,128)}) custom-call(bf16[128,1408]{1,0:T(8,128)(2,1)} %bitcast.45, f32[128,1280]{1,0:T(8,128)} %copy-done.4, bf16[1536,1280]{1,0:T(8,128)(2,1)} %copy-done), custom_call_target="tpu_custom_call" | custom-call | tf_op jit(solution)/shard_map/gradient/pallas_call | solution.py:309
  220.3 11.0 %all_to_all.47 = bf16[4,32,1664]{2,1,0:T(8,128)(2,1)S(1)} all-to-all(bf16[4,32,1664]{2,1,0:T(8,128)(2,1)} %bitcast.50), channel_id=1, replica_groups=mesh['x'=4,'c'=2,'z'=16,'y'=4] {'y'}, dimensions={0} | all-to-all | bytes 851968 | tf_op jit(solution)/shard_map/all_to_all | solution.py:191
  231.5 22.4 %all_to_all.48.parts_ref = f32[16,2,1664]{2,1,0:T(2,128)S(1)} all-to-all(f32[16,2,1664]{2,1,0:T(2,128)S(1)} %reshape.76), channel_id=1, replica_groups=mesh['x'=4,'c'=2,'z'=16,'y'=4] {'z'}, dimensions={0} | all-to-all | bytes 425984 | tf_op jit(solution)/shard_map/all_to_all | solution.py:191
  254.1 17.5 %all_to_all.49 = bf16[16,2,1664]{2,1,0:T(2,128)(2,1)S(1)} all-to-all(bf16[16,2,1664]{2,1,0:T(2,128)(2,1)S(1)} %broadcast_in_dim.63), channel_id=1, replica_groups=mesh['x'=4,'c'=2,'z'=16,'y'=4] {'z'}, dimensions={0} | all-to-all | bytes 212992 | tf_op jit(solution)/shard_map/all_to_all | solution.py:191
  271.7 9.9 %all_to_all.50 = bf16[4,32,1664]{2,1,0:T(8,128)(2,1)S(1)} all-to-all(bf16[4,32,1664]{2,1,0:T(8,128)(2,1)S(1)} %broadcast_in_dim.65), channel_id=1, replica_groups=mesh['x'=4,'c'=2,'z'=16,'y'=4] {'y'}, dimensions={0} | all-to-all | bytes 851968 | tf_op jit(solution)/shard_map/all_to_all | solution.py:191
  (76 shorter events, 19.2 us)
Async XLA Ops:
  0.6 28.2 %copy-start.9 = (s32[512,8]{0,1:T(8,128)S(1)}, s32[512,8]{0,1:T(8,128)}, u32[]{:S(2)}) copy-start(s32[512,8]{0,1:T(8,128)} %param.13) | copy-start | bytes 49156
  0.6 28.8 %copy-start.7 = (s32[512,8]{0,1:T(8,128)S(1)}, s32[512,8]{0,1:T(8,128)}, u32[]{:S(2)}) copy-start(s32[512,8]{0,1:T(8,128)} %param.12) | copy-start | bytes 49156
  2.3 27.9 %copy-start.8 = (s32[512,8]{0,1:T(8,128)S(1)}, s32[512,8]{0,1:T(8,128)}, u32[]{:S(2)}) copy-start(s32[512,8]{0,1:T(8,128)} %param.14) | copy-start | bytes 49156
  2.3 44.4 %all-to-all-start = ((bf16[16,16,1024]{2,1,0:T(8,128)(2,1)}), bf16[16,16,1024]{2,1,0:T(8,128)(2,1)S(1)}, u32[]{:S(2)}, u32[]{:S(2)}) async-start(bf16[16,16,1024]{2,1,0:T(8,128)(2,1)} %broadcast_in_dim.32), calls=%async_computation | async-start | bytes 1048576 | tf_op jit(solution)/shard_map/all_to_all | solution.py:191
  17.6 36.3 %collective-permute-start.6 = (bf16[192,1280]{1,0:T(8,128)(2,1)}, bf16[192,1280]{1,0:T(8,128)(2,1)}, u32[]{:S(2)}, u32[]{:S(2)}) collective-permute-start(bf16[192,1280]{1,0:T(8,128)(2,1)} %param.11), channel_id=1, source_target_pairs={{0,384},{128,0},{256,128},{384,256},{1,385},{129,1},{257,129},{385... | collective-permute-start | bytes 1474568 | tf_op jit(solution)/shard_map/ppermute | solution.py:199
  20.4 33.6 %collective-permute-start.7 = (bf16[192,1280]{1,0:T(8,128)(2,1)}, bf16[192,1280]{1,0:T(8,128)(2,1)}, u32[]{:S(2)}, u32[]{:S(2)}) collective-permute-start(bf16[192,1280]{1,0:T(8,128)(2,1)} %param.11), channel_id=1, source_target_pairs={{0,256},{128,384},{256,0},{384,128},{1,257},{129,385},{257,1},{385... | collective-permute-start | bytes 1474568 | tf_op jit(solution)/shard_map/ppermute | solution.py:199
  23.4 30.5 %collective-permute-start.8 = (bf16[192,1280]{1,0:T(8,128)(2,1)}, bf16[192,1280]{1,0:T(8,128)(2,1)}, u32[]{:S(2)}, u32[]{:S(2)}) collective-permute-start(bf16[192,1280]{1,0:T(8,128)(2,1)} %param.11), channel_id=1, source_target_pairs={{0,128},{128,256},{256,384},{384,0},{1,129},{129,257},{257,385},{3... | collective-permute-start | bytes 1474568 | tf_op jit(solution)/shard_map/ppermute | solution.py:199
  48.3 24.8 %all-to-all-start.1 = ((bf16[4,16,16,1024]{3,2,1,0:T(8,128)(2,1)}), bf16[4,16,16,1024]{3,2,1,0:T(8,128)(2,1)}, u32[]{:S(2)}, u32[]{:S(2)}) async-start(bf16[4,16,16,1024]{3,2,1,0:T(8,128)(2,1)} %broadcast_in_dim.56), calls=%async_computation.1 | async-start | bytes 4194304 | tf_op jit(solution)/shard_map/all_to_all | solution.py:191
  73.9 1.6 copy-start.2
  75.5 5.1 %copy-start.1 = (bf16[768,1280]{1,0:T(8,128)(2,1)S(1)}, bf16[768,1280]{1,0:T(8,128)(2,1)}, u32[]{:S(2)}) copy-start(bf16[768,1280]{1,0:T(8,128)(2,1)} %constant_dynamic-update-slice_fusion.3) | copy-start | bytes 5898244
  78.6 17.9 %collective-permute-start = (f32[384,1024]{1,0:T(8,128)S(1)}, f32[384,1024]{1,0:T(8,128)S(1)}, u32[]{:S(2)}, u32[]{:S(2)}) collective-permute-start(f32[384,1024]{1,0:T(8,128)S(1)} %get-tuple-element.20), channel_id=1, source_target_pairs={{0,64},{64,0},{1,65},{65,1},{2,66},{66,2},{3,67},{67,3},{4,68},{68... | collective-permute-start | bytes 4718600 | tf_op jit(solution)/shard_map/ppermute | solution.py:207
  82.7 6.7 %collective-permute-start.1 = (f32[128,1024]{1,0:T(8,128)S(1)}, f32[128,1024]{1,0:T(8,128)S(1)}, u32[]{:S(2)}, u32[]{:S(2)}) collective-permute-start(f32[128,1024]{1,0:T(8,128)S(1)} %get-tuple-element.21), channel_id=1, source_target_pairs={{0,64},{64,0},{1,65},{65,1},{2,66},{66,2},{3,67},{67,3},{4,68},{68... | collective-permute-start | bytes 1572872 | tf_op jit(solution)/shard_map/ppermute | solution.py:207
  86.2 24.1 %collective-permute-start.9 = (bf16[768,1280]{1,0:T(8,128)(2,1)S(1)}, bf16[768,1280]{1,0:T(8,128)(2,1)S(1)}, u32[]{:S(2)}, u32[]{:S(2)}) collective-permute-start(bf16[768,1280]{1,0:T(8,128)(2,1)S(1)} %constant_dynamic-update-slice_fusion.mine_ref), channel_id=1, source_target_pairs={{0,64},{64,0},{1,65},{65,1},{2,66},{66,2},{3,67},{67,3},{4,68},{68... | collective-permute-start | bytes 5898248 | tf_op jit(solution)/shard_map/ppermute | solution.py:207
  89.5 11.8 %collective-permute-start.4 = (f32[64,1024]{1,0:T(8,128)S(1)}, f32[64,1024]{1,0:T(8,128)S(1)}, u32[]{:S(2)}, u32[]{:S(2)}) collective-permute-start(f32[64,1024]{1,0:T(8,128)S(1)} %get-tuple-element.38), channel_id=1, source_target_pairs={{0,384},{128,0},{256,128},{384,256},{1,385},{129,1},{257,129},{385... | collective-permute-start | bytes 786440 | tf_op jit(solution)/shard_map/ppermute | solution.py:199
  92.2 10.3 %collective-permute-start.2 = (f32[64,1024]{1,0:T(8,128)S(1)}, f32[64,1024]{1,0:T(8,128)S(1)}, u32[]{:S(2)}, u32[]{:S(2)}) collective-permute-start(f32[64,1024]{1,0:T(8,128)S(1)} %get-tuple-element.39), channel_id=1, source_target_pairs={{0,128},{128,256},{256,384},{384,0},{1,129},{129,257},{257,385},{3... | collective-permute-start | bytes 786440 | tf_op jit(solution)/shard_map/ppermute | solution.py:199
  96.8 13.4 %copy-start.5 = (bf16[128,1536]{1,0:T(8,128)(2,1)S(1)}, bf16[128,1536]{1,0:T(8,128)(2,1)}, u32[]{:S(2)}) copy-start(bf16[128,1536]{1,0:T(8,128)(2,1)} %hidden_ref.1) | copy-start | bytes 1179652
  102.7 16.2 %collective-permute-start.3 = (f32[128,1024]{1,0:T(8,128)S(1)}, f32[128,1024]{1,0:T(8,128)S(1)}, u32[]{:S(2)}, u32[]{:S(2)}) collective-permute-start(f32[128,1024]{1,0:T(8,128)S(1)} %pad_maximum_fusion), channel_id=1, source_target_pairs={{0,128},{128,256},{256,384},{384,0},{1,129},{129,257},{257,385},{3... | collective-permute-start | bytes 1572872 | tf_op jit(solution)/shard_map/ppermute | solution.py:199
  108.3 16.0 %collective-permute-start.5 = (f32[128,1024]{1,0:T(8,128)S(1)}, f32[128,1024]{1,0:T(8,128)S(1)}, u32[]{:S(2)}, u32[]{:S(2)}) collective-permute-start(f32[128,1024]{1,0:T(8,128)S(1)} %pad_maximum_fusion.1), channel_id=1, source_target_pairs={{0,384},{128,0},{256,128},{384,256},{1,385},{129,1},{257,129},{385... | collective-permute-start | bytes 1572872 | tf_op jit(solution)/shard_map/ppermute | solution.py:199
  112.0 1.9 copy-start
  113.8 41.4 %copy-start.4 = (f32[128,1280]{1,0:T(8,128)}, f32[128,1280]{1,0:T(8,128)S(1)}, u32[]{:S(2)}) copy-start(f32[128,1280]{1,0:T(8,128)S(1)} %get-tuple-element.30.logits_ref) | copy-start | bytes 1966084
  156.4 15.9 %all-to-all-start.3 = ((bf16[4,128,1152]{2,1,0:T(8,128)(2,1)}), bf16[4,128,1152]{2,1,0:T(8,128)(2,1)}, u32[]{:S(2)}, u32[]{:S(2)}) async-start(bf16[4,128,1152]{2,1,0:T(8,128)(2,1)} %broadcast_in_dim.62), calls=%async_computation.3 | async-start | bytes 2359296 | tf_op jit(solution)/shard_map/all_to_all | solution.py:191
  172.3 1.0 copy-start.3
  231.4 51.0 %copy-start.6 = (f32[128,128]{1,0:T(8,128)S(1)}, f32[128,128]{1,0:T(8,128)}, u32[]{:S(2)}) copy-start(f32[128,128]{1,0:T(8,128)} %get-tuple-element.32) | copy-start | bytes 196612

commit v5 on v3

--- a/solution.py
+++ b/solution.py
@@ -26,7 +26,7 @@
 F32 = jnp.float32
 BF16 = jnp.bfloat16
 VMEM_BYTES = 24 * 1024 * 1024
-WHOLE_VMEM = 60 * 1024 * 1024
+WHOLE_VMEM = 117 * 512 * 1024
 
 
 def kernel_call(kernel, out_shape, scratch=(), name=None, inputs=""):
@@ -41,8 +41,8 @@
     )
 
 
-def arriving(array, dtype=BF16):
-    return [pltpu.VMEM(array, dtype), pltpu.SemaphoreType.DMA]
+def arriving(shape):
+    return [pltpu.VMEM(shape, BF16), pltpu.SemaphoreType.DMA]
 
 
 def base_kernel():
@@ -118,6 +118,14 @@
     peak = jnp.max(logits, axis=1, keepdims=True)
     out_ref[:, :TCOLS] = jnp.exp(logits - peak).astype(BF16)
     out_ref[:, TCOLS:] = pack_lanes(out_ref.shape[0], [peak, stats_ref[:, 0:1], stats_ref[:, 1:2]])
+
+
+def weight_kernel(place_ref, count_ref, out_ref):
+    place = place_ref[...]
+    count = count_ref[...].astype(F32)
+    for b in range(SB_DEV):
+        rows = lax.broadcasted_iota(jnp.int32, (N_VOC, FANOUT * TBLOCKS), 0) + b * N_VOC
+        out_ref[b * N_VOC : (b + 1) * N_VOC, :] = jnp.where(rows == place, count, 0.0).astype(BF16)
 
 
 def align_kernel(recv_ref, table_ref, source_ref, shift_ref, out_ref, rolled_ref, weight_ref, sem):
@@ -155,8 +163,8 @@
         out_ref[t, :, SCOLS:] = pack_lanes(N_VOC, [log_total])
 
 
-def grad_kernel(target_ref, logits_ref, source_ref, out_ref, log_ref, head_ref, sem):
-    copy = pltpu.make_async_copy(source_ref, head_ref, sem)
+def grad_kernel(target_ref, logits_ref, source_ref, out_ref, log_ref, turned_ref, sem):
+    copy = pltpu.make_async_copy(source_ref, turned_ref, sem)
     copy.start()
     log_total = unpack_lane(target_ref[:, SCOLS:], 0)
     target = target_ref[:, :SCOLS].astype(F32)
@@ -164,9 +172,7 @@
     cross = jnp.sum(target * logits, axis=1, keepdims=True)
     grad = (loss_scale * (jnp.exp(logits - log_total) - target)).astype(BF16)
     copy.wait()
-    out_ref[:, :DS] = lax.dot_general(
-        grad, head_ref[...], (((1,), (1,)), ((), ())), preferred_element_type=F32
-    )
+    out_ref[:, :DS] = jnp.dot(grad, turned_ref[...], preferred_element_type=F32)
     out_ref[:, DS:] = jnp.broadcast_to(cross, (out_ref.shape[0], BLOCK))
     log_ref[...] = jnp.broadcast_to(log_total, log_ref.shape)
 
@@ -245,19 +251,15 @@
     spots = jnp.stack([lax.axis_index("x"), lax.axis_index("c")]).astype(jnp.int32)
 
     rows = spread(teacher_hidden, "z", NZ)
-    head_mine = jnp.concatenate(
-        [student_head, send_x(student_head, -1), send_x(student_head, 2), send_x(student_head, 1)], axis=0
-    )
+    pieces = [student_head, send_x(student_head, -1), send_x(student_head, 2), send_x(student_head, 1)]
+    pieces = lax.optimization_barrier((rows, *pieces))[1:]
+    head_mine = jnp.concatenate(pieces, axis=0)
     head_theirs = send_c(head_mine)
     rows = spread(rows, "y", NY)
 
     shift = by_source(pair_shift)
     place = by_source(pair_block * N_VOC + pair_owner).T.reshape(1, -1)
     count = by_source(pair_count).T.reshape(1, -1)
-    weight = jnp.where(
-        place == lax.broadcasted_iota(jnp.int32, (SBLOCKS, TBLOCKS * FANOUT), 0), count, 0
-    ).astype(BF16)
-
     head_full, student_logits, stats = kernel_call(
         student_kernel,
         (
@@ -269,29 +271,36 @@
         "student",
         "svvv",
     )(spots, student_hidden, head_mine, head_theirs)
-    rows, weight, shift, stats = lax.optimization_barrier((rows, weight, shift, stats))
+    rows, place, count, shift, stats = lax.optimization_barrier((rows, place, count, shift, stats))
 
     own, before, after = logit_parts(rows, teacher_head, spots)
     outgoing = kernel_call(
         softmax_kernel, jax.ShapeDtypeStruct((tok_rows, TCOLS + BLOCK), BF16), name="softmax", inputs="vvvv"
     )(own, before, after, stats)
+    weight = kernel_call(
+        weight_kernel,
+        jax.ShapeDtypeStruct((SBLOCKS, FANOUT * TBLOCKS), BF16),
+        name="weight",
+        inputs="vv",
+    )(place, count)
     received = exchange(outgoing.reshape(N_VOC, OWN, TCOLS + BLOCK), ("z", "y"))
     target = kernel_call(
         align_kernel,
         jax.ShapeDtypeStruct((OWN, N_VOC, SCOLS + BLOCK), BF16),
-        [pltpu.VMEM((FANOUT * TBLOCKS, OWN * BLOCK), BF16)] + arriving((SBLOCKS, FANOUT * TBLOCKS)),
+        [pltpu.VMEM((FANOUT * TBLOCKS, OWN * BLOCK), BF16)] + arriving(weight.shape),
         "align",
         "vvhv",
     )(received.transpose(1, 0, 2), base_kernel(), weight, shift)
     target = exchange(target.transpose(1, 0, 2), ("z", "y")).reshape(tok_rows, SCOLS + BLOCK)
 
+    turned = head_full.T
     terms, log_total = kernel_call(
         grad_kernel,
         (jax.ShapeDtypeStruct((tok_rows, WIDE), F32), jax.ShapeDtypeStruct((tok_rows, BLOCK), F32)),
-        arriving((DS, SCOLS)),
+        arriving(turned.shape),
         "gradient",
         "vvh",
-    )(target, student_logits, head_full)
+    )(target, student_logits, turned)
     terms = exchange(terms.reshape(NY, tok_rows // NY, WIDE), "y").sum(axis=0)
     terms = exchange(terms.reshape(NZ, OWN, WIDE), "z")
     result = kernel_call(

time: 272 us -> 273 us (level)
  blocking collectives: 88.8 us -> 59.5 us
  waiting for transfers between devices: 71.3 us -> 93.5 us
  local copies, waits for them, and re-layouts: 18.8 us -> 28.1 us
  starting transfers between devices: 62.7 us -> 66.9 us
  other arithmetic: 6 us -> 2.11 us
    all_to_all x5 -> x4, blocking collectives: 88.8 us -> 59.5 us  [exchange(): return lax.all_to_all(value, axis, split_axis=0, concat_axis=0, tiled=True)]
    all_to_all x3 -> x4, waiting for transfers between devices: 36.1 us -> 57.6 us  [exchange(): return lax.all_to_all(value, axis, split_axis=0, concat_axis=0, tiled=True)]
    pallas_call x0 -> x1, local copies, waits for them, and re-layouts: none -> 6.3 us  [body(): kernel_call(student_kernel, (jax.ShapeDtypeStruct((DS, SCOLS), BF16), jax...]
    convert_element_type x1 -> x0, other arithmetic: 4.01 us -> none  [body(): weight = jnp.where(place == lax.broadcasted_iota(jnp.int32, (SBLOCKS, TBL...]
    all_to_all x3 -> x4, starting transfers between devices: 33.2 us -> 35.8 us  [exchange(): return lax.all_to_all(value, axis, split_axis=0, concat_axis=0, tiled=True)]
    unnamed x23 -> x25, local copies, waits for them, and re-layouts: 8 us -> 10.3 us
  transfers between devices with their start and end apart: 13 -> 14, of which waited for: 9 -> 11; matrix products, arithmetic and copies ran while one was open for 5% -> 5% of each run, Pallas kernels for 1% -> 2%
where the time goes in v5:
time: 273 us; the launch traced here: 272 us
  waiting for transfers between devices  93.5 us (34%)
  starting transfers between devices  66.9 us (25%)
  blocking collectives  59.5 us (22%)
  local copies, waits for them, and re-layouts  28.1 us (10%)
  Pallas kernels  19.2 us (7%)
    all_to_all x4, blocking collectives, exchange(): return lax.all_to_all(value, axis, split_axis=0, concat_axis=0, tiled=True)  59.5 us
    all_to_all x4, waiting for transfers between devices, exchange(): return lax.all_to_all(value, axis, split_axis=0, concat_axis=0, tiled=True)  57.6 us
    all_to_all x4, starting transfers between devices, exchange(): return lax.all_to_all(value, axis, split_axis=0, concat_axis=0, tiled=True)  35.8 us
    ppermute x7, waiting for transfers between devices, send(): lax.ppermute(value, axis, [(i, (i + step) % size) for i in range(size)])  35.5 us
    ppermute x7, starting transfers between devices, send(): lax.ppermute(value, axis, [(i, (i + step) % size) for i in range(size)])  24.9 us
    unnamed x25, local copies, waits for them, and re-layouts  10.3 us
    pallas_call x1, Pallas kernels, body(): kernel_call(align_kernel, jax.ShapeDtypeStruct((OWN, N_VOC, SCOLS + BLOCK...  7.78 us
    pallas_call x1, local copies, waits for them, and re-layouts, body(): kernel_call(student_kernel, (jax.ShapeDtypeStruct((DS, SCOLS), BF16), jax...  6.3 us
  transfers between devices with their start and end apart: 14, of which 11 were waited for; matrix products, arithmetic and copies ran while one was open for 5% of the time, Pallas kernels for 2%

profile of v5, /device:TPU:6, one launch (start us, length us, event | category | flops | bytes accessed | tf_op | source)
XLA Modules:
  0.0 271.5 jit_solution(10760243377128457871)
XLA Ops:
  2.3 15.2 %all-to-all-start = ((bf16[16,16,1024]{2,1,0:T(8,128)(2,1)}), bf16[16,16,1024]{2,1,0:T(8,128)(2,1)S(1)}, u32[]{:S(2)}, u32[]{:S(2)}) async-start(bf16[16,16,1024]{2,1,0:T(8,128)(2,1)} %broadcast_in_dim.10), calls=%async_computation | async-start | bytes 1048576 | tf_op jit(solution)/shard_map/all_to_all | solution.py:189
  17.5 3.3 %collective-permute-start.1 = (bf16[192,1280]{1,0:T(8,128)(2,1)}, bf16[192,1280]{1,0:T(8,128)(2,1)S(1)}, u32[]{:S(2)}, u32[]{:S(2)}) collective-permute-start(bf16[192,1280]{1,0:T(8,128)(2,1)} %param.11), channel_id=1, source_target_pairs={{0,256},{128,384},{256,0},{384,128},{1,257},{129,385},{257,1},{385... | collective-permute-start | bytes 1474568 | tf_op jit(solution)/shard_map/ppermute | solution.py:197
  20.8 1.9 collective-permute-start
  22.7 5.1 %collective-permute-start.2 = (bf16[192,1280]{1,0:T(8,128)(2,1)}, bf16[192,1280]{1,0:T(8,128)(2,1)S(1)}, u32[]{:S(2)}, u32[]{:S(2)}) collective-permute-start(bf16[192,1280]{1,0:T(8,128)(2,1)} %param.11), channel_id=1, source_target_pairs={{0,128},{128,256},{256,384},{384,0},{1,129},{129,257},{257,385},{3... | collective-permute-start | bytes 1474568 | tf_op jit(solution)/shard_map/ppermute | solution.py:197
  27.9 7.3 %collective-permute-done.1 = bf16[192,1280]{1,0:T(8,128)(2,1)S(1)} collective-permute-done((bf16[192,1280]{1,0:T(8,128)(2,1)}, bf16[192,1280]{1,0:T(8,128)(2,1)S(1)}, u32[]{:S(2)}, u32[]{:S(2)}) %collective-permute-start.1) | collective-permute-done | bytes 491552 | tf_op jit(solution)/shard_map/ppermute | solution.py:197
  35.2 9.1 %collective-permute-done = bf16[192,1280]{1,0:T(8,128)(2,1)S(1)} collective-permute-done((bf16[192,1280]{1,0:T(8,128)(2,1)}, bf16[192,1280]{1,0:T(8,128)(2,1)S(1)}, u32[]{:S(2)}, u32[]{:S(2)}) %collective-permute-start) | collective-permute-done | bytes 491552 | tf_op jit(solution)/shard_map/ppermute | solution.py:197
  44.3 2.2 all-to-all-done
  54.4 4.6 %all-to-all-start.1 = ((bf16[4,16,16,1024]{3,2,1,0:T(8,128)(2,1)}), bf16[4,16,16,1024]{3,2,1,0:T(8,128)(2,1)S(1)}, u32[]{:S(2)}, u32[]{:S(2)}) async-start(bf16[4,16,16,1024]{3,2,1,0:T(8,128)(2,1)} %broadcast_in_dim.11), calls=%async_computation.1 | async-start | bytes 4194304 | tf_op jit(solution)/shard_map/all_to_all | solution.py:189
  61.0 3.3 %student.1 = (bf16[1536,1280]{1,0:T(8,128)(2,1)S(1)}, f32[128,1280]{1,0:T(8,128)S(1)}, f32[128,128]{1,0:T(8,128)S(1)}) custom-call(s32[2]{0:T(128)S(1)} %pad_add_fusion.spots_ref, bf16[128,1536]{1,0:T(8,128)(2,1)S(1)} %copy-done.4, bf16[768,1280]{1,0:T(8,128)(2,1)} %constant_dynamic-update-slice_fusion.mine_ref, ...), custom_call_target="tpu_custom_call" | custom-call | tf_op jit(solution)/shard_map/student/pallas_call | solution.py:263
  64.3 1.9 copy-done.1
  67.1 18.9 %all-to-all-done.1 = bf16[4,16,16,1024]{3,2,1,0:T(8,128)(2,1)S(1)} async-done(((bf16[4,16,16,1024]{3,2,1,0:T(8,128)(2,1)}), bf16[4,16,16,1024]{3,2,1,0:T(8,128)(2,1)S(1)}, u32[]{:S(2)}, u32[]{:S(2)}) %all-to-all-start.1) | async-done | bytes 2097184 | tf_op jit(solution)/shard_map/all_to_all | solution.py:189
  87.6 1.9 rows.1
  91.4 2.4 collective-permute-start.5
  95.7 2.7 %collective-permute-start.8 = (f32[64,1024]{1,0:T(8,128)S(1)}, f32[64,1024]{1,0:T(8,128)S(1)}, u32[]{:S(2)}, u32[]{:S(2)}) collective-permute-start(f32[64,1024]{1,0:T(8,128)S(1)} %get-tuple-element.40), channel_id=1, source_target_pairs={{0,384},{128,0},{256,128},{384,256},{1,385},{129,1},{257,129},{385... | collective-permute-start | bytes 786440 | tf_op jit(solution)/shard_map/ppermute | solution.py:197
  98.4 4.3 %collective-permute-start.6 = (f32[64,1024]{1,0:T(8,128)S(1)}, f32[64,1024]{1,0:T(8,128)S(1)}, u32[]{:S(2)}, u32[]{:S(2)}) collective-permute-start(f32[64,1024]{1,0:T(8,128)S(1)} %get-tuple-element.41), channel_id=1, source_target_pairs={{0,128},{128,256},{256,384},{384,0},{1,129},{129,257},{257,385},{3... | collective-permute-start | bytes 786440 | tf_op jit(solution)/shard_map/ppermute | solution.py:197
  103.1 4.1 %collective-permute-done.8 = f32[64,1024]{1,0:T(8,128)S(1)} collective-permute-done((f32[64,1024]{1,0:T(8,128)S(1)}, f32[64,1024]{1,0:T(8,128)S(1)}, u32[]{:S(2)}, u32[]{:S(2)}) %collective-permute-start.8) | collective-permute-done | bytes 262176 | tf_op jit(solution)/shard_map/ppermute | solution.py:197
  108.6 5.5 %collective-permute-start.7 = (f32[128,1024]{1,0:T(8,128)S(1)}, f32[128,1024]{1,0:T(8,128)S(1)}, u32[]{:S(2)}, u32[]{:S(2)}) collective-permute-start(f32[128,1024]{1,0:T(8,128)S(1)} %pad_maximum_fusion), channel_id=1, source_target_pairs={{0,128},{128,256},{256,384},{384,0},{1,129},{129,257},{257,385},{3... | collective-permute-start | bytes 1572872 | tf_op jit(solution)/shard_map/ppermute | solution.py:197
  116.2 8.3 %collective-permute-done.7.prev_ref = f32[128,1024]{1,0:T(8,128)S(1)} collective-permute-done((f32[128,1024]{1,0:T(8,128)S(1)}, f32[128,1024]{1,0:T(8,128)S(1)}, u32[]{:S(2)}, u32[]{:S(2)}) %collective-permute-start.7) | collective-permute-done | bytes 524320 | tf_op jit(solution)/shard_map/ppermute | solution.py:197
  124.5 5.4 %collective-permute-done.9.next_ref = f32[128,1024]{1,0:T(8,128)S(1)} collective-permute-done((f32[128,1024]{1,0:T(8,128)S(1)}, f32[128,1024]{1,0:T(8,128)S(1)}, u32[]{:S(2)}, u32[]{:S(2)}) %collective-permute-start.9) | collective-permute-done | bytes 524320 | tf_op jit(solution)/shard_map/ppermute | solution.py:197
  130.9 11.2 %all-to-all-start.2 = ((bf16[64,2,1152]{2,1,0:T(2,128)(2,1)}), bf16[64,2,1152]{2,1,0:T(2,128)(2,1)S(1)}, u32[]{:S(2)}, u32[]{:S(2)}) async-start(bf16[64,2,1152]{2,1,0:T(2,128)(2,1)} %reshape.60), calls=%async_computation.2 | async-start | bytes 589824 | tf_op jit(solution)/shard_map/all_to_all | solution.py:189
  143.8 2.3 copy-done
  146.1 17.9 %all-to-all-done.2 = bf16[64,2,1152]{2,1,0:T(2,128)(2,1)S(1)} async-done(((bf16[64,2,1152]{2,1,0:T(2,128)(2,1)}), bf16[64,2,1152]{2,1,0:T(2,128)(2,1)S(1)}, u32[]{:S(2)}, u32[]{:S(2)}) %all-to-all-start.2) | async-done | bytes 294944 | tf_op jit(solution)/shard_map/all_to_all | solution.py:189
  164.8 7.8 %align.1 = bf16[2,64,1408]{2,1,0:T(8,128)(2,1)} custom-call(bf16[2,64,1152]{2,1,0:T(8,128)(2,1)} %bitcast.41, bf16[128,128]{1,0:T(8,128)(2,1)} %fusion.3.table_ref, bf16[640,4096]{1,0:T(8,128)(2,1)} %copy-done, s32[512,8]{1,0:T(8,128)} %bitcast.42), custom_call_target="tpu_custom_call" | custom-call | tf_op jit(solution)/shard_map/align/pallas_call | solution.py:287
  172.6 2.1 copy.29
  174.7 4.8 %all-to-all-start.3 = ((bf16[64,2,1408]{2,1,0:T(2,128)(2,1)}), bf16[64,2,1408]{2,1,0:T(2,128)(2,1)S(1)}, u32[]{:S(2)}, u32[]{:S(2)}) async-start(bf16[64,2,1408]{2,1,0:T(2,128)(2,1)} %copy.29), calls=%async_computation.3 | async-start | bytes 720896 | tf_op jit(solution)/shard_map/all_to_all | solution.py:189
  179.5 6.3 %copy.30 = bf16[1536,1280]{0,1:T(8,128)(2,1)} copy(bf16[1536,1280]{1,0:T(8,128)(2,1)} %copy-done.1) | data formatting | bytes 7864320 | tf_op jit(solution)/shard_map/student/pallas_call | solution.py:263
  185.8 18.5 %all-to-all-done.3 = bf16[64,2,1408]{2,1,0:T(2,128)(2,1)S(1)} async-done(((bf16[64,2,1408]{2,1,0:T(2,128)(2,1)}), bf16[64,2,1408]{2,1,0:T(2,128)(2,1)S(1)}, u32[]{:S(2)}, u32[]{:S(2)}) %all-to-all-start.3) | async-done | bytes 360480 | tf_op jit(solution)/shard_map/all_to_all | solution.py:189
  205.2 4.9 %gradient.1 = (f32[128,1664]{1,0:T(8,128)}, f32[128,128]{1,0:T(8,128)}) custom-call(bf16[128,1408]{1,0:T(8,128)(2,1)} %reshape.61.target_ref, f32[128,1280]{1,0:T(8,128)} %copy-done.3, bf16[1280,1536]{1,0:T(8,128)(2,1)} %bitcast.37), custom_call_target="tpu_custom_call" | custom-call | tf_op jit(solution)/shard_map/gradient/pallas_call | solution.py:297
  210.1 13.4 %all_to_all.40 = f32[4,32,1664]{2,1,0:T(8,128)S(1)} all-to-all(f32[4,32,1664]{2,1,0:T(8,128)} %bitcast.46), channel_id=1, replica_groups=mesh['x'=4,'c'=2,'z'=16,'y'=4] {'y'}, dimensions={0} | all-to-all | bytes 1703936 | tf_op jit(solution)/shard_map/all_to_all | solution.py:189
  223.8 19.3 %all_to_all.41.parts_ref = f32[16,2,1664]{2,1,0:T(2,128)S(1)} all-to-all(f32[16,2,1664]{2,1,0:T(2,128)S(1)} %reshape.63), channel_id=1, replica_groups=mesh['x'=4,'c'=2,'z'=16,'y'=4] {'z'}, dimensions={0} | all-to-all | bytes 425984 | tf_op jit(solution)/shard_map/all_to_all | solution.py:189
  243.2 16.8 %all_to_all.42 = bf16[16,2,1664]{2,1,0:T(2,128)(2,1)S(1)} all-to-all(bf16[16,2,1664]{2,1,0:T(2,128)(2,1)S(1)} %broadcast_in_dim.12), channel_id=1, replica_groups=mesh['x'=4,'c'=2,'z'=16,'y'=4] {'z'}, dimensions={0} | all-to-all | bytes 212992 | tf_op jit(solution)/shard_map/all_to_all | solution.py:189
  260.1 9.9 %all_to_all.43 = bf16[4,32,1664]{2,1,0:T(8,128)(2,1)S(1)} all-to-all(bf16[4,32,1664]{2,1,0:T(8,128)(2,1)S(1)} %broadcast_in_dim.14), channel_id=1, replica_groups=mesh['x'=4,'c'=2,'z'=16,'y'=4] {'y'}, dimensions={0} | all-to-all | bytes 851968 | tf_op jit(solution)/shard_map/all_to_all | solution.py:189
  (67 shorter events, 27.5 us)
Async XLA Ops:
  2.3 44.3 %all-to-all-start = ((bf16[16,16,1024]{2,1,0:T(8,128)(2,1)}), bf16[16,16,1024]{2,1,0:T(8,128)(2,1)S(1)}, u32[]{:S(2)}, u32[]{:S(2)}) async-start(bf16[16,16,1024]{2,1,0:T(8,128)(2,1)} %broadcast_in_dim.10), calls=%async_computation | async-start | bytes 1048576 | tf_op jit(solution)/shard_map/all_to_all | solution.py:189
  17.5 17.7 %collective-permute-start.1 = (bf16[192,1280]{1,0:T(8,128)(2,1)}, bf16[192,1280]{1,0:T(8,128)(2,1)S(1)}, u32[]{:S(2)}, u32[]{:S(2)}) collective-permute-start(bf16[192,1280]{1,0:T(8,128)(2,1)} %param.11), channel_id=1, source_target_pairs={{0,256},{128,384},{256,0},{384,128},{1,257},{129,385},{257,1},{385... | collective-permute-start | bytes 1474568 | tf_op jit(solution)/shard_map/ppermute | solution.py:197
  20.8 23.5 %collective-permute-start = (bf16[192,1280]{1,0:T(8,128)(2,1)}, bf16[192,1280]{1,0:T(8,128)(2,1)S(1)}, u32[]{:S(2)}, u32[]{:S(2)}) collective-permute-start(bf16[192,1280]{1,0:T(8,128)(2,1)} %param.11), channel_id=1, source_target_pairs={{0,384},{128,0},{256,128},{384,256},{1,385},{129,1},{257,129},{385... | collective-permute-start | bytes 1474568 | tf_op jit(solution)/shard_map/ppermute | solution.py:197
  22.7 21.6 %collective-permute-start.2 = (bf16[192,1280]{1,0:T(8,128)(2,1)}, bf16[192,1280]{1,0:T(8,128)(2,1)S(1)}, u32[]{:S(2)}, u32[]{:S(2)}) collective-permute-start(bf16[192,1280]{1,0:T(8,128)(2,1)} %param.11), channel_id=1, source_target_pairs={{0,128},{128,256},{256,384},{384,0},{1,129},{129,257},{257,385},{3... | collective-permute-start | bytes 1474568 | tf_op jit(solution)/shard_map/ppermute | solution.py:197
  50.9 10.1 %collective-permute-start.3 = (bf16[768,1280]{1,0:T(8,128)(2,1)}, bf16[768,1280]{1,0:T(8,128)(2,1)}, u32[]{:S(2)}, u32[]{:S(2)}) collective-permute-start(bf16[768,1280]{1,0:T(8,128)(2,1)} %constant_dynamic-update-slice_fusion.mine_ref), channel_id=1, source_target_pairs={{0,64},{64,0},{1,65},{65,1},{2,66},{66,2},{3,67},{67,3},{4,68},{68... | collective-permute-start | bytes 5898248 | tf_op jit(solution)/shard_map/ppermute | solution.py:205
  54.4 4.6 %copy-start.6 = (s32[512,8]{0,1:T(8,128)S(1)}, s32[512,8]{0,1:T(8,128)}, u32[]{:S(2)}) copy-start(s32[512,8]{0,1:T(8,128)} %param.12) | copy-start | bytes 49156
  54.4 4.6 %copy-start.7 = (s32[512,8]{0,1:T(8,128)S(1)}, s32[512,8]{0,1:T(8,128)}, u32[]{:S(2)}) copy-start(s32[512,8]{0,1:T(8,128)} %param.13) | copy-start | bytes 49156
  54.4 5.0 %copy-start.8 = (s32[512,8]{0,1:T(8,128)S(1)}, s32[512,8]{0,1:T(8,128)}, u32[]{:S(2)}) copy-start(s32[512,8]{0,1:T(8,128)} %param.14) | copy-start | bytes 49156
  54.4 6.1 %copy-start.9 = (s32[512,8]{0,1:T(8,128)S(1)}, s32[512,8]{0,1:T(8,128)}, u32[]{:S(2)}) copy-start(s32[512,8]{0,1:T(8,128)} %param.15) | copy-start | bytes 49156
  54.4 31.6 %all-to-all-start.1 = ((bf16[4,16,16,1024]{3,2,1,0:T(8,128)(2,1)}), bf16[4,16,16,1024]{3,2,1,0:T(8,128)(2,1)S(1)}, u32[]{:S(2)}, u32[]{:S(2)}) async-start(bf16[4,16,16,1024]{3,2,1,0:T(8,128)(2,1)} %broadcast_in_dim.11), calls=%async_computation.1 | async-start | bytes 4194304 | tf_op jit(solution)/shard_map/all_to_all | solution.py:189
  59.0 2.0 copy-start.4
  64.3 2.0 copy-start.1
  66.3 0.8 copy-start.3
  86.0 1.6 copy-start.2
  89.5 13.2 %collective-permute-start.4 = (f32[384,1024]{1,0:T(8,128)S(1)}, f32[384,1024]{1,0:T(8,128)S(1)}, u32[]{:S(2)}, u32[]{:S(2)}) collective-permute-start(f32[384,1024]{1,0:T(8,128)S(1)} %get-tuple-element.26), channel_id=1, source_target_pairs={{0,64},{64,0},{1,65},{65,1},{2,66},{66,2},{3,67},{67,3},{4,68},{68... | collective-permute-start | bytes 4718600 | tf_op jit(solution)/shard_map/ppermute | solution.py:205
  91.4 4.1 %collective-permute-start.5 = (f32[128,1024]{1,0:T(8,128)S(1)}, f32[128,1024]{1,0:T(8,128)S(1)}, u32[]{:S(2)}, u32[]{:S(2)}) collective-permute-start(f32[128,1024]{1,0:T(8,128)S(1)} %get-tuple-element.27), channel_id=1, source_target_pairs={{0,64},{64,0},{1,65},{65,1},{2,66},{66,2},{3,67},{67,3},{4,68},{68... | collective-permute-start | bytes 1572872 | tf_op jit(solution)/shard_map/ppermute | solution.py:205
  95.7 11.5 %collective-permute-start.8 = (f32[64,1024]{1,0:T(8,128)S(1)}, f32[64,1024]{1,0:T(8,128)S(1)}, u32[]{:S(2)}, u32[]{:S(2)}) collective-permute-start(f32[64,1024]{1,0:T(8,128)S(1)} %get-tuple-element.40), channel_id=1, source_target_pairs={{0,384},{128,0},{256,128},{384,256},{1,385},{129,1},{257,129},{385... | collective-permute-start | bytes 786440 | tf_op jit(solution)/shard_map/ppermute | solution.py:197
  98.4 10.0 %collective-permute-start.6 = (f32[64,1024]{1,0:T(8,128)S(1)}, f32[64,1024]{1,0:T(8,128)S(1)}, u32[]{:S(2)}, u32[]{:S(2)}) collective-permute-start(f32[64,1024]{1,0:T(8,128)S(1)} %get-tuple-element.41), channel_id=1, source_target_pairs={{0,128},{128,256},{256,384},{384,0},{1,129},{129,257},{257,385},{3... | collective-permute-start | bytes 786440 | tf_op jit(solution)/shard_map/ppermute | solution.py:197
  108.6 15.9 %collective-permute-start.7 = (f32[128,1024]{1,0:T(8,128)S(1)}, f32[128,1024]{1,0:T(8,128)S(1)}, u32[]{:S(2)}, u32[]{:S(2)}) collective-permute-start(f32[128,1024]{1,0:T(8,128)S(1)} %pad_maximum_fusion), channel_id=1, source_target_pairs={{0,128},{128,256},{256,384},{384,0},{1,129},{129,257},{257,385},{3... | collective-permute-start | bytes 1572872 | tf_op jit(solution)/shard_map/ppermute | solution.py:197
  114.2 15.7 %collective-permute-start.9 = (f32[128,1024]{1,0:T(8,128)S(1)}, f32[128,1024]{1,0:T(8,128)S(1)}, u32[]{:S(2)}, u32[]{:S(2)}) collective-permute-start(f32[128,1024]{1,0:T(8,128)S(1)} %pad_maximum_fusion.1), channel_id=1, source_target_pairs={{0,384},{128,0},{256,128},{384,256},{1,385},{129,1},{257,129},{385... | collective-permute-start | bytes 1572872 | tf_op jit(solution)/shard_map/ppermute | solution.py:197
  130.9 33.1 %all-to-all-start.2 = ((bf16[64,2,1152]{2,1,0:T(2,128)(2,1)}), bf16[64,2,1152]{2,1,0:T(2,128)(2,1)S(1)}, u32[]{:S(2)}, u32[]{:S(2)}) async-start(bf16[64,2,1152]{2,1,0:T(2,128)(2,1)} %reshape.60), calls=%async_computation.2 | async-start | bytes 589824 | tf_op jit(solution)/shard_map/all_to_all | solution.py:189
  143.8 2.3 copy-start
  174.7 29.7 %all-to-all-start.3 = ((bf16[64,2,1408]{2,1,0:T(2,128)(2,1)}), bf16[64,2,1408]{2,1,0:T(2,128)(2,1)S(1)}, u32[]{:S(2)}, u32[]{:S(2)}) async-start(bf16[64,2,1408]{2,1,0:T(2,128)(2,1)} %copy.29), calls=%async_computation.3 | async-start | bytes 720896 | tf_op jit(solution)/shard_map/all_to_all | solution.py:189
  223.6 47.2 %copy-start.5 = (f32[128,128]{1,0:T(8,128)S(1)}, f32[128,128]{1,0:T(8,128)}, u32[]{:S(2)}) copy-start(f32[128,128]{1,0:T(8,128)} %get-tuple-element.34) | copy-start | bytes 196612

commit v6 on v5

--- a/solution.py
+++ b/solution.py
@@ -5,6 +5,7 @@
 from jax.experimental.pallas import tpu as pltpu
 from jax.sharding import Mesh
 from jax.sharding import PartitionSpec as P
+
 
 BLOCK = 128
 TB_DEV = 8
@@ -29,7 +30,7 @@
 WHOLE_VMEM = 117 * 512 * 1024
 
 
-def kernel_call(kernel, out_shape, scratch=(), name=None, inputs=""):
+def kernel_call(kernel, out_shape, scratch=(), inputs=""):
     spaces = {"s": pltpu.SMEM, "v": pltpu.VMEM, "h": pl.ANY}
     return pl.pallas_call(
         kernel,
@@ -37,7 +38,6 @@
         in_specs=[pl.BlockSpec(memory_space=spaces[kind]) for kind in inputs],
         scratch_shapes=list(scratch),
         compiler_params=pltpu.CompilerParams(vmem_limit_bytes=WHOLE_VMEM if "h" in inputs else VMEM_BYTES),
-        name=name,
     )
 
 
@@ -82,8 +82,8 @@
 
 def student_kernel(spots_ref, hidden_ref, mine_ref, theirs_ref, head_ref, logits_ref, stats_ref):
     c = spots_ref[1]
-    for step in range(NX):
-        rows = slice(step * PIECE, (step + 1) * PIECE)
+    for place, step in enumerate((0, 1, 3, 2)):
+        rows = slice(place * PIECE, (place + 1) * PIECE)
         put_rows(head_ref, spots_ref, step, c, mine_ref[rows, :])
         put_rows(head_ref, spots_ref, step, 1 - c, theirs_ref[rows, :])
     logits = jnp.dot(hidden_ref[...], head_ref[...], preferred_element_type=F32)
@@ -221,7 +221,6 @@
             jax.ShapeDtypeStruct((4 * chunk, width), BF16),
         ),
         [pltpu.VMEM(rows.shape, BF16), pltpu.VMEM((4 * chunk, width), BF16)] ,
-        "rows",
         "svv",
     )(spots, rows, head)
     far_theirs = send_c(far_theirs)
@@ -237,7 +236,7 @@
     return near[2 * chunk :], send_x(after, 1), send_x(before, -1)
 
 
-def body(
+def step(
     teacher_hidden,
     teacher_head,
     student_hidden,
@@ -251,8 +250,7 @@
     spots = jnp.stack([lax.axis_index("x"), lax.axis_index("c")]).astype(jnp.int32)
 
     rows = spread(teacher_hidden, "z", NZ)
-    pieces = [student_head, send_x(student_head, -1), send_x(student_head, 2), send_x(student_head, 1)]
-    pieces = lax.optimization_barrier((rows, *pieces))[1:]
+    pieces = [student_head, send_x(student_head, -1), send_x(student_head, 1), send_x(student_head, 2)]
     head_mine = jnp.concatenate(pieces, axis=0)
     head_theirs = send_c(head_mine)
     rows = spread(rows, "y", NY)
@@ -268,27 +266,22 @@
             jax.ShapeDtypeStruct((tok_rows, BLOCK), F32),
         ),
         (),
-        "student",
         "svvv",
     )(spots, student_hidden, head_mine, head_theirs)
     rows, place, count, shift, stats = lax.optimization_barrier((rows, place, count, shift, stats))
 
     own, before, after = logit_parts(rows, teacher_head, spots)
     outgoing = kernel_call(
-        softmax_kernel, jax.ShapeDtypeStruct((tok_rows, TCOLS + BLOCK), BF16), name="softmax", inputs="vvvv"
+        softmax_kernel, jax.ShapeDtypeStruct((tok_rows, TCOLS + BLOCK), BF16), inputs="vvvv"
     )(own, before, after, stats)
     weight = kernel_call(
-        weight_kernel,
-        jax.ShapeDtypeStruct((SBLOCKS, FANOUT * TBLOCKS), BF16),
-        name="weight",
-        inputs="vv",
+        weight_kernel, jax.ShapeDtypeStruct((SBLOCKS, FANOUT * TBLOCKS), BF16), inputs="vv"
     )(place, count)
     received = exchange(outgoing.reshape(N_VOC, OWN, TCOLS + BLOCK), ("z", "y"))
     target = kernel_call(
         align_kernel,
         jax.ShapeDtypeStruct((OWN, N_VOC, SCOLS + BLOCK), BF16),
         [pltpu.VMEM((FANOUT * TBLOCKS, OWN * BLOCK), BF16)] + arriving(weight.shape),
-        "align",
         "vvhv",
     )(received.transpose(1, 0, 2), base_kernel(), weight, shift)
     target = exchange(target.transpose(1, 0, 2), ("z", "y")).reshape(tok_rows, SCOLS + BLOCK)
@@ -298,14 +291,11 @@
         grad_kernel,
         (jax.ShapeDtypeStruct((tok_rows, WIDE), F32), jax.ShapeDtypeStruct((tok_rows, BLOCK), F32)),
         arriving(turned.shape),
-        "gradient",
         "vvh",
     )(target, student_logits, turned)
     terms = exchange(terms.reshape(NY, tok_rows // NY, WIDE), "y").sum(axis=0)
     terms = exchange(terms.reshape(NZ, OWN, WIDE), "z")
-    result = kernel_call(
-        finish_kernel, jax.ShapeDtypeStruct((OWN, WIDE), BF16), name="finish", inputs="v"
-    )(terms)
+    result = kernel_call(finish_kernel, jax.ShapeDtypeStruct((OWN, WIDE), BF16), inputs="v")(terms)
     result = spread(result, "z", NZ).reshape(NZ * OWN, WIDE)
     result = spread(result, "y", NY).reshape(tok_rows, WIDE)
     token_loss = log_total[:, 0] - unpack_lane(result[:, DS:], 0)[:, 0]
@@ -327,4 +317,4 @@
         P(),
     )
     out_specs = (P(tok), P(tok, None))
-    return jax.shard_map(body, mesh=grid, in_specs=in_specs, out_specs=out_specs, check_vma=False)
+    return jax.shard_map(step, mesh=grid, in_specs=in_specs, out_specs=out_specs, check_vma=False)

time: 273 us -> 274 us (level); the launches traced: 272 us -> 270 us
  transfers between devices with their start and end apart: 14 -> 14, of which waited for: 11 -> 10; matrix products, arithmetic and copies ran while one was open for 5% -> 6% of each run, Pallas kernels for 2% -> 2%
where the time goes in v6:
time: 274 us; the launch traced here: 270 us
  waiting for transfers between devices  90.8 us (33%)
  starting transfers between devices  67.9 us (25%)
  blocking collectives  59.5 us (22%)
  local copies, waits for them, and re-layouts  28.1 us (10%)
  Pallas kernels  19.2 us (7%)
    all_to_all x4, blocking collectives, exchange(): return lax.all_to_all(value, axis, split_axis=0, concat_axis=0, tiled=True)  59.5 us
    all_to_all x4, waiting for transfers between devices, exchange(): return lax.all_to_all(value, axis, split_axis=0, concat_axis=0, tiled=True)  55.4 us
    all_to_all x4, starting transfers between devices, exchange(): return lax.all_to_all(value, axis, split_axis=0, concat_axis=0, tiled=True)  38 us
    ppermute x7, waiting for transfers between devices, send(): lax.ppermute(value, axis, [(i, (i + step) % size) for i in range(size)])  34.9 us
    ppermute x7, starting transfers between devices, send(): lax.ppermute(value, axis, [(i, (i + step) % size) for i in range(size)])  23.6 us
    unnamed x25, local copies, waits for them, and re-layouts  10.3 us
    pallas_call x1, Pallas kernels, step(): kernel_call(align_kernel, jax.ShapeDtypeStruct((OWN, N_VOC, SCOLS + BLOCK...  7.78 us
    pallas_call x1, local copies, waits for them, and re-layouts, step(): kernel_call(student_kernel, (jax.ShapeDtypeStruct((DS, SCOLS), BF16), jax...  6.3 us
  transfers between devices with their start and end apart: 14, of which 10 were waited for; matrix products, arithmetic and copies ran while one was open for 6% of the time, Pallas kernels for 2%

profile of v6, /device:TPU:6, one launch (start us, length us, event | category | flops | bytes accessed | tf_op | source)
XLA Modules:
  0.0 269.7 jit_solution(15277339287806598260)
XLA Ops:
  2.3 15.2 %all-to-all-start = ((bf16[16,16,1024]{2,1,0:T(8,128)(2,1)}), bf16[16,16,1024]{2,1,0:T(8,128)(2,1)S(1)}, u32[]{:S(2)}, u32[]{:S(2)}) async-start(bf16[16,16,1024]{2,1,0:T(8,128)(2,1)} %broadcast_in_dim.10), calls=%async_computation | async-start | bytes 1048576 | tf_op jit(solution)/shard_map/all_to_all | solution.py:189
  17.5 2.7 %collective-permute-start = (bf16[192,1280]{1,0:T(8,128)(2,1)}, bf16[192,1280]{1,0:T(8,128)(2,1)S(1)}, u32[]{:S(2)}, u32[]{:S(2)}) collective-permute-start(bf16[192,1280]{1,0:T(8,128)(2,1)} %param.11), channel_id=1, source_target_pairs={{0,384},{128,0},{256,128},{384,256},{1,385},{129,1},{257,129},{385... | collective-permute-start | bytes 1474568 | tf_op jit(solution)/shard_map/ppermute | solution.py:197
  20.2 4.3 %collective-permute-start.1 = (bf16[192,1280]{1,0:T(8,128)(2,1)}, bf16[192,1280]{1,0:T(8,128)(2,1)S(1)}, u32[]{:S(2)}, u32[]{:S(2)}) collective-permute-start(bf16[192,1280]{1,0:T(8,128)(2,1)} %param.11), channel_id=1, source_target_pairs={{0,128},{128,256},{256,384},{384,0},{1,129},{129,257},{257,385},{3... | collective-permute-start | bytes 1474568 | tf_op jit(solution)/shard_map/ppermute | solution.py:197
  24.5 2.1 collective-permute-start.2
  28.5 15.5 %collective-permute-done = bf16[192,1280]{1,0:T(8,128)(2,1)S(1)} collective-permute-done((bf16[192,1280]{1,0:T(8,128)(2,1)}, bf16[192,1280]{1,0:T(8,128)(2,1)S(1)}, u32[]{:S(2)}, u32[]{:S(2)}) %collective-permute-start) | collective-permute-done | bytes 491552 | tf_op jit(solution)/shard_map/ppermute | solution.py:197
  50.5 4.6 %all-to-all-start.1 = ((bf16[4,16,16,1024]{3,2,1,0:T(8,128)(2,1)}), bf16[4,16,16,1024]{3,2,1,0:T(8,128)(2,1)S(1)}, u32[]{:S(2)}, u32[]{:S(2)}) async-start(bf16[4,16,16,1024]{3,2,1,0:T(8,128)(2,1)} %broadcast_in_dim.11), calls=%async_computation.1 | async-start | bytes 4194304 | tf_op jit(solution)/shard_map/all_to_all | solution.py:189
  57.1 3.3 %shard_map.95 = (bf16[1536,1280]{1,0:T(8,128)(2,1)S(1)}, f32[128,1280]{1,0:T(8,128)S(1)}, f32[128,128]{1,0:T(8,128)S(1)}) custom-call(s32[2]{0:T(128)S(1)} %pad_add_fusion.spots_ref, bf16[128,1536]{1,0:T(8,128)(2,1)S(1)} %copy-done.4, bf16[768,1280]{1,0:T(8,128)(2,1)} %constant_dynamic-update-slice_fusion.mine_ref, ...), custom_call_target="tpu_custom_call" | custom-call | tf_op jit(solution)/shard_map/pallas_call | solution.py:261
  60.4 1.9 copy-done.1
  63.2 18.9 %all-to-all-done.1 = bf16[4,16,16,1024]{3,2,1,0:T(8,128)(2,1)S(1)} async-done(((bf16[4,16,16,1024]{3,2,1,0:T(8,128)(2,1)}), bf16[4,16,16,1024]{3,2,1,0:T(8,128)(2,1)S(1)}, u32[]{:S(2)}, u32[]{:S(2)}) %all-to-all-start.1) | async-done | bytes 2097184 | tf_op jit(solution)/shard_map/all_to_all | solution.py:189
  83.7 1.9 shard_map.96
  85.6 1.9 collective-permute-start.4
  87.6 2.4 collective-permute-start.5
  91.8 5.5 %collective-permute-start.6 = (f32[64,1024]{1,0:T(8,128)S(1)}, f32[64,1024]{1,0:T(8,128)S(1)}, u32[]{:S(2)}, u32[]{:S(2)}) collective-permute-start(f32[64,1024]{1,0:T(8,128)S(1)} %get-tuple-element.33), channel_id=1, source_target_pairs={{0,128},{128,256},{256,384},{384,0},{1,129},{129,257},{257,385},{3... | collective-permute-start | bytes 786440 | tf_op jit(solution)/shard_map/ppermute | solution.py:197
  97.3 1.9 collective-permute-start.8
  99.6 3.6 %collective-permute-done.6 = f32[64,1024]{1,0:T(8,128)S(1)} collective-permute-done((f32[64,1024]{1,0:T(8,128)S(1)}, f32[64,1024]{1,0:T(8,128)S(1)}, u32[]{:S(2)}, u32[]{:S(2)}) %collective-permute-start.6) | collective-permute-done | bytes 262176 | tf_op jit(solution)/shard_map/ppermute | solution.py:197
  103.2 5.3 %collective-permute-done.8 = f32[64,1024]{1,0:T(8,128)S(1)} collective-permute-done((f32[64,1024]{1,0:T(8,128)S(1)}, f32[64,1024]{1,0:T(8,128)S(1)}, u32[]{:S(2)}, u32[]{:S(2)}) %collective-permute-start.8) | collective-permute-done | bytes 262176 | tf_op jit(solution)/shard_map/ppermute | solution.py:197
  108.7 1.9 collective-permute-start.9
  110.7 5.1 %collective-permute-start.7 = (f32[128,1024]{1,0:T(8,128)S(1)}, f32[128,1024]{1,0:T(8,128)S(1)}, u32[]{:S(2)}, u32[]{:S(2)}) collective-permute-start(f32[128,1024]{1,0:T(8,128)S(1)} %pad_maximum_fusion), channel_id=1, source_target_pairs={{0,128},{128,256},{256,384},{384,0},{1,129},{129,257},{257,385},{3... | collective-permute-start | bytes 1572872 | tf_op jit(solution)/shard_map/ppermute | solution.py:197
  115.8 8.8 %collective-permute-done.9.next_ref = f32[128,1024]{1,0:T(8,128)S(1)} collective-permute-done((f32[128,1024]{1,0:T(8,128)S(1)}, f32[128,1024]{1,0:T(8,128)S(1)}, u32[]{:S(2)}, u32[]{:S(2)}) %collective-permute-start.9) | collective-permute-done | bytes 524320 | tf_op jit(solution)/shard_map/ppermute | solution.py:197
  126.9 13.4 %all-to-all-start.2 = ((bf16[64,2,1152]{2,1,0:T(2,128)(2,1)}), bf16[64,2,1152]{2,1,0:T(2,128)(2,1)S(1)}, u32[]{:S(2)}, u32[]{:S(2)}) async-start(bf16[64,2,1152]{2,1,0:T(2,128)(2,1)} %reshape.60), calls=%async_computation.2 | async-start | bytes 589824 | tf_op jit(solution)/shard_map/all_to_all | solution.py:189
  142.0 2.3 copy-done
  144.3 17.9 %all-to-all-done.2 = bf16[64,2,1152]{2,1,0:T(2,128)(2,1)S(1)} async-done(((bf16[64,2,1152]{2,1,0:T(2,128)(2,1)}), bf16[64,2,1152]{2,1,0:T(2,128)(2,1)S(1)}, u32[]{:S(2)}, u32[]{:S(2)}) %all-to-all-start.2) | async-done | bytes 294944 | tf_op jit(solution)/shard_map/all_to_all | solution.py:189
  163.0 7.8 %shard_map.99 = bf16[2,64,1408]{2,1,0:T(8,128)(2,1)} custom-call(bf16[2,64,1152]{2,1,0:T(8,128)(2,1)} %bitcast.41, bf16[128,128]{1,0:T(8,128)(2,1)} %fusion.3.table_ref, bf16[640,4096]{1,0:T(8,128)(2,1)} %copy-done, s32[512,8]{1,0:T(8,128)} %bitcast.42), custom_call_target="tpu_custom_call" | custom-call | tf_op jit(solution)/shard_map/pallas_call | solution.py:281
  170.8 2.1 copy.29
  172.9 4.8 %all-to-all-start.3 = ((bf16[64,2,1408]{2,1,0:T(2,128)(2,1)}), bf16[64,2,1408]{2,1,0:T(2,128)(2,1)S(1)}, u32[]{:S(2)}, u32[]{:S(2)}) async-start(bf16[64,2,1408]{2,1,0:T(2,128)(2,1)} %copy.29), calls=%async_computation.3 | async-start | bytes 720896 | tf_op jit(solution)/shard_map/all_to_all | solution.py:189
  177.7 6.3 %copy.30 = bf16[1536,1280]{0,1:T(8,128)(2,1)} copy(bf16[1536,1280]{1,0:T(8,128)(2,1)} %copy-done.1) | data formatting | bytes 7864320 | tf_op jit(solution)/shard_map/pallas_call | solution.py:261
  184.0 18.5 %all-to-all-done.3 = bf16[64,2,1408]{2,1,0:T(2,128)(2,1)S(1)} async-done(((bf16[64,2,1408]{2,1,0:T(2,128)(2,1)}), bf16[64,2,1408]{2,1,0:T(2,128)(2,1)S(1)}, u32[]{:S(2)}, u32[]{:S(2)}) %all-to-all-start.3) | async-done | bytes 360480 | tf_op jit(solution)/shard_map/all_to_all | solution.py:189
  203.4 4.9 %shard_map.100 = (f32[128,1664]{1,0:T(8,128)}, f32[128,128]{1,0:T(8,128)}) custom-call(bf16[128,1408]{1,0:T(8,128)(2,1)} %reshape.61.target_ref, f32[128,1280]{1,0:T(8,128)} %copy-done.3, bf16[1280,1536]{1,0:T(8,128)(2,1)} %bitcast.37), custom_call_target="tpu_custom_call" | custom-call | tf_op jit(solution)/shard_map/pallas_call | solution.py:290
  208.3 13.4 %all_to_all.40 = f32[4,32,1664]{2,1,0:T(8,128)S(1)} all-to-all(f32[4,32,1664]{2,1,0:T(8,128)} %bitcast.46), channel_id=1, replica_groups=mesh['x'=4,'c'=2,'z'=16,'y'=4] {'y'}, dimensions={0} | all-to-all | bytes 1703936 | tf_op jit(solution)/shard_map/all_to_all | solution.py:189
  222.0 19.3 %all_to_all.41.parts_ref = f32[16,2,1664]{2,1,0:T(2,128)S(1)} all-to-all(f32[16,2,1664]{2,1,0:T(2,128)S(1)} %reshape.63), channel_id=1, replica_groups=mesh['x'=4,'c'=2,'z'=16,'y'=4] {'z'}, dimensions={0} | all-to-all | bytes 425984 | tf_op jit(solution)/shard_map/all_to_all | solution.py:189
  241.5 16.8 %all_to_all.42 = bf16[16,2,1664]{2,1,0:T(2,128)(2,1)S(1)} all-to-all(bf16[16,2,1664]{2,1,0:T(2,128)(2,1)S(1)} %broadcast_in_dim.12), channel_id=1, replica_groups=mesh['x'=4,'c'=2,'z'=16,'y'=4] {'z'}, dimensions={0} | all-to-all | bytes 212992 | tf_op jit(solution)/shard_map/all_to_all | solution.py:189
  258.3 9.9 %all_to_all.43 = bf16[4,32,1664]{2,1,0:T(8,128)(2,1)S(1)} all-to-all(bf16[4,32,1664]{2,1,0:T(8,128)(2,1)S(1)} %broadcast_in_dim.14), channel_id=1, replica_groups=mesh['x'=4,'c'=2,'z'=16,'y'=4] {'y'}, dimensions={0} | all-to-all | bytes 851968 | tf_op jit(solution)/shard_map/all_to_all | solution.py:189
  (67 shorter events, 24.1 us)
Async XLA Ops:
  2.3 46.6 %all-to-all-start = ((bf16[16,16,1024]{2,1,0:T(8,128)(2,1)}), bf16[16,16,1024]{2,1,0:T(8,128)(2,1)S(1)}, u32[]{:S(2)}, u32[]{:S(2)}) async-start(bf16[16,16,1024]{2,1,0:T(8,128)(2,1)} %broadcast_in_dim.10), calls=%async_computation | async-start | bytes 1048576 | tf_op jit(solution)/shard_map/all_to_all | solution.py:189
  17.5 26.5 %collective-permute-start = (bf16[192,1280]{1,0:T(8,128)(2,1)}, bf16[192,1280]{1,0:T(8,128)(2,1)S(1)}, u32[]{:S(2)}, u32[]{:S(2)}) collective-permute-start(bf16[192,1280]{1,0:T(8,128)(2,1)} %param.11), channel_id=1, source_target_pairs={{0,384},{128,0},{256,128},{384,256},{1,385},{129,1},{257,129},{385... | collective-permute-start | bytes 1474568 | tf_op jit(solution)/shard_map/ppermute | solution.py:197
  20.2 25.1 %collective-permute-start.1 = (bf16[192,1280]{1,0:T(8,128)(2,1)}, bf16[192,1280]{1,0:T(8,128)(2,1)S(1)}, u32[]{:S(2)}, u32[]{:S(2)}) collective-permute-start(bf16[192,1280]{1,0:T(8,128)(2,1)} %param.11), channel_id=1, source_target_pairs={{0,128},{128,256},{256,384},{384,0},{1,129},{129,257},{257,385},{3... | collective-permute-start | bytes 1474568 | tf_op jit(solution)/shard_map/ppermute | solution.py:197
  24.5 21.6 %collective-permute-start.2 = (bf16[192,1280]{1,0:T(8,128)(2,1)}, bf16[192,1280]{1,0:T(8,128)(2,1)S(1)}, u32[]{:S(2)}, u32[]{:S(2)}) collective-permute-start(bf16[192,1280]{1,0:T(8,128)(2,1)} %param.11), channel_id=1, source_target_pairs={{0,256},{128,384},{256,0},{384,128},{1,257},{129,385},{257,1},{385... | collective-permute-start | bytes 1474568 | tf_op jit(solution)/shard_map/ppermute | solution.py:197
  47.0 10.1 %collective-permute-start.3 = (bf16[768,1280]{1,0:T(8,128)(2,1)}, bf16[768,1280]{1,0:T(8,128)(2,1)}, u32[]{:S(2)}, u32[]{:S(2)}) collective-permute-start(bf16[768,1280]{1,0:T(8,128)(2,1)} %constant_dynamic-update-slice_fusion.mine_ref), channel_id=1, source_target_pairs={{0,64},{64,0},{1,65},{65,1},{2,66},{66,2},{3,67},{67,3},{4,68},{68... | collective-permute-start | bytes 5898248 | tf_op jit(solution)/shard_map/ppermute | solution.py:205
  50.5 4.6 %copy-start.6 = (s32[512,8]{0,1:T(8,128)S(1)}, s32[512,8]{0,1:T(8,128)}, u32[]{:S(2)}) copy-start(s32[512,8]{0,1:T(8,128)} %param.14) | copy-start | bytes 49156
  50.5 5.7 %copy-start.7 = (s32[512,8]{0,1:T(8,128)S(1)}, s32[512,8]{0,1:T(8,128)}, u32[]{:S(2)}) copy-start(s32[512,8]{0,1:T(8,128)} %param.12) | copy-start | bytes 49156
  50.5 5.7 %copy-start.8 = (s32[512,8]{0,1:T(8,128)S(1)}, s32[512,8]{0,1:T(8,128)}, u32[]{:S(2)}) copy-start(s32[512,8]{0,1:T(8,128)} %param.13) | copy-start | bytes 49156
  50.5 6.1 %copy-start.9 = (s32[512,8]{0,1:T(8,128)S(1)}, s32[512,8]{0,1:T(8,128)}, u32[]{:S(2)}) copy-start(s32[512,8]{0,1:T(8,128)} %param.15) | copy-start | bytes 49156
  50.5 31.6 %all-to-all-start.1 = ((bf16[4,16,16,1024]{3,2,1,0:T(8,128)(2,1)}), bf16[4,16,16,1024]{3,2,1,0:T(8,128)(2,1)S(1)}, u32[]{:S(2)}, u32[]{:S(2)}) async-start(bf16[4,16,16,1024]{3,2,1,0:T(8,128)(2,1)} %broadcast_in_dim.11), calls=%async_computation.1 | async-start | bytes 4194304 | tf_op jit(solution)/shard_map/all_to_all | solution.py:189
  55.1 2.0 copy-start.4
  60.4 2.0 copy-start.1
  62.4 0.8 copy-start.3
  82.1 1.6 copy-start.2
  85.6 13.6 %collective-permute-start.4 = (f32[384,1024]{1,0:T(8,128)S(1)}, f32[384,1024]{1,0:T(8,128)S(1)}, u32[]{:S(2)}, u32[]{:S(2)}) collective-permute-start(f32[384,1024]{1,0:T(8,128)S(1)} %get-tuple-element.18), channel_id=1, source_target_pairs={{0,64},{64,0},{1,65},{65,1},{2,66},{66,2},{3,67},{67,3},{4,68},{68... | collective-permute-start | bytes 4718600 | tf_op jit(solution)/shard_map/ppermute | solution.py:205
  87.6 4.1 %collective-permute-start.5 = (f32[128,1024]{1,0:T(8,128)S(1)}, f32[128,1024]{1,0:T(8,128)S(1)}, u32[]{:S(2)}, u32[]{:S(2)}) collective-permute-start(f32[128,1024]{1,0:T(8,128)S(1)} %get-tuple-element.19), channel_id=1, source_target_pairs={{0,64},{64,0},{1,65},{65,1},{2,66},{66,2},{3,67},{67,3},{4,68},{68... | collective-permute-start | bytes 1572872 | tf_op jit(solution)/shard_map/ppermute | solution.py:205
  91.8 11.4 %collective-permute-start.6 = (f32[64,1024]{1,0:T(8,128)S(1)}, f32[64,1024]{1,0:T(8,128)S(1)}, u32[]{:S(2)}, u32[]{:S(2)}) collective-permute-start(f32[64,1024]{1,0:T(8,128)S(1)} %get-tuple-element.33), channel_id=1, source_target_pairs={{0,128},{128,256},{256,384},{384,0},{1,129},{129,257},{257,385},{3... | collective-permute-start | bytes 786440 | tf_op jit(solution)/shard_map/ppermute | solution.py:197
  97.3 11.2 %collective-permute-start.8 = (f32[64,1024]{1,0:T(8,128)S(1)}, f32[64,1024]{1,0:T(8,128)S(1)}, u32[]{:S(2)}, u32[]{:S(2)}) collective-permute-start(f32[64,1024]{1,0:T(8,128)S(1)} %get-tuple-element.32), channel_id=1, source_target_pairs={{0,384},{128,0},{256,128},{384,256},{1,385},{129,1},{257,129},{385... | collective-permute-start | bytes 786440 | tf_op jit(solution)/shard_map/ppermute | solution.py:197
  108.7 16.0 %collective-permute-start.9 = (f32[128,1024]{1,0:T(8,128)S(1)}, f32[128,1024]{1,0:T(8,128)S(1)}, u32[]{:S(2)}, u32[]{:S(2)}) collective-permute-start(f32[128,1024]{1,0:T(8,128)S(1)} %pad_maximum_fusion.1), channel_id=1, source_target_pairs={{0,384},{128,0},{256,128},{384,256},{1,385},{129,1},{257,129},{385... | collective-permute-start | bytes 1572872 | tf_op jit(solution)/shard_map/ppermute | solution.py:197
  110.7 15.2 %collective-permute-start.7 = (f32[128,1024]{1,0:T(8,128)S(1)}, f32[128,1024]{1,0:T(8,128)S(1)}, u32[]{:S(2)}, u32[]{:S(2)}) collective-permute-start(f32[128,1024]{1,0:T(8,128)S(1)} %pad_maximum_fusion), channel_id=1, source_target_pairs={{0,128},{128,256},{256,384},{384,0},{1,129},{129,257},{257,385},{3... | collective-permute-start | bytes 1572872 | tf_op jit(solution)/shard_map/ppermute | solution.py:197
  126.9 35.3 %all-to-all-start.2 = ((bf16[64,2,1152]{2,1,0:T(2,128)(2,1)}), bf16[64,2,1152]{2,1,0:T(2,128)(2,1)S(1)}, u32[]{:S(2)}, u32[]{:S(2)}) async-start(bf16[64,2,1152]{2,1,0:T(2,128)(2,1)} %reshape.60), calls=%async_computation.2 | async-start | bytes 589824 | tf_op jit(solution)/shard_map/all_to_all | solution.py:189
  142.0 2.3 copy-start
  172.9 29.7 %all-to-all-start.3 = ((bf16[64,2,1408]{2,1,0:T(2,128)(2,1)}), bf16[64,2,1408]{2,1,0:T(2,128)(2,1)S(1)}, u32[]{:S(2)}, u32[]{:S(2)}) async-start(bf16[64,2,1408]{2,1,0:T(2,128)(2,1)} %copy.29), calls=%async_computation.3 | async-start | bytes 720896 | tf_op jit(solution)/shard_map/all_to_all | solution.py:189
  221.8 47.2 %copy-start.5 = (f32[128,128]{1,0:T(8,128)S(1)}, f32[128,128]{1,0:T(8,128)}, u32[]{:S(2)}) copy-start(f32[128,128]{1,0:T(8,128)} %get-tuple-element.26) | copy-start | bytes 196612

commit v7 on v6

--- a/solution.py
+++ b/solution.py
@@ -27,22 +27,18 @@
 F32 = jnp.float32
 BF16 = jnp.bfloat16
 VMEM_BYTES = 24 * 1024 * 1024
-WHOLE_VMEM = 117 * 512 * 1024
-
-
-def kernel_call(kernel, out_shape, scratch=(), inputs=""):
-    spaces = {"s": pltpu.SMEM, "v": pltpu.VMEM, "h": pl.ANY}
+
+
+def kernel_call(kernel, out_shape, scratch=(), inputs="", flops=0):
+    spaces = {"s": pltpu.SMEM, "v": pltpu.VMEM}
     return pl.pallas_call(
         kernel,
         out_shape=out_shape,
         in_specs=[pl.BlockSpec(memory_space=spaces[kind]) for kind in inputs],
         scratch_shapes=list(scratch),
-        compiler_params=pltpu.CompilerParams(vmem_limit_bytes=WHOLE_VMEM if "h" in inputs else VMEM_BYTES),
+        compiler_params=pltpu.CompilerParams(vmem_limit_bytes=VMEM_BYTES),
+        cost_estimate=pl.CostEstimate(flops=flops, bytes_accessed=1 << 20, transcendentals=0) if flops else None,
     )
-
-
-def arriving(shape):
-    return [pltpu.VMEM(shape, BF16), pltpu.SemaphoreType.DMA]
 
 
 def base_kernel():
@@ -128,9 +124,7 @@
         out_ref[b * N_VOC : (b + 1) * N_VOC, :] = jnp.where(rows == place, count, 0.0).astype(BF16)
 
 
-def align_kernel(recv_ref, table_ref, source_ref, shift_ref, out_ref, rolled_ref, weight_ref, sem):
-    copy = pltpu.make_async_copy(source_ref, weight_ref, sem)
-    copy.start()
+def roll_kernel(recv_ref, table_ref, shift_ref, rolled_ref):
     lanes = lax.broadcasted_iota(jnp.int32, (TBLOCKS, BLOCK), 1)
     for t in range(OWN):
         extra = recv_ref[t, :, TCOLS:]
@@ -146,7 +140,9 @@
             index = (lanes - shift_ref[:, k : k + 1]) & (BLOCK - 1)
             rolled = jnp.take_along_axis(smooth, index, axis=1)
             rolled_ref[k * TBLOCKS : (k + 1) * TBLOCKS, t * BLOCK : (t + 1) * BLOCK] = rolled.astype(BF16)
-    copy.wait()
+
+
+def align_kernel(recv_ref, rolled_ref, weight_ref, out_ref):
     aligned = jnp.dot(weight_ref[...], rolled_ref[...], preferred_element_type=F32)
     for t in range(OWN):
         mine = aligned[:, t * BLOCK : (t + 1) * BLOCK]
@@ -163,18 +159,19 @@
         out_ref[t, :, SCOLS:] = pack_lanes(N_VOC, [log_total])
 
 
-def grad_kernel(target_ref, logits_ref, source_ref, out_ref, log_ref, turned_ref, sem):
-    copy = pltpu.make_async_copy(source_ref, turned_ref, sem)
-    copy.start()
+def grad_kernel(target_ref, logits_ref, grad_ref, cross_ref, log_ref):
     log_total = unpack_lane(target_ref[:, SCOLS:], 0)
     target = target_ref[:, :SCOLS].astype(F32)
     logits = logits_ref[...]
     cross = jnp.sum(target * logits, axis=1, keepdims=True)
-    grad = (loss_scale * (jnp.exp(logits - log_total) - target)).astype(BF16)
-    copy.wait()
-    out_ref[:, :DS] = jnp.dot(grad, turned_ref[...], preferred_element_type=F32)
-    out_ref[:, DS:] = jnp.broadcast_to(cross, (out_ref.shape[0], BLOCK))
+    grad_ref[...] = (loss_scale * (jnp.exp(logits - log_total) - target)).astype(BF16)
+    cross_ref[...] = jnp.broadcast_to(cross, cross_ref.shape)
     log_ref[...] = jnp.broadcast_to(log_total, log_ref.shape)
+
+
+def terms_kernel(grad_ref, turned_ref, cross_ref, out_ref):
+    out_ref[:, :DS] = jnp.dot(grad_ref[...], turned_ref[...], preferred_element_type=F32)
+    out_ref[:, DS:] = cross_ref[...]
 
 
 def finish_kernel(parts_ref, out_ref):
@@ -278,21 +275,24 @@
         weight_kernel, jax.ShapeDtypeStruct((SBLOCKS, FANOUT * TBLOCKS), BF16), inputs="vv"
     )(place, count)
     received = exchange(outgoing.reshape(N_VOC, OWN, TCOLS + BLOCK), ("z", "y"))
+    received = received.transpose(1, 0, 2)
+    rolled = kernel_call(
+        roll_kernel, jax.ShapeDtypeStruct((FANOUT * TBLOCKS, OWN * BLOCK), BF16), inputs="vvv", flops=3_000_000_000
+    )(received, base_kernel(), shift)
     target = kernel_call(
-        align_kernel,
-        jax.ShapeDtypeStruct((OWN, N_VOC, SCOLS + BLOCK), BF16),
-        [pltpu.VMEM((FANOUT * TBLOCKS, OWN * BLOCK), BF16)] + arriving(weight.shape),
-        "vvhv",
-    )(received.transpose(1, 0, 2), base_kernel(), weight, shift)
+        align_kernel, jax.ShapeDtypeStruct((OWN, N_VOC, SCOLS + BLOCK), BF16), inputs="vvv"
+    )(received, rolled, weight)
     target = exchange(target.transpose(1, 0, 2), ("z", "y")).reshape(tok_rows, SCOLS + BLOCK)
 
     turned = head_full.T
-    terms, log_total = kernel_call(
+    lane_shape = jax.ShapeDtypeStruct((tok_rows, BLOCK), F32)
+    grad, cross, log_total = kernel_call(
         grad_kernel,
-        (jax.ShapeDtypeStruct((tok_rows, WIDE), F32), jax.ShapeDtypeStruct((tok_rows, BLOCK), F32)),
-        arriving(turned.shape),
-        "vvh",
-    )(target, student_logits, turned)
+        (jax.ShapeDtypeStruct((tok_rows, SCOLS), BF16), lane_shape, lane_shape),
+        inputs="vv",
+        flops=4_000_000_000,
+    )(target, student_logits)
+    terms = kernel_call(terms_kernel, jax.ShapeDtypeStruct((tok_rows, WIDE), F32), inputs="vvv")(grad, turned, cross)
     terms = exchange(terms.reshape(NY, tok_rows // NY, WIDE), "y").sum(axis=0)
     terms = exchange(terms.reshape(NZ, OWN, WIDE), "z")
     result = kernel_call(finish_kernel, jax.ShapeDtypeStruct((OWN, WIDE), BF16), inputs="v")(terms)

time: 274 us -> 266 us (0.971); the launches traced: 270 us -> 265 us
  Pallas kernels: 19.2 us -> 13.4 us
  waiting for transfers between devices: 90.8 us -> 94 us
    pallas_call x1, Pallas kernels: 7.78 us -> 1.68 us  [step(): kernel_call(align_kernel, jax.ShapeDtypeStruct((OWN, N_VOC, SCOLS + BLOCK...]
    unnamed x25 -> x27, local copies, waits for them, and re-layouts: 10.3 us -> 11.3 us
where the time goes in v7:
time: 266 us; the launch traced here: 265 us
  waiting for transfers between devices  94 us (35%)
  starting transfers between devices  68.4 us (26%)
  blocking collectives  59.6 us (22%)
  local copies, waits for them, and re-layouts  26 us (10%)
  Pallas kernels  13.4 us (5%)
    all_to_all x4, blocking collectives, exchange(): return lax.all_to_all(value, axis, split_axis=0, concat_axis=0, tiled=True)  59.6 us
    all_to_all x4, waiting for transfers between devices, exchange(): return lax.all_to_all(value, axis, split_axis=0, concat_axis=0, tiled=True)  58.1 us
    all_to_all x4, starting transfers between devices, exchange(): return lax.all_to_all(value, axis, split_axis=0, concat_axis=0, tiled=True)  38.1 us
    ppermute x7, waiting for transfers between devices, send(): lax.ppermute(value, axis, [(i, (i + step) % size) for i in range(size)])  35.5 us
    ppermute x7, starting transfers between devices, send(): lax.ppermute(value, axis, [(i, (i + step) % size) for i in range(size)])  24.1 us
    unnamed x27, local copies, waits for them, and re-layouts  11.3 us
    pallas_call x1, local copies, waits for them, and re-layouts, step(): kernel_call(student_kernel, (jax.ShapeDtypeStruct((DS, SCOLS), BF16), jax...  6.28 us
    ppermute x3, starting transfers between devices, send_c(): return lax.ppermute(value, 'c', [(0, 1), (1, 0)])  6.24 us
  transfers between devices with their start and end apart: 14, of which 10 were waited for; matrix products, arithmetic and copies ran while one was open for 6% of the time, Pallas kernels for 2%

profile of v7, /device:TPU:6, one launch (start us, length us, event | category | flops | bytes accessed | tf_op | source)
XLA Modules:
  0.0 265.2 jit_solution(17931557348574323341)
XLA Ops:
  2.3 15.2 %all-to-all-start = ((bf16[16,16,1024]{2,1,0:T(8,128)(2,1)}), bf16[16,16,1024]{2,1,0:T(8,128)(2,1)S(1)}, u32[]{:S(2)}, u32[]{:S(2)}) async-start(bf16[16,16,1024]{2,1,0:T(8,128)(2,1)} %broadcast_in_dim.10), calls=%async_computation | async-start | bytes 1048576 | tf_op jit(solution)/shard_map/all_to_all | solution.py:186
  17.5 2.7 %collective-permute-start = (bf16[192,1280]{1,0:T(8,128)(2,1)}, bf16[192,1280]{1,0:T(8,128)(2,1)S(1)}, u32[]{:S(2)}, u32[]{:S(2)}) collective-permute-start(bf16[192,1280]{1,0:T(8,128)(2,1)} %param.11), channel_id=1, source_target_pairs={{0,384},{128,0},{256,128},{384,256},{1,385},{129,1},{257,129},{385... | collective-permute-start | bytes 1474568 | tf_op jit(solution)/shard_map/ppermute | solution.py:194
  20.2 4.3 %collective-permute-start.1 = (bf16[192,1280]{1,0:T(8,128)(2,1)}, bf16[192,1280]{1,0:T(8,128)(2,1)S(1)}, u32[]{:S(2)}, u32[]{:S(2)}) collective-permute-start(bf16[192,1280]{1,0:T(8,128)(2,1)} %param.11), channel_id=1, source_target_pairs={{0,128},{128,256},{256,384},{384,0},{1,129},{129,257},{257,385},{3... | collective-permute-start | bytes 1474568 | tf_op jit(solution)/shard_map/ppermute | solution.py:194
  24.5 2.1 collective-permute-start.2
  26.7 1.9 constant_dynamic-update-slice_fusion.3
  28.5 15.5 %collective-permute-done = bf16[192,1280]{1,0:T(8,128)(2,1)S(1)} collective-permute-done((bf16[192,1280]{1,0:T(8,128)(2,1)}, bf16[192,1280]{1,0:T(8,128)(2,1)S(1)}, u32[]{:S(2)}, u32[]{:S(2)}) %collective-permute-start) | collective-permute-done | bytes 491552 | tf_op jit(solution)/shard_map/ppermute | solution.py:194
  47.0 1.9 collective-permute-start.3
  50.6 4.6 %all-to-all-start.1 = ((bf16[4,16,16,1024]{3,2,1,0:T(8,128)(2,1)}), bf16[4,16,16,1024]{3,2,1,0:T(8,128)(2,1)S(1)}, u32[]{:S(2)}, u32[]{:S(2)}) async-start(bf16[4,16,16,1024]{3,2,1,0:T(8,128)(2,1)} %broadcast_in_dim.11), calls=%async_computation.1 | async-start | bytes 4194304 | tf_op jit(solution)/shard_map/all_to_all | solution.py:186
  56.5 3.3 %shard_map.95 = (bf16[1536,1280]{1,0:T(8,128)(2,1)S(1)}, f32[128,1280]{1,0:T(8,128)S(1)}, f32[128,128]{1,0:T(8,128)S(1)}) custom-call(s32[2]{0:T(128)S(1)} %pad_add_fusion.spots_ref, bf16[128,1536]{1,0:T(8,128)(2,1)S(1)} %copy-done.4, bf16[768,1280]{1,0:T(8,128)(2,1)} %constant_dynamic-update-slice_fusion.mine_ref, ...), custom_call_target="tpu_custom_call" | custom-call | tf_op jit(solution)/shard_map/pallas_call | solution.py:258
  59.9 2.0 copy-done.2
  61.8 20.4 %all-to-all-done.1 = bf16[4,16,16,1024]{3,2,1,0:T(8,128)(2,1)S(1)} async-done(((bf16[4,16,16,1024]{3,2,1,0:T(8,128)(2,1)}), bf16[4,16,16,1024]{3,2,1,0:T(8,128)(2,1)S(1)}, u32[]{:S(2)}, u32[]{:S(2)}) %all-to-all-start.1) | async-done | bytes 2097184 | tf_op jit(solution)/shard_map/all_to_all | solution.py:186
  83.8 1.9 shard_map.96
  85.7 1.9 collective-permute-start.4
  87.6 2.4 collective-permute-start.5
  91.9 2.5 collective-permute-start.8
  94.4 4.9 %collective-permute-start.6 = (f32[64,1024]{1,0:T(8,128)S(1)}, f32[64,1024]{1,0:T(8,128)S(1)}, u32[]{:S(2)}, u32[]{:S(2)}) collective-permute-start(f32[64,1024]{1,0:T(8,128)S(1)} %get-tuple-element.35), channel_id=1, source_target_pairs={{0,128},{128,256},{256,384},{384,0},{1,129},{129,257},{257,385},{3... | collective-permute-start | bytes 786440 | tf_op jit(solution)/shard_map/ppermute | solution.py:194
  99.6 4.3 %collective-permute-done.8 = f32[64,1024]{1,0:T(8,128)S(1)} collective-permute-done((f32[64,1024]{1,0:T(8,128)S(1)}, f32[64,1024]{1,0:T(8,128)S(1)}, u32[]{:S(2)}, u32[]{:S(2)}) %collective-permute-start.8) | collective-permute-done | bytes 262176 | tf_op jit(solution)/shard_map/ppermute | solution.py:194
  105.3 5.6 %collective-permute-start.7 = (f32[128,1024]{1,0:T(8,128)S(1)}, f32[128,1024]{1,0:T(8,128)S(1)}, u32[]{:S(2)}, u32[]{:S(2)}) collective-permute-start(f32[128,1024]{1,0:T(8,128)S(1)} %pad_maximum_fusion), channel_id=1, source_target_pairs={{0,128},{128,256},{256,384},{384,0},{1,129},{129,257},{257,385},{3... | collective-permute-start | bytes 1572872 | tf_op jit(solution)/shard_map/ppermute | solution.py:194
  111.0 1.9 collective-permute-start.9
  113.0 8.6 %collective-permute-done.7.prev_ref = f32[128,1024]{1,0:T(8,128)S(1)} collective-permute-done((f32[128,1024]{1,0:T(8,128)S(1)}, f32[128,1024]{1,0:T(8,128)S(1)}, u32[]{:S(2)}, u32[]{:S(2)}) %collective-permute-start.7) | collective-permute-done | bytes 524320 | tf_op jit(solution)/shard_map/ppermute | solution.py:194
  121.6 5.4 %collective-permute-done.9.next_ref = f32[128,1024]{1,0:T(8,128)S(1)} collective-permute-done((f32[128,1024]{1,0:T(8,128)S(1)}, f32[128,1024]{1,0:T(8,128)S(1)}, u32[]{:S(2)}, u32[]{:S(2)}) %collective-permute-start.9) | collective-permute-done | bytes 524320 | tf_op jit(solution)/shard_map/ppermute | solution.py:194
  128.0 13.4 %all-to-all-start.2 = ((bf16[64,2,1152]{2,1,0:T(2,128)(2,1)}), bf16[64,2,1152]{2,1,0:T(2,128)(2,1)S(1)}, u32[]{:S(2)}, u32[]{:S(2)}) async-start(bf16[64,2,1152]{2,1,0:T(2,128)(2,1)} %reshape.60), calls=%async_computation.2 | async-start | bytes 589824 | tf_op jit(solution)/shard_map/all_to_all | solution.py:186
  142.5 2.3 copy-done
  144.8 18.8 %all-to-all-done.2 = bf16[64,2,1152]{2,1,0:T(2,128)(2,1)S(1)} async-done(((bf16[64,2,1152]{2,1,0:T(2,128)(2,1)}), bf16[64,2,1152]{2,1,0:T(2,128)(2,1)S(1)}, u32[]{:S(2)}, u32[]{:S(2)}) %all-to-all-start.2) | async-done | bytes 294944 | tf_op jit(solution)/shard_map/all_to_all | solution.py:186
  163.6 4.3 %shard_map.98.rolled_ref = bf16[4096,256]{1,0:T(8,128)(2,1)S(1)} custom-call(bf16[2,64,1152]{2,1,0:T(8,128)(2,1)S(1)} %bitcast.40, bf16[128,128]{1,0:T(8,128)(2,1)S(1)} %fusion.3.table_ref, s32[512,8]{1,0:T(8,128)S(1)} %bitcast.42), custom_call_target="tpu_custom_call" | custom-call | flops 3000000000 | bytes 1048576 | tf_op jit(solution)/shard_map/pallas_call | solution.py:279
  170.7 4.8 %all-to-all-start.3 = ((bf16[64,2,1408]{2,1,0:T(2,128)(2,1)}), bf16[64,2,1408]{2,1,0:T(2,128)(2,1)S(1)}, u32[]{:S(2)}, u32[]{:S(2)}) async-start(bf16[64,2,1408]{2,1,0:T(2,128)(2,1)} %copy.29), calls=%async_computation.3 | async-start | bytes 720896 | tf_op jit(solution)/shard_map/all_to_all | solution.py:186
  175.6 6.3 %copy.30 = bf16[1536,1280]{0,1:T(8,128)(2,1)} copy(bf16[1536,1280]{1,0:T(8,128)(2,1)} %copy-done.2) | data formatting | bytes 7864320 | tf_op jit(solution)/shard_map/pallas_call | solution.py:258
  181.9 18.9 %all-to-all-done.3 = bf16[64,2,1408]{2,1,0:T(2,128)(2,1)S(1)} async-done(((bf16[64,2,1408]{2,1,0:T(2,128)(2,1)}), bf16[64,2,1408]{2,1,0:T(2,128)(2,1)S(1)}, u32[]{:S(2)}, u32[]{:S(2)}) %all-to-all-start.3) | async-done | bytes 360480 | tf_op jit(solution)/shard_map/all_to_all | solution.py:186
  203.7 13.2 %all_to_all.40 = f32[4,32,1664]{2,1,0:T(8,128)S(1)} all-to-all(f32[4,32,1664]{2,1,0:T(8,128)S(1)} %bitcast.38), channel_id=1, replica_groups=mesh['x'=4,'c'=2,'z'=16,'y'=4] {'y'}, dimensions={0} | all-to-all | bytes 1703936 | tf_op jit(solution)/shard_map/all_to_all | solution.py:186
  217.0 19.0 %all_to_all.41.parts_ref = f32[16,2,1664]{2,1,0:T(2,128)S(1)} all-to-all(f32[16,2,1664]{2,1,0:T(2,128)S(1)} %reshape.63), channel_id=1, replica_groups=mesh['x'=4,'c'=2,'z'=16,'y'=4] {'z'}, dimensions={0} | all-to-all | bytes 425984 | tf_op jit(solution)/shard_map/all_to_all | solution.py:186
  236.2 17.5 %all_to_all.42 = bf16[16,2,1664]{2,1,0:T(2,128)(2,1)S(1)} all-to-all(bf16[16,2,1664]{2,1,0:T(2,128)(2,1)S(1)} %broadcast_in_dim.12), channel_id=1, replica_groups=mesh['x'=4,'c'=2,'z'=16,'y'=4] {'z'}, dimensions={0} | all-to-all | bytes 212992 | tf_op jit(solution)/shard_map/all_to_all | solution.py:186
  253.8 9.9 %all_to_all.43 = bf16[4,32,1664]{2,1,0:T(8,128)(2,1)S(1)} all-to-all(bf16[4,32,1664]{2,1,0:T(8,128)(2,1)S(1)} %broadcast_in_dim.14), channel_id=1, replica_groups=mesh['x'=4,'c'=2,'z'=16,'y'=4] {'y'}, dimensions={0} | all-to-all | bytes 851968 | tf_op jit(solution)/shard_map/all_to_all | solution.py:186
  (72 shorter events, 22.4 us)
Async XLA Ops:
  2.3 46.7 %all-to-all-start = ((bf16[16,16,1024]{2,1,0:T(8,128)(2,1)}), bf16[16,16,1024]{2,1,0:T(8,128)(2,1)S(1)}, u32[]{:S(2)}, u32[]{:S(2)}) async-start(bf16[16,16,1024]{2,1,0:T(8,128)(2,1)} %broadcast_in_dim.10), calls=%async_computation | async-start | bytes 1048576 | tf_op jit(solution)/shard_map/all_to_all | solution.py:186
  17.5 26.5 %collective-permute-start = (bf16[192,1280]{1,0:T(8,128)(2,1)}, bf16[192,1280]{1,0:T(8,128)(2,1)S(1)}, u32[]{:S(2)}, u32[]{:S(2)}) collective-permute-start(bf16[192,1280]{1,0:T(8,128)(2,1)} %param.11), channel_id=1, source_target_pairs={{0,384},{128,0},{256,128},{384,256},{1,385},{129,1},{257,129},{385... | collective-permute-start | bytes 1474568 | tf_op jit(solution)/shard_map/ppermute | solution.py:194
  20.2 25.1 %collective-permute-start.1 = (bf16[192,1280]{1,0:T(8,128)(2,1)}, bf16[192,1280]{1,0:T(8,128)(2,1)S(1)}, u32[]{:S(2)}, u32[]{:S(2)}) collective-permute-start(bf16[192,1280]{1,0:T(8,128)(2,1)} %param.11), channel_id=1, source_target_pairs={{0,128},{128,256},{256,384},{384,0},{1,129},{129,257},{257,385},{3... | collective-permute-start | bytes 1474568 | tf_op jit(solution)/shard_map/ppermute | solution.py:194
  24.5 21.6 %collective-permute-start.2 = (bf16[192,1280]{1,0:T(8,128)(2,1)}, bf16[192,1280]{1,0:T(8,128)(2,1)S(1)}, u32[]{:S(2)}, u32[]{:S(2)}) collective-permute-start(bf16[192,1280]{1,0:T(8,128)(2,1)} %param.11), channel_id=1, source_target_pairs={{0,256},{128,384},{256,0},{384,128},{1,257},{129,385},{257,1},{385... | collective-permute-start | bytes 1474568 | tf_op jit(solution)/shard_map/ppermute | solution.py:194
  47.0 9.5 %collective-permute-start.3 = (bf16[768,1280]{1,0:T(8,128)(2,1)}, bf16[768,1280]{1,0:T(8,128)(2,1)}, u32[]{:S(2)}, u32[]{:S(2)}) collective-permute-start(bf16[768,1280]{1,0:T(8,128)(2,1)} %constant_dynamic-update-slice_fusion.mine_ref), channel_id=1, source_target_pairs={{0,64},{64,0},{1,65},{65,1},{2,66},{66,2},{3,67},{67,3},{4,68},{68... | collective-permute-start | bytes 5898248 | tf_op jit(solution)/shard_map/ppermute | solution.py:202
  50.6 4.6 %copy-start.5 = (s32[512,8]{0,1:T(8,128)S(1)}, s32[512,8]{0,1:T(8,128)}, u32[]{:S(2)}) copy-start(s32[512,8]{0,1:T(8,128)} %param.12) | copy-start | bytes 49156
  50.6 4.6 %copy-start.6 = (s32[512,8]{0,1:T(8,128)S(1)}, s32[512,8]{0,1:T(8,128)}, u32[]{:S(2)}) copy-start(s32[512,8]{0,1:T(8,128)} %param.13) | copy-start | bytes 49156
  50.6 5.0 %copy-start.7 = (s32[512,8]{0,1:T(8,128)S(1)}, s32[512,8]{0,1:T(8,128)}, u32[]{:S(2)}) copy-start(s32[512,8]{0,1:T(8,128)} %param.14) | copy-start | bytes 49156
  50.6 5.5 %copy-start.8 = (s32[512,8]{0,1:T(8,128)S(1)}, s32[512,8]{0,1:T(8,128)}, u32[]{:S(2)}) copy-start(s32[512,8]{0,1:T(8,128)} %param.15) | copy-start | bytes 49156
  50.6 31.6 %all-to-all-start.1 = ((bf16[4,16,16,1024]{3,2,1,0:T(8,128)(2,1)}), bf16[4,16,16,1024]{3,2,1,0:T(8,128)(2,1)S(1)}, u32[]{:S(2)}, u32[]{:S(2)}) async-start(bf16[4,16,16,1024]{3,2,1,0:T(8,128)(2,1)} %broadcast_in_dim.11), calls=%async_computation.1 | async-start | bytes 4194304 | tf_op jit(solution)/shard_map/all_to_all | solution.py:186
  55.2 1.4 copy-start.4
  59.9 2.0 copy-start.2
  82.2 1.6 copy-start.3
  85.7 13.6 %collective-permute-start.4 = (f32[384,1024]{1,0:T(8,128)S(1)}, f32[384,1024]{1,0:T(8,128)S(1)}, u32[]{:S(2)}, u32[]{:S(2)}) collective-permute-start(f32[384,1024]{1,0:T(8,128)S(1)} %get-tuple-element.19), channel_id=1, source_target_pairs={{0,64},{64,0},{1,65},{65,1},{2,66},{66,2},{3,67},{67,3},{4,68},{68... | collective-permute-start | bytes 4718600 | tf_op jit(solution)/shard_map/ppermute | solution.py:202
  87.6 4.1 %collective-permute-start.5 = (f32[128,1024]{1,0:T(8,128)S(1)}, f32[128,1024]{1,0:T(8,128)S(1)}, u32[]{:S(2)}, u32[]{:S(2)}) collective-permute-start(f32[128,1024]{1,0:T(8,128)S(1)} %get-tuple-element.20), channel_id=1, source_target_pairs={{0,64},{64,0},{1,65},{65,1},{2,66},{66,2},{3,67},{67,3},{4,68},{68... | collective-permute-start | bytes 1572872 | tf_op jit(solution)/shard_map/ppermute | solution.py:202
  91.9 12.1 %collective-permute-start.8 = (f32[64,1024]{1,0:T(8,128)S(1)}, f32[64,1024]{1,0:T(8,128)S(1)}, u32[]{:S(2)}, u32[]{:S(2)}) collective-permute-start(f32[64,1024]{1,0:T(8,128)S(1)} %get-tuple-element.34), channel_id=1, source_target_pairs={{0,384},{128,0},{256,128},{384,256},{1,385},{129,1},{257,129},{385... | collective-permute-start | bytes 786440 | tf_op jit(solution)/shard_map/ppermute | solution.py:194
  94.4 10.8 %collective-permute-start.6 = (f32[64,1024]{1,0:T(8,128)S(1)}, f32[64,1024]{1,0:T(8,128)S(1)}, u32[]{:S(2)}, u32[]{:S(2)}) collective-permute-start(f32[64,1024]{1,0:T(8,128)S(1)} %get-tuple-element.35), channel_id=1, source_target_pairs={{0,128},{128,256},{256,384},{384,0},{1,129},{129,257},{257,385},{3... | collective-permute-start | bytes 786440 | tf_op jit(solution)/shard_map/ppermute | solution.py:194
  105.3 16.3 %collective-permute-start.7 = (f32[128,1024]{1,0:T(8,128)S(1)}, f32[128,1024]{1,0:T(8,128)S(1)}, u32[]{:S(2)}, u32[]{:S(2)}) collective-permute-start(f32[128,1024]{1,0:T(8,128)S(1)} %pad_maximum_fusion), channel_id=1, source_target_pairs={{0,128},{128,256},{256,384},{384,0},{1,129},{129,257},{257,385},{3... | collective-permute-start | bytes 1572872 | tf_op jit(solution)/shard_map/ppermute | solution.py:194
  111.0 16.0 %collective-permute-start.9 = (f32[128,1024]{1,0:T(8,128)S(1)}, f32[128,1024]{1,0:T(8,128)S(1)}, u32[]{:S(2)}, u32[]{:S(2)}) collective-permute-start(f32[128,1024]{1,0:T(8,128)S(1)} %pad_maximum_fusion.1), channel_id=1, source_target_pairs={{0,384},{128,0},{256,128},{384,256},{1,385},{129,1},{257,129},{385... | collective-permute-start | bytes 1572872 | tf_op jit(solution)/shard_map/ppermute | solution.py:194
  128.0 35.6 %all-to-all-start.2 = ((bf16[64,2,1152]{2,1,0:T(2,128)(2,1)}), bf16[64,2,1152]{2,1,0:T(2,128)(2,1)S(1)}, u32[]{:S(2)}, u32[]{:S(2)}) async-start(bf16[64,2,1152]{2,1,0:T(2,128)(2,1)} %reshape.60), calls=%async_computation.2 | async-start | bytes 589824 | tf_op jit(solution)/shard_map/all_to_all | solution.py:186
  142.5 2.3 copy-start
  163.6 4.3 %slice-start = ((s8[5242880]{0:T(1024)(128)(4,1)}), s8[4194304]{0:T(1024)(128)(4,1)S(1)}, s32[]{:S(2)}) async-start(s8[5242880]{0:T(1024)(128)(4,1)} %bitcast.34), calls=%async_computation.8 | async-start | bytes 8388608
  163.6 4.3 %slice-start.1 = ((s8[5242880]{0:T(1024)(128)(4,1)}), s8[1048576]{0:T(1024)(128)(4,1)S(1)}, s32[]{:S(2)}) async-start(s8[5242880]{0:T(1024)(128)(4,1)} %bitcast.34), calls=%async_computation.9 | async-start | bytes 2097152
  170.7 30.0 %all-to-all-start.3 = ((bf16[64,2,1408]{2,1,0:T(2,128)(2,1)}), bf16[64,2,1408]{2,1,0:T(2,128)(2,1)S(1)}, u32[]{:S(2)}, u32[]{:S(2)}) async-start(bf16[64,2,1408]{2,1,0:T(2,128)(2,1)} %copy.29), calls=%async_computation.3 | async-start | bytes 720896 | tf_op jit(solution)/shard_map/all_to_all | solution.py:186
  200.9 2.1 copy-start.1

commit v8 on v7

--- a/solution.py
+++ b/solution.py
@@ -130,12 +130,9 @@
         extra = recv_ref[t, :, TCOLS:]
         peak = unpack_lane(extra, 0)
         scale = jnp.exp(peak - jnp.max(peak, axis=0, keepdims=True))
-        smooth = []
-        for j in range(TB_DEV):
-            probs = recv_ref[t, :, j * BLOCK : (j + 1) * BLOCK]
-            tile = jnp.dot(probs, table_ref[...], preferred_element_type=F32) * scale
-            smooth.append(tile.astype(BF16).astype(F32))
-        smooth = jnp.concatenate(smooth, axis=0)
+        blocks = jnp.concatenate([recv_ref[t, :, j * BLOCK : (j + 1) * BLOCK] for j in range(TB_DEV)], axis=0)
+        smooth = jnp.dot(blocks, table_ref[...], preferred_element_type=F32)
+        smooth = (smooth * jnp.concatenate([scale] * TB_DEV, axis=0)).astype(BF16).astype(F32)
         for k in range(FANOUT):
             index = (lanes - shift_ref[:, k : k + 1]) & (BLOCK - 1)
             rolled = jnp.take_along_axis(smooth, index, axis=1)
@@ -275,6 +272,7 @@
         weight_kernel, jax.ShapeDtypeStruct((SBLOCKS, FANOUT * TBLOCKS), BF16), inputs="vv"
     )(place, count)
     received = exchange(outgoing.reshape(N_VOC, OWN, TCOLS + BLOCK), ("z", "y"))
+    received, turned = lax.optimization_barrier((received, head_full.T))
     received = received.transpose(1, 0, 2)
     rolled = kernel_call(
         roll_kernel, jax.ShapeDtypeStruct((FANOUT * TBLOCKS, OWN * BLOCK), BF16), inputs="vvv", flops=3_000_000_000
@@ -284,7 +282,6 @@
     )(received, rolled, weight)
     target = exchange(target.transpose(1, 0, 2), ("z", "y")).reshape(tok_rows, SCOLS + BLOCK)
 
-    turned = head_full.T
     lane_shape = jax.ShapeDtypeStruct((tok_rows, BLOCK), F32)
     grad, cross, log_total = kernel_call(
         grad_kernel,

time: 266 us -> 265 us (level)
  blocking collectives: 59.6 us -> 89.4 us
  waiting for transfers between devices: 94 us -> 68.8 us
  starting transfers between devices: 68.4 us -> 63.5 us
    all_to_all x4 -> x5, blocking collectives: 59.6 us -> 89.4 us  [exchange(): return lax.all_to_all(value, axis, split_axis=0, concat_axis=0, tiled=True)]
    all_to_all x4 -> x3, waiting for transfers between devices: 58.1 us -> 32.9 us  [exchange(): return lax.all_to_all(value, axis, split_axis=0, concat_axis=0, tiled=True)]
    all_to_all x4 -> x3, starting transfers between devices: 38.1 us -> 33.2 us  [exchange(): return lax.all_to_all(value, axis, split_axis=0, concat_axis=0, tiled=True)]
  transfers between devices with their start and end apart: 14 -> 13, of which waited for: 10 -> 9; matrix products, arithmetic and copies ran while one was open for 6% -> 6% of each run, Pallas kernels for 2% -> 2%
where the time goes in v8:
time: 265 us; the launch traced here: 264 us
  blocking collectives  89.4 us (34%)
  waiting for transfers between devices  68.8 us (26%)
  starting transfers between devices  63.5 us (24%)
  local copies, waits for them, and re-layouts  25.2 us (10%)
  Pallas kernels  13.4 us (5%)
    all_to_all x5, blocking collectives, exchange(): return lax.all_to_all(value, axis, split_axis=0, concat_axis=0, tiled=True)  89.4 us
    ppermute x7, waiting for transfers between devices, send(): lax.ppermute(value, axis, [(i, (i + step) % size) for i in range(size)])  35.5 us
    all_to_all x3, starting transfers between devices, exchange(): return lax.all_to_all(value, axis, split_axis=0, concat_axis=0, tiled=True)  33.2 us
    all_to_all x3, waiting for transfers between devices, exchange(): return lax.all_to_all(value, axis, split_axis=0, concat_axis=0, tiled=True)  32.9 us
    ppermute x7, starting transfers between devices, send(): lax.ppermute(value, axis, [(i, (i + step) % size) for i in range(size)])  24.1 us
    unnamed x27, local copies, waits for them, and re-layouts  11.2 us
    pallas_call x1, local copies, waits for them, and re-layouts, step(): kernel_call(student_kernel, (jax.ShapeDtypeStruct((DS, SCOLS), BF16), jax...  6.38 us
    ppermute x3, starting transfers between devices, send_c(): return lax.ppermute(value, 'c', [(0, 1), (1, 0)])  6.24 us
  transfers between devices with their start and end apart: 13, of which 9 were waited for; matrix products, arithmetic and copies ran while one was open for 6% of the time, Pallas kernels for 2%

profile of v8, /device:TPU:6, one launch (start us, length us, event | category | flops | bytes accessed | tf_op | source)
XLA Modules:
  0.0 264.2 jit_solution(9987682664973490047)
XLA Ops:
  2.2 15.2 %all-to-all-start = ((bf16[16,16,1024]{2,1,0:T(8,128)(2,1)}), bf16[16,16,1024]{2,1,0:T(8,128)(2,1)S(1)}, u32[]{:S(2)}, u32[]{:S(2)}) async-start(bf16[16,16,1024]{2,1,0:T(8,128)(2,1)} %broadcast_in_dim.10), calls=%async_computation | async-start | bytes 1048576 | tf_op jit(solution)/shard_map/all_to_all | solution.py:183
  17.4 2.7 %collective-permute-start = (bf16[192,1280]{1,0:T(8,128)(2,1)}, bf16[192,1280]{1,0:T(8,128)(2,1)S(1)}, u32[]{:S(2)}, u32[]{:S(2)}) collective-permute-start(bf16[192,1280]{1,0:T(8,128)(2,1)} %param.11), channel_id=1, source_target_pairs={{0,384},{128,0},{256,128},{384,256},{1,385},{129,1},{257,129},{385... | collective-permute-start | bytes 1474568 | tf_op jit(solution)/shard_map/ppermute | solution.py:191
  20.2 4.3 %collective-permute-start.1 = (bf16[192,1280]{1,0:T(8,128)(2,1)}, bf16[192,1280]{1,0:T(8,128)(2,1)S(1)}, u32[]{:S(2)}, u32[]{:S(2)}) collective-permute-start(bf16[192,1280]{1,0:T(8,128)(2,1)} %param.11), channel_id=1, source_target_pairs={{0,128},{128,256},{256,384},{384,0},{1,129},{129,257},{257,385},{3... | collective-permute-start | bytes 1474568 | tf_op jit(solution)/shard_map/ppermute | solution.py:191
  24.5 2.1 collective-permute-start.2
  26.6 1.9 constant_dynamic-update-slice_fusion.3
  28.5 15.5 %collective-permute-done = bf16[192,1280]{1,0:T(8,128)(2,1)S(1)} collective-permute-done((bf16[192,1280]{1,0:T(8,128)(2,1)}, bf16[192,1280]{1,0:T(8,128)(2,1)S(1)}, u32[]{:S(2)}, u32[]{:S(2)}) %collective-permute-start) | collective-permute-done | bytes 491552 | tf_op jit(solution)/shard_map/ppermute | solution.py:191
  46.9 1.9 collective-permute-start.3
  50.5 4.6 %all-to-all-start.1 = ((bf16[4,16,16,1024]{3,2,1,0:T(8,128)(2,1)}), bf16[4,16,16,1024]{3,2,1,0:T(8,128)(2,1)S(1)}, u32[]{:S(2)}, u32[]{:S(2)}) async-start(bf16[4,16,16,1024]{3,2,1,0:T(8,128)(2,1)} %broadcast_in_dim.11), calls=%async_computation.1 | async-start | bytes 4194304 | tf_op jit(solution)/shard_map/all_to_all | solution.py:183
  56.4 3.3 %shard_map.95 = (bf16[1536,1280]{1,0:T(8,128)(2,1)S(1)}, f32[128,1280]{1,0:T(8,128)S(1)}, f32[128,128]{1,0:T(8,128)S(1)}) custom-call(s32[2]{0:T(128)S(1)} %pad_add_fusion.spots_ref, bf16[128,1536]{1,0:T(8,128)(2,1)S(1)} %copy-done.4, bf16[768,1280]{1,0:T(8,128)(2,1)} %constant_dynamic-update-slice_fusion.mine_ref, ...), custom_call_target="tpu_custom_call" | custom-call | tf_op jit(solution)/shard_map/pallas_call | solution.py:255
  59.8 1.9 copy-done.2
  61.6 20.4 %all-to-all-done.1 = bf16[4,16,16,1024]{3,2,1,0:T(8,128)(2,1)S(1)} async-done(((bf16[4,16,16,1024]{3,2,1,0:T(8,128)(2,1)}), bf16[4,16,16,1024]{3,2,1,0:T(8,128)(2,1)S(1)}, u32[]{:S(2)}, u32[]{:S(2)}) %all-to-all-start.1) | async-done | bytes 2097184 | tf_op jit(solution)/shard_map/all_to_all | solution.py:183
  83.7 1.9 shard_map.96
  85.6 1.9 collective-permute-start.4
  87.5 2.4 collective-permute-start.5
  91.8 2.5 collective-permute-start.8
  94.3 4.8 %collective-permute-start.6 = (f32[64,1024]{1,0:T(8,128)S(1)}, f32[64,1024]{1,0:T(8,128)S(1)}, u32[]{:S(2)}, u32[]{:S(2)}) collective-permute-start(f32[64,1024]{1,0:T(8,128)S(1)} %get-tuple-element.39), channel_id=1, source_target_pairs={{0,128},{128,256},{256,384},{384,0},{1,129},{129,257},{257,385},{3... | collective-permute-start | bytes 786440 | tf_op jit(solution)/shard_map/ppermute | solution.py:191
  99.5 4.3 %collective-permute-done.8 = f32[64,1024]{1,0:T(8,128)S(1)} collective-permute-done((f32[64,1024]{1,0:T(8,128)S(1)}, f32[64,1024]{1,0:T(8,128)S(1)}, u32[]{:S(2)}, u32[]{:S(2)}) %collective-permute-start.8) | collective-permute-done | bytes 262176 | tf_op jit(solution)/shard_map/ppermute | solution.py:191
  105.2 5.6 %collective-permute-start.7 = (f32[128,1024]{1,0:T(8,128)S(1)}, f32[128,1024]{1,0:T(8,128)S(1)}, u32[]{:S(2)}, u32[]{:S(2)}) collective-permute-start(f32[128,1024]{1,0:T(8,128)S(1)} %pad_maximum_fusion), channel_id=1, source_target_pairs={{0,128},{128,256},{256,384},{384,0},{1,129},{129,257},{257,385},{3... | collective-permute-start | bytes 1572872 | tf_op jit(solution)/shard_map/ppermute | solution.py:191
  110.9 1.9 collective-permute-start.9
  112.9 8.6 %collective-permute-done.7.prev_ref = f32[128,1024]{1,0:T(8,128)S(1)} collective-permute-done((f32[128,1024]{1,0:T(8,128)S(1)}, f32[128,1024]{1,0:T(8,128)S(1)}, u32[]{:S(2)}, u32[]{:S(2)}) %collective-permute-start.7) | collective-permute-done | bytes 524320 | tf_op jit(solution)/shard_map/ppermute | solution.py:191
  121.5 5.4 %collective-permute-done.9.next_ref = f32[128,1024]{1,0:T(8,128)S(1)} collective-permute-done((f32[128,1024]{1,0:T(8,128)S(1)}, f32[128,1024]{1,0:T(8,128)S(1)}, u32[]{:S(2)}, u32[]{:S(2)}) %collective-permute-start.9) | collective-permute-done | bytes 524320 | tf_op jit(solution)/shard_map/ppermute | solution.py:191
  127.9 13.4 %all-to-all-start.2 = ((bf16[64,2,1152]{2,1,0:T(2,128)(2,1)}), bf16[64,2,1152]{2,1,0:T(2,128)(2,1)S(1)}, u32[]{:S(2)}, u32[]{:S(2)}) async-start(bf16[64,2,1152]{2,1,0:T(2,128)(2,1)} %reshape.60), calls=%async_computation.2 | async-start | bytes 589824 | tf_op jit(solution)/shard_map/all_to_all | solution.py:183
  141.4 6.4 %copy.28 = bf16[1536,1280]{0,1:T(8,128)(2,1)} copy(bf16[1536,1280]{1,0:T(8,128)(2,1)} %copy-done.2) | data formatting | bytes 7864320 | tf_op jit(solution)/shard_map/pallas_call | solution.py:255
  148.7 2.3 copy-done
  151.1 12.4 %all-to-all-done.2 = bf16[64,2,1152]{2,1,0:T(2,128)(2,1)S(1)} async-done(((bf16[64,2,1152]{2,1,0:T(2,128)(2,1)}), bf16[64,2,1152]{2,1,0:T(2,128)(2,1)S(1)}, u32[]{:S(2)}, u32[]{:S(2)}) %all-to-all-start.2) | async-done | bytes 294944 | tf_op jit(solution)/shard_map/all_to_all | solution.py:183
  163.5 4.3 %shard_map.98.rolled_ref = bf16[4096,256]{1,0:T(8,128)(2,1)S(1)} custom-call(bf16[2,64,1152]{2,1,0:T(8,128)(2,1)S(1)} %bitcast.40, bf16[128,128]{1,0:T(8,128)(2,1)S(1)} %fusion.3.table_ref, s32[512,8]{1,0:T(8,128)S(1)} %bitcast.42), custom_call_target="tpu_custom_call" | custom-call | flops 3000000000 | bytes 1048576 | tf_op jit(solution)/shard_map/pallas_call | solution.py:277
  169.9 29.8 %all_to_all.40 = bf16[64,2,1408]{2,1,0:T(2,128)(2,1)S(1)} all-to-all(bf16[64,2,1408]{2,1,0:T(2,128)(2,1)S(1)} %copy.30), channel_id=1, replica_groups=mesh['x'=4,'c'=2,'z'=16,'y'=4] {'z','y'}, dimensions={0} | all-to-all | bytes 720896 | tf_op jit(solution)/shard_map/all_to_all | solution.py:183
  200.2 1.8 copy-done.1
  202.7 13.2 %all_to_all.41 = f32[4,32,1664]{2,1,0:T(8,128)S(1)} all-to-all(f32[4,32,1664]{2,1,0:T(8,128)S(1)} %bitcast.38), channel_id=1, replica_groups=mesh['x'=4,'c'=2,'z'=16,'y'=4] {'y'}, dimensions={0} | all-to-all | bytes 1703936 | tf_op jit(solution)/shard_map/all_to_all | solution.py:183
  216.0 19.0 %all_to_all.42.parts_ref = f32[16,2,1664]{2,1,0:T(2,128)S(1)} all-to-all(f32[16,2,1664]{2,1,0:T(2,128)S(1)} %reshape.63), channel_id=1, replica_groups=mesh['x'=4,'c'=2,'z'=16,'y'=4] {'z'}, dimensions={0} | all-to-all | bytes 425984 | tf_op jit(solution)/shard_map/all_to_all | solution.py:183
  235.1 17.5 %all_to_all.43 = bf16[16,2,1664]{2,1,0:T(2,128)(2,1)S(1)} all-to-all(bf16[16,2,1664]{2,1,0:T(2,128)(2,1)S(1)} %broadcast_in_dim.12), channel_id=1, replica_groups=mesh['x'=4,'c'=2,'z'=16,'y'=4] {'z'}, dimensions={0} | all-to-all | bytes 212992 | tf_op jit(solution)/shard_map/all_to_all | solution.py:183
  252.8 9.9 %all_to_all.44 = bf16[4,32,1664]{2,1,0:T(8,128)(2,1)S(1)} all-to-all(bf16[4,32,1664]{2,1,0:T(8,128)(2,1)S(1)} %broadcast_in_dim.14), channel_id=1, replica_groups=mesh['x'=4,'c'=2,'z'=16,'y'=4] {'y'}, dimensions={0} | all-to-all | bytes 851968 | tf_op jit(solution)/shard_map/all_to_all | solution.py:183
  (71 shorter events, 19.8 us)
Async XLA Ops:
  2.2 46.6 %all-to-all-start = ((bf16[16,16,1024]{2,1,0:T(8,128)(2,1)}), bf16[16,16,1024]{2,1,0:T(8,128)(2,1)S(1)}, u32[]{:S(2)}, u32[]{:S(2)}) async-start(bf16[16,16,1024]{2,1,0:T(8,128)(2,1)} %broadcast_in_dim.10), calls=%async_computation | async-start | bytes 1048576 | tf_op jit(solution)/shard_map/all_to_all | solution.py:183
  17.4 26.5 %collective-permute-start = (bf16[192,1280]{1,0:T(8,128)(2,1)}, bf16[192,1280]{1,0:T(8,128)(2,1)S(1)}, u32[]{:S(2)}, u32[]{:S(2)}) collective-permute-start(bf16[192,1280]{1,0:T(8,128)(2,1)} %param.11), channel_id=1, source_target_pairs={{0,384},{128,0},{256,128},{384,256},{1,385},{129,1},{257,129},{385... | collective-permute-start | bytes 1474568 | tf_op jit(solution)/shard_map/ppermute | solution.py:191
  20.2 25.1 %collective-permute-start.1 = (bf16[192,1280]{1,0:T(8,128)(2,1)}, bf16[192,1280]{1,0:T(8,128)(2,1)S(1)}, u32[]{:S(2)}, u32[]{:S(2)}) collective-permute-start(bf16[192,1280]{1,0:T(8,128)(2,1)} %param.11), channel_id=1, source_target_pairs={{0,128},{128,256},{256,384},{384,0},{1,129},{129,257},{257,385},{3... | collective-permute-start | bytes 1474568 | tf_op jit(solution)/shard_map/ppermute | solution.py:191
  24.5 21.6 %collective-permute-start.2 = (bf16[192,1280]{1,0:T(8,128)(2,1)}, bf16[192,1280]{1,0:T(8,128)(2,1)S(1)}, u32[]{:S(2)}, u32[]{:S(2)}) collective-permute-start(bf16[192,1280]{1,0:T(8,128)(2,1)} %param.11), channel_id=1, source_target_pairs={{0,256},{128,384},{256,0},{384,128},{1,257},{129,385},{257,1},{385... | collective-permute-start | bytes 1474568 | tf_op jit(solution)/shard_map/ppermute | solution.py:191
  46.9 9.5 %collective-permute-start.3 = (bf16[768,1280]{1,0:T(8,128)(2,1)}, bf16[768,1280]{1,0:T(8,128)(2,1)}, u32[]{:S(2)}, u32[]{:S(2)}) collective-permute-start(bf16[768,1280]{1,0:T(8,128)(2,1)} %constant_dynamic-update-slice_fusion.mine_ref), channel_id=1, source_target_pairs={{0,64},{64,0},{1,65},{65,1},{2,66},{66,2},{3,67},{67,3},{4,68},{68... | collective-permute-start | bytes 5898248 | tf_op jit(solution)/shard_map/ppermute | solution.py:199
  50.5 4.6 %copy-start.5 = (s32[512,8]{0,1:T(8,128)S(1)}, s32[512,8]{0,1:T(8,128)}, u32[]{:S(2)}) copy-start(s32[512,8]{0,1:T(8,128)} %param.12) | copy-start | bytes 49156
  50.5 4.6 %copy-start.6 = (s32[512,8]{0,1:T(8,128)S(1)}, s32[512,8]{0,1:T(8,128)}, u32[]{:S(2)}) copy-start(s32[512,8]{0,1:T(8,128)} %param.13) | copy-start | bytes 49156
  50.5 5.0 %copy-start.7 = (s32[512,8]{0,1:T(8,128)S(1)}, s32[512,8]{0,1:T(8,128)}, u32[]{:S(2)}) copy-start(s32[512,8]{0,1:T(8,128)} %param.14) | copy-start | bytes 49156
  50.5 5.5 %copy-start.8 = (s32[512,8]{0,1:T(8,128)S(1)}, s32[512,8]{0,1:T(8,128)}, u32[]{:S(2)}) copy-start(s32[512,8]{0,1:T(8,128)} %param.15) | copy-start | bytes 49156
  50.5 31.6 %all-to-all-start.1 = ((bf16[4,16,16,1024]{3,2,1,0:T(8,128)(2,1)}), bf16[4,16,16,1024]{3,2,1,0:T(8,128)(2,1)S(1)}, u32[]{:S(2)}, u32[]{:S(2)}) async-start(bf16[4,16,16,1024]{3,2,1,0:T(8,128)(2,1)} %broadcast_in_dim.11), calls=%async_computation.1 | async-start | bytes 4194304 | tf_op jit(solution)/shard_map/all_to_all | solution.py:183
  55.1 1.4 copy-start.4
  59.8 1.9 copy-start.2
  82.1 1.6 copy-start.3
  85.6 13.6 %collective-permute-start.4 = (f32[384,1024]{1,0:T(8,128)S(1)}, f32[384,1024]{1,0:T(8,128)S(1)}, u32[]{:S(2)}, u32[]{:S(2)}) collective-permute-start(f32[384,1024]{1,0:T(8,128)S(1)} %get-tuple-element.21), channel_id=1, source_target_pairs={{0,64},{64,0},{1,65},{65,1},{2,66},{66,2},{3,67},{67,3},{4,68},{68... | collective-permute-start | bytes 4718600 | tf_op jit(solution)/shard_map/ppermute | solution.py:199
  87.5 4.1 %collective-permute-start.5 = (f32[128,1024]{1,0:T(8,128)S(1)}, f32[128,1024]{1,0:T(8,128)S(1)}, u32[]{:S(2)}, u32[]{:S(2)}) collective-permute-start(f32[128,1024]{1,0:T(8,128)S(1)} %get-tuple-element.22), channel_id=1, source_target_pairs={{0,64},{64,0},{1,65},{65,1},{2,66},{66,2},{3,67},{67,3},{4,68},{68... | collective-permute-start | bytes 1572872 | tf_op jit(solution)/shard_map/ppermute | solution.py:199
  91.8 12.1 %collective-permute-start.8 = (f32[64,1024]{1,0:T(8,128)S(1)}, f32[64,1024]{1,0:T(8,128)S(1)}, u32[]{:S(2)}, u32[]{:S(2)}) collective-permute-start(f32[64,1024]{1,0:T(8,128)S(1)} %get-tuple-element.38), channel_id=1, source_target_pairs={{0,384},{128,0},{256,128},{384,256},{1,385},{129,1},{257,129},{385... | collective-permute-start | bytes 786440 | tf_op jit(solution)/shard_map/ppermute | solution.py:191
  94.3 10.7 %collective-permute-start.6 = (f32[64,1024]{1,0:T(8,128)S(1)}, f32[64,1024]{1,0:T(8,128)S(1)}, u32[]{:S(2)}, u32[]{:S(2)}) collective-permute-start(f32[64,1024]{1,0:T(8,128)S(1)} %get-tuple-element.39), channel_id=1, source_target_pairs={{0,128},{128,256},{256,384},{384,0},{1,129},{129,257},{257,385},{3... | collective-permute-start | bytes 786440 | tf_op jit(solution)/shard_map/ppermute | solution.py:191
  105.2 16.3 %collective-permute-start.7 = (f32[128,1024]{1,0:T(8,128)S(1)}, f32[128,1024]{1,0:T(8,128)S(1)}, u32[]{:S(2)}, u32[]{:S(2)}) collective-permute-start(f32[128,1024]{1,0:T(8,128)S(1)} %pad_maximum_fusion), channel_id=1, source_target_pairs={{0,128},{128,256},{256,384},{384,0},{1,129},{129,257},{257,385},{3... | collective-permute-start | bytes 1572872 | tf_op jit(solution)/shard_map/ppermute | solution.py:191
  110.9 16.0 %collective-permute-start.9 = (f32[128,1024]{1,0:T(8,128)S(1)}, f32[128,1024]{1,0:T(8,128)S(1)}, u32[]{:S(2)}, u32[]{:S(2)}) collective-permute-start(f32[128,1024]{1,0:T(8,128)S(1)} %pad_maximum_fusion.1), channel_id=1, source_target_pairs={{0,384},{128,0},{256,128},{384,256},{1,385},{129,1},{257,129},{385... | collective-permute-start | bytes 1572872 | tf_op jit(solution)/shard_map/ppermute | solution.py:191
  127.9 35.6 %all-to-all-start.2 = ((bf16[64,2,1152]{2,1,0:T(2,128)(2,1)}), bf16[64,2,1152]{2,1,0:T(2,128)(2,1)S(1)}, u32[]{:S(2)}, u32[]{:S(2)}) async-start(bf16[64,2,1152]{2,1,0:T(2,128)(2,1)} %reshape.60), calls=%async_computation.2 | async-start | bytes 589824 | tf_op jit(solution)/shard_map/all_to_all | solution.py:183
  148.7 2.3 copy-start
  163.5 4.3 %slice-start = ((s8[5242880]{0:T(1024)(128)(4,1)}), s8[4194304]{0:T(1024)(128)(4,1)S(1)}, s32[]{:S(2)}) async-start(s8[5242880]{0:T(1024)(128)(4,1)} %bitcast.34), calls=%async_computation.8 | async-start | bytes 8388608
  163.5 4.3 %slice-start.1 = ((s8[5242880]{0:T(1024)(128)(4,1)}), s8[1048576]{0:T(1024)(128)(4,1)S(1)}, s32[]{:S(2)}) async-start(s8[5242880]{0:T(1024)(128)(4,1)} %bitcast.34), calls=%async_computation.9 | async-start | bytes 2097152
  199.9 2.1 copy-start.1
